TPU v7x, 32 devices: a whole 2x2x4 slice. The times are simulated.
32 devices in a mesh: grp: 2 (over y), tgt: 4 (over z), shot: 4 (over x, core).
Axes of the slice: x: 2, y: 2, z: 4, core: 2. Of those that a mesh axis runs over, the one named last changes fastest.
Arguments:
- adjoint_now: float32 [8, 16, 32, 256], P(('grp', 'shot'), 'tgt'), parts along dimension 0, may hold values from -6 to 6
- adjoint_later: float32 [8, 16, 32, 256], P(('grp', 'shot'), 'tgt'), parts along dimension 0, may hold values from -6 to 6
- courant: float32 [16, 32, 256], P('tgt'), may hold values from 0.15 to 0.45
- fwd_acc: bfloat16 [8, 4, 16, 32, 256], P(('grp', 'shot'), None, 'tgt'), parts along dimension 0, may hold values from -6 to 6
- surf_dest: int32 [1024, 1], P('tgt'), may hold values from 0 to 3; in each aligned block of 256 rows (0 to 255, 256 to 511, ...) at most 128 rows name the same one
- surf_cell: int32 [1024], P('tgt'), may hold values from 0 to 32767
- surf_vals: float32 [8, 4, 1024], P(('grp', 'shot'), None, 'tgt'), parts along dimension 0, may hold values from -6 to 6
Outputs:
- adjoint_final: float32 [8, 16, 32, 256], P(('grp', 'shot'), 'tgt'), parts along dimension 0
- grad: float32 [32, 32, 256], P(('grp', 'tgt')), parts along dimension 0
There are 2 independent parts, one for each index of `grp`. A program takes and returns all parts, laid end to end along the dimension named above; an argument that names none is the same for every part. Nothing has to cross between parts.
Inputs may be any that keep to these rules, and one draw needn't show every extreme that they name: `surf_dest`: in each owner's list of 256 entries at most 128 entries name one slab, a bound that some block reaches of them; every slab is named somewhere. `surf_cell`: several entries may name the same cell; their values add.
All inputs are finite; a program needn't handle non-finite values.
Results may differ from a plain program's by a relative error of at most 0.0003.
Values sent between devices are 32-bit elements; how exact they have to be, the bound alone decides.
No kernel may reach another device: no remote copies, remote signals or barrier semaphores. Data moves between devices by JAX's collectives and lax.ppermute only.
A program may use at most 128 MiB of HBM per device.

v0:
```python
import jax
import jax.numpy as jnp
from jax import lax
from jax.sharding import PartitionSpec as P

STEPS = 4
CAP = 128


COEFFS = (-205.0 / 72.0, 8.0 / 5.0, -1.0 / 5.0, 8.0 / 315.0, -1.0 / 560.0)


def with_halo(block, sides, width):
    for axis, dim in sides:
        count = lax.axis_size(axis)
        forward = [(i, i + 1) for i in range(count - 1)]
        backward = [(target, source) for source, target in forward]
        low = lax.ppermute(
            lax.slice_in_dim(block, block.shape[dim] - width, None, axis=dim), axis, forward
        )
        high = lax.ppermute(lax.slice_in_dim(block, 0, width, axis=dim), axis, backward)
        block = jnp.concatenate([low, block, high], axis=dim)
    return block


def laplace(padded):
    cells_x = padded.shape[0] - 8
    cells_y = padded.shape[1] - 8
    cells_z = padded.shape[2] - 8
    center = padded[4 : 4 + cells_x, 4 : 4 + cells_y, 4 : 4 + cells_z]
    total = 3.0 * COEFFS[0] * center
    for offset in range(1, 5):
        pairs = (
            padded[4 + offset : 4 + offset + cells_x, 4 : 4 + cells_y, 4 : 4 + cells_z]
            + padded[4 - offset : 4 - offset + cells_x, 4 : 4 + cells_y, 4 : 4 + cells_z]
        )
        pairs = (
            pairs
            + padded[4 : 4 + cells_x, 4 + offset : 4 + offset + cells_y, 4 : 4 + cells_z]
            + padded[4 : 4 + cells_x, 4 - offset : 4 - offset + cells_y, 4 : 4 + cells_z]
        )
        pairs = (
            pairs
            + padded[4 : 4 + cells_x, 4 : 4 + cells_y, 4 + offset : 4 + offset + cells_z]
            + padded[4 : 4 + cells_x, 4 : 4 + cells_y, 4 - offset : 4 - offset + cells_z]
        )
        total = total + COEFFS[offset] * pairs
    return total


def accumulate(grad_total, term):
    return grad_total + term


def inject_by_slots(surf_dest, surf_cell, surf_vals, cells):
    owners = lax.axis_size("tgt")
    target = surf_dest[:, 0]
    onehot_table = (target[:, None] == jnp.arange(owners, dtype=jnp.int32)[None, :]).astype(
        jnp.int32
    )
    ranks = jnp.sum((jnp.cumsum(onehot_table, axis=0) - 1) * onehot_table, axis=1)
    position = target * CAP + ranks
    cell_row = (
        jnp.full((owners * CAP,), -1.0, jnp.float32).at[position].set(surf_cell.astype(jnp.float32))
    )
    value_rows = jnp.zeros((STEPS, owners * CAP), jnp.float32).at[:, position].set(surf_vals[0])
    packed = jnp.concatenate([cell_row[None, :], value_rows], axis=0).reshape(
        STEPS + 1, owners, CAP
    )
    arrived = lax.all_to_all(packed, "tgt", split_axis=1, concat_axis=1, tiled=True)
    flat = arrived.reshape(STEPS + 1, owners * CAP)
    where_to = jnp.where(flat[0] >= 0.0, flat[0], float(cells)).astype(jnp.int32)
    return jnp.zeros((STEPS, cells), jnp.float32).at[:, where_to].add(flat[1:], mode="drop")


def on_device(adjoint_now, adjoint_later, courant, fwd_acc, surf_dest, surf_cell, surf_vals):
    current = adjoint_now[0]
    later_field = adjoint_later[0]
    grid_shape = current.shape
    cells = grid_shape[0] * grid_shape[1] * grid_shape[2]
    inject = inject_by_slots(surf_dest, surf_cell, surf_vals, cells)
    grad_total = jnp.zeros(grid_shape, jnp.float32)
    square = courant * courant
    for step in range(STEPS):
        padded = with_halo(current, (("tgt", 0),), 4)
        padded = jnp.pad(padded, ((0, 0), (4, 4), (4, 4)))
        fresh = (
            2.0 * current
            - later_field
            + square * laplace(padded)
            + inject[step].reshape(grid_shape)
        )
        term = fwd_acc[0, step].astype(jnp.float32) * fresh / courant
        grad_total = accumulate(grad_total, term)
        later_field = current
        current = fresh
    grad_total = lax.psum(grad_total, "shot")
    return (current[None], grad_total)


def solution(mesh):
    in_specs = (
        P(("grp", "shot"), "tgt", None, None),
        P(("grp", "shot"), "tgt", None, None),
        P("tgt", None, None),
        P(("grp", "shot"), None, "tgt", None, None),
        P("tgt", None),
        P("tgt"),
        P(("grp", "shot"), None, "tgt"),
    )
    out_specs = (P(("grp", "shot"), "tgt", None, None), P(("grp", "tgt"), None, None))
    return jax.shard_map(
        on_device, mesh=mesh, in_specs=in_specs, out_specs=out_specs, check_vma=False
    )
```

profile of v0, /device:TPU:0, one launch (start us, length us, event | category | flops | bytes accessed | tf_op | source)
XLA Modules:
  0.0 151.7 jit_solution(5388115988067436681)
XLA Ops:
  7.2 0.7 compare_convert_fusion
  7.8 1.2 reduce-window.6
  9.1 0.1 slice.502
  9.1 0.1 copy.22
  9.3 0.1 copy.23
  9.4 0.1 add_bitcast_fusion
  9.4 0.7 fusion.119
  10.1 0.7 compare_select_fusion.2
  10.8 0.8 copy.24
  11.7 1.2 scatter_custom_fusion.1
  12.9 0.1 copy.26
  13.0 0.7 convert_element_type.48
  13.7 1.4 scatter_custom_fusion
  15.1 0.6 pad_maximum_fusion.8
  15.7 6.3 %all-to-all-start = ((f32[5,4,128]{2,0,1:T(8,128)}), f32[5,4,128]{2,0,1:T(8,128)S(1)}, u32[]{:S(2)}, u32[]{:S(2)}) async-start(f32[5,4,128]{2,0,1:T(8,128)} %pad_maximum_fusion.8), calls=%async_computation | async-start | bytes 32768 | tf_op jit(solution)/shard_map/all_to_all | solution.py:70
  22.0 0.0 all-reduce.6.cloned.1.call-start
  22.0 1.3 collective-permute-start
  23.3 4.6 %collective-permute-start.1 = (f32[4,32,256]{2,1,0:T(8,128)}, f32[4,32,256]{2,1,0:T(8,128)S(1)}, u32[]{:S(2)}, u32[]{:S(2)}) collective-permute-start(f32[4,32,256]{2,1,0:T(8,128)} %bitcast.55), channel_id=1, source_target_pairs={{0,4},{4,8},{8,12},{1,5},{5,9},{9,13},{2,6},{6,10},{10,14},{3,7},{... | collective-permute-start | bytes 393224 | tf_op jit(solution)/shard_map/ppermute | solution.py:18
  27.9 0.0 all-to-all-done
  27.9 0.1 copy.27
  28.1 9.0 %scatter_custom_fusion.2 = f32[4,32768]{0,1:T(8,128)} fusion(s32[512]{0:T(512)S(1)} %bitcast.66, f32[512,4]{1,0:T(8,128)S(1)} %copy.27, f32[]{:T(128)} %constant.16.clone.1), kind=kCustom, calls=%fused_computation.7 | custom fusion | flops 2048 | bytes 524292 | tf_op jit(solution)/shard_map/scatter-add | solution.py:73
  37.1 0.0 copy-start.1
  37.1 0.0 copy-start
  37.1 0.0 copy-start.3
  37.1 0.0 copy-start.2
  37.1 41.4 %slice_reduce_fusion.3 = (f32[32768]{0:T(1024)S(1)}, f32[32768]{0:T(1024)S(1)}, f32[32768]{0:T(1024)S(1)}, f32[32768]{0:T(1024)S(1)}) fusion(f32[4,32768]{0,1:T(8,128)} %scatter_custom_fusion.2), kind=kLoop, calls=%fused_computation.6 | loop fusion | bytes 1048576 | tf_op jit(solution)/shard_map/slice | solution.py:91
  78.5 0.0 collective-permute-done
  78.5 0.0 collective-permute-done.1
  78.5 0.0 copy-done.1
  78.5 0.3 select_maximum_fusion.6
  78.8 0.0 copy-done
  78.8 0.0 copy-done.3
  78.8 0.6 fusion.86
  79.4 1.3 collective-permute-start.2
  80.7 4.6 %collective-permute-start.3 = (f32[4,32,256]{2,1,0:T(8,128)S(1)}, f32[4,32,256]{2,1,0:T(8,128)S(1)}, u32[]{:S(2)}, u32[]{:S(2)}) collective-permute-start(f32[4,32,256]{2,1,0:T(8,128)S(1)} %fusion.86), channel_id=1, source_target_pairs={{0,4},{4,8},{8,12},{1,5},{5,9},{9,13},{2,6},{6,10},{10,14},{3,7},{... | collective-permute-start | bytes 393224 | tf_op jit(solution)/shard_map/ppermute | solution.py:18
  85.3 1.0 collective-permute-done.2
  86.3 1.5 collective-permute-done.3
  87.8 0.3 select_maximum_fusion.4
  88.0 0.6 fusion.63
  88.6 1.3 collective-permute-start.4
  89.9 5.0 %collective-permute-start.5 = (f32[4,32,256]{2,1,0:T(8,128)S(1)}, f32[4,32,256]{2,1,0:T(8,128)S(1)}, u32[]{:S(2)}, u32[]{:S(2)}) collective-permute-start(f32[4,32,256]{2,1,0:T(8,128)S(1)} %fusion.63), channel_id=1, source_target_pairs={{0,4},{4,8},{8,12},{1,5},{5,9},{9,13},{2,6},{6,10},{10,14},{3,7},{... | collective-permute-start | bytes 393224 | tf_op jit(solution)/shard_map/ppermute | solution.py:18
  95.0 1.0 collective-permute-done.4
  95.9 1.5 collective-permute-done.5
  97.4 0.3 select_maximum_fusion.2
  97.7 0.6 fusion.40
  98.3 1.3 collective-permute-start.6
  99.6 5.0 %collective-permute-start.7 = (f32[4,32,256]{2,1,0:T(8,128)S(1)}, f32[4,32,256]{2,1,0:T(8,128)S(1)}, u32[]{:S(2)}, u32[]{:S(2)}) collective-permute-start(f32[4,32,256]{2,1,0:T(8,128)S(1)} %fusion.40), channel_id=1, source_target_pairs={{0,4},{4,8},{8,12},{1,5},{5,9},{9,13},{2,6},{6,10},{10,14},{3,7},{... | collective-permute-start | bytes 393224 | tf_op jit(solution)/shard_map/ppermute | solution.py:18
  104.6 1.0 collective-permute-done.6
  105.6 1.5 collective-permute-done.7
  107.1 0.3 select_maximum_fusion
  107.4 0.0 copy-done.2
  107.4 1.3 fusion.110
  108.7 0.0 all-reduce.6.cloned.1.call-update
  108.7 34.6 %all-reduce.6.cloned.1.call-done = f32[4,32,256]{2,1,0:T(8,128)} async-done(((f32[4,32,256]{2,1,0:T(8,128)}), f32[4,32,256]{2,1,0:T(8,128)}) %all-reduce.6.cloned.1.call-update) | async-done | bytes 131088 | tf_op jit(solution)/shard_map/psum | solution.py:97
  143.3 1.6 %copy.31 = f32[4,32,256]{2,1,0:T(8,128)} copy(f32[4,32,256]{2,1,0:T(8,128)} %all-reduce.6.cloned.1.call-done) | data formatting | bytes 262144
  (8 shorter events, 0.2 us)
Async XLA Ops:
  15.7 12.2 %all-to-all-start = ((f32[5,4,128]{2,0,1:T(8,128)}), f32[5,4,128]{2,0,1:T(8,128)S(1)}, u32[]{:S(2)}, u32[]{:S(2)}) async-start(f32[5,4,128]{2,0,1:T(8,128)} %pad_maximum_fusion.8), calls=%async_computation | async-start | bytes 32768 | tf_op jit(solution)/shard_map/all_to_all | solution.py:70
  22.0 121.2 %all-reduce.6.cloned.1.call-start = ((), (), s32[]{:S(2)}) async-start(), calls=%async_computation.1 | async-start | bytes 262144 | tf_op jit(solution)/shard_map/psum | solution.py:97
  22.0 56.5 %collective-permute-start = (f32[4,32,256]{2,1,0:T(8,128)}, f32[4,32,256]{2,1,0:T(8,128)S(1)}, u32[]{:S(2)}, u32[]{:S(2)}) collective-permute-start(f32[4,32,256]{2,1,0:T(8,128)} %bitcast.54), channel_id=1, source_target_pairs={{4,0},{8,4},{12,8},{5,1},{9,5},{13,9},{6,2},{10,6},{14,10},{7,3},{... | collective-permute-start | bytes 393224 | tf_op jit(solution)/shard_map/ppermute | solution.py:21
  23.3 55.2 %collective-permute-start.1 = (f32[4,32,256]{2,1,0:T(8,128)}, f32[4,32,256]{2,1,0:T(8,128)S(1)}, u32[]{:S(2)}, u32[]{:S(2)}) collective-permute-start(f32[4,32,256]{2,1,0:T(8,128)} %bitcast.55), channel_id=1, source_target_pairs={{0,4},{4,8},{8,12},{1,5},{5,9},{9,13},{2,6},{6,10},{10,14},{3,7},{... | collective-permute-start | bytes 393224 | tf_op jit(solution)/shard_map/ppermute | solution.py:18
  37.1 41.5 %copy-start.1 = (f32[1,4,32,256]{3,2,1,0:T(8,128)S(1)}, f32[1,4,32,256]{3,2,1,0:T(8,128)}, u32[]{:S(2)}) copy-start(f32[1,4,32,256]{3,2,1,0:T(8,128)} %param.7) | copy-start | bytes 393220
  37.1 41.7 %copy-start = (f32[4,32,256]{2,1,0:T(8,128)S(1)}, f32[4,32,256]{2,1,0:T(8,128)}, u32[]{:S(2)}) copy-start(f32[4,32,256]{2,1,0:T(8,128)} %param.9) | copy-start | bytes 393220
  37.1 41.7 %copy-start.3 = (f32[1,4,32,256]{3,2,1,0:T(8,128)S(1)}, f32[1,4,32,256]{3,2,1,0:T(8,128)}, u32[]{:S(2)}) copy-start(f32[1,4,32,256]{3,2,1,0:T(8,128)} %param.8) | copy-start | bytes 393220
  37.1 70.3 %copy-start.2 = (bf16[1,4,4,32,256]{4,3,2,1,0:T(8,128)(2,1)S(1)}, bf16[1,4,4,32,256]{4,3,2,1,0:T(8,128)(2,1)}, u32[]{:S(2)}) copy-start(bf16[1,4,4,32,256]{4,3,2,1,0:T(8,128)(2,1)} %param.10) | copy-start | bytes 786436
  79.4 6.9 %collective-permute-start.2 = (f32[4,32,256]{2,1,0:T(8,128)S(1)}, f32[4,32,256]{2,1,0:T(8,128)S(1)}, u32[]{:S(2)}, u32[]{:S(2)}) collective-permute-start(f32[4,32,256]{2,1,0:T(8,128)S(1)} %fusion.86), channel_id=1, source_target_pairs={{4,0},{8,4},{12,8},{5,1},{9,5},{13,9},{6,2},{10,6},{14,10},{7,3},{... | collective-permute-start | bytes 393224 | tf_op jit(solution)/shard_map/ppermute | solution.py:21
  80.7 7.1 %collective-permute-start.3 = (f32[4,32,256]{2,1,0:T(8,128)S(1)}, f32[4,32,256]{2,1,0:T(8,128)S(1)}, u32[]{:S(2)}, u32[]{:S(2)}) collective-permute-start(f32[4,32,256]{2,1,0:T(8,128)S(1)} %fusion.86), channel_id=1, source_target_pairs={{0,4},{4,8},{8,12},{1,5},{5,9},{9,13},{2,6},{6,10},{10,14},{3,7},{... | collective-permute-start | bytes 393224 | tf_op jit(solution)/shard_map/ppermute | solution.py:18
  88.6 7.3 %collective-permute-start.4 = (f32[4,32,256]{2,1,0:T(8,128)S(1)}, f32[4,32,256]{2,1,0:T(8,128)S(1)}, u32[]{:S(2)}, u32[]{:S(2)}) collective-permute-start(f32[4,32,256]{2,1,0:T(8,128)S(1)} %fusion.63), channel_id=1, source_target_pairs={{4,0},{8,4},{12,8},{5,1},{9,5},{13,9},{6,2},{10,6},{14,10},{7,3},{... | collective-permute-start | bytes 393224 | tf_op jit(solution)/shard_map/ppermute | solution.py:21
  89.9 7.5 %collective-permute-start.5 = (f32[4,32,256]{2,1,0:T(8,128)S(1)}, f32[4,32,256]{2,1,0:T(8,128)S(1)}, u32[]{:S(2)}, u32[]{:S(2)}) collective-permute-start(f32[4,32,256]{2,1,0:T(8,128)S(1)} %fusion.63), channel_id=1, source_target_pairs={{0,4},{4,8},{8,12},{1,5},{5,9},{9,13},{2,6},{6,10},{10,14},{3,7},{... | collective-permute-start | bytes 393224 | tf_op jit(solution)/shard_map/ppermute | solution.py:18
  98.3 7.3 %collective-permute-start.6 = (f32[4,32,256]{2,1,0:T(8,128)S(1)}, f32[4,32,256]{2,1,0:T(8,128)S(1)}, u32[]{:S(2)}, u32[]{:S(2)}) collective-permute-start(f32[4,32,256]{2,1,0:T(8,128)S(1)} %fusion.40), channel_id=1, source_target_pairs={{4,0},{8,4},{12,8},{5,1},{9,5},{13,9},{6,2},{10,6},{14,10},{7,3},{... | collective-permute-start | bytes 393224 | tf_op jit(solution)/shard_map/ppermute | solution.py:21
  99.6 7.5 %collective-permute-start.7 = (f32[4,32,256]{2,1,0:T(8,128)S(1)}, f32[4,32,256]{2,1,0:T(8,128)S(1)}, u32[]{:S(2)}, u32[]{:S(2)}) collective-permute-start(f32[4,32,256]{2,1,0:T(8,128)S(1)} %fusion.40), channel_id=1, source_target_pairs={{0,4},{4,8},{8,12},{1,5},{5,9},{9,13},{2,6},{6,10},{10,14},{3,7},{... | collective-permute-start | bytes 393224 | tf_op jit(solution)/shard_map/ppermute | solution.py:18
Sparse Core Ops, SparseCore 0:
  108.8 34.3 all-reduce.5
where the time goes:
time: 152 us
  local copies, waits for them, and re-layouts  47.1 us (31%)
  waiting for transfers between devices  41.9 us (28%)
  starting transfers between devices  30.6 us (20%)
  other arithmetic  17.8 us (12%)
  between operations  14.3 us (9%)
    slice x1, local copies, waits for them, and re-layouts, on_device(): inject[step].reshape(grid_shape)  41.4 us
    psum x1, waiting for transfers between devices, on_device(): grad_total = lax.psum(grad_total, 'shot')  34.6 us
    ppermute x4, starting transfers between devices, with_halo(): lax.ppermute(lax.slice_in_dim(block, block.shape[dim] - width, None, axis...  19.1 us
    scatter-add x1, other arithmetic, inject_by_slots(): jnp.zeros((STEPS, cells), jnp.float32).at[:, where_to]  8.99 us
    all_to_all x1, starting transfers between devices, inject_by_slots(): lax.all_to_all(packed, 'tgt', split_axis=1, concat_axis=1, tiled=True)  6.32 us
    ppermute x4, starting transfers between devices, with_halo(): lax.ppermute(lax.slice_in_dim(block, 0, width, axis=dim), axis, backward)  5.16 us
    ppermute x4, waiting for transfers between devices, with_halo(): lax.ppermute(lax.slice_in_dim(block, block.shape[dim] - width, None, axis...  4.49 us
  transfers between devices with their start and end apart: 10, of which 7 were waited for; matrix products, arithmetic and copies ran while one was open for 33% of the time, Pallas kernels for 0%

commit v1 on v0

v1 whole, which is shorter than its diff:
```python
import functools

import jax
import jax.numpy as jnp
from jax import lax
from jax.experimental import pallas as pl
from jax.experimental.pallas import tpu as pltpu
from jax.sharding import PartitionSpec as P

CAP = 128
GATHER_LIMIT = 4096

COEFFS = (-205.0 / 72.0, 8.0 / 5.0, -1.0 / 5.0, 8.0 / 315.0, -1.0 / 560.0)


def swap_pairs(count, first):
    partner = list(range(count))
    for left in range(first, count - 1, 2):
        partner[left], partner[left + 1] = left + 1, left
    return list(enumerate(partner))


def neighbours(slab, axis):
    count = lax.axis_size(axis)
    here = lax.axis_index(axis)
    even = here % 2 == 0
    outer = lax.ppermute(slab, axis, swap_pairs(count, 1))
    inner = lax.ppermute(slab, axis, swap_pairs(count, 0))
    low = jnp.where(here == 0, 0.0, jnp.where(even, outer, inner))
    high = jnp.where(here == count - 1, 0.0, jnp.where(even, inner, outer))
    return low, high


def laplace(padded):
    cells_x = padded.shape[0] - 8
    cells_y = padded.shape[1] - 8
    cells_z = padded.shape[2] - 8
    center = padded[4 : 4 + cells_x, 4 : 4 + cells_y, 4 : 4 + cells_z]
    total = 3.0 * COEFFS[0] * center
    for offset in range(1, 5):
        pairs = (
            padded[4 + offset : 4 + offset + cells_x, 4 : 4 + cells_y, 4 : 4 + cells_z]
            + padded[4 - offset : 4 - offset + cells_x, 4 : 4 + cells_y, 4 : 4 + cells_z]
        )
        pairs = (
            pairs
            + padded[4 : 4 + cells_x, 4 + offset : 4 + offset + cells_y, 4 : 4 + cells_z]
            + padded[4 : 4 + cells_x, 4 - offset : 4 - offset + cells_y, 4 : 4 + cells_z]
        )
        pairs = (
            pairs
            + padded[4 : 4 + cells_x, 4 : 4 + cells_y, 4 + offset : 4 + offset + cells_z]
            + padded[4 : 4 + cells_x, 4 : 4 + cells_y, 4 - offset : 4 - offset + cells_z]
        )
        total = total + COEFFS[offset] * pairs
    return total


def gathered_entries(surf_dest, surf_cell, surf_vals):
    steps = surf_vals.shape[1]
    owners = lax.axis_size("tgt")
    count = surf_cell.shape[0]
    pad = -(2 + steps) % 8
    table = jnp.concatenate(
        [
            surf_dest.reshape(1, count).astype(jnp.float32),
            surf_cell.reshape(1, count).astype(jnp.float32),
            surf_vals[0],
            jnp.zeros((pad, count), jnp.float32),
        ],
        axis=0,
    )
    if owners * count <= GATHER_LIMIT:
        tables = [table]
        for shift in range(1, owners):
            if owners & (owners - 1) == 0:
                route = [(i, i ^ shift) for i in range(owners)]
            else:
                route = [(i, (i + shift) % owners) for i in range(owners)]
            tables.append(lax.ppermute(table, "tgt", route))
        return tables
    target = surf_dest[:, 0]
    onehot_table = (target[:, None] == jnp.arange(owners, dtype=jnp.int32)[None, :]).astype(
        jnp.int32
    )
    ranks = jnp.sum((jnp.cumsum(onehot_table, axis=0) - 1) * onehot_table, axis=1)
    position = target * CAP + ranks
    slots = jnp.full((2 + steps + pad, owners * CAP), -1.0, jnp.float32)
    slots = slots.at[:, position].set(table)
    arrived = lax.all_to_all(
        slots.reshape(-1, owners, CAP), "tgt", split_axis=1, concat_axis=1, tiled=True
    )
    flat = arrived.reshape(-1, owners * CAP)
    chunk = 1024 if owners * CAP % 1024 == 0 else CAP
    return [flat[:, i : i + chunk] for i in range(0, owners * CAP, chunk)]


def inject_kernel(steps, here_ref, *refs):
    out_ref = refs[-1]
    rows, lanes = out_ref.shape[1], out_ref.shape[2]
    here = here_ref[0].astype(jnp.float32)
    total = None
    for table_ref in refs[:-1]:
        table = table_ref[...]
        count = table.shape[1]
        slab = table[0:1]
        cell = table[1:2].astype(jnp.int32)
        row = jnp.where(slab == here, cell // lanes, -1)
        lane = cell % lanes
        in_row = lax.broadcasted_iota(jnp.int32, (rows, count), 0) == row
        in_lane = lax.broadcasted_iota(jnp.int32, (lanes, count), 0) == lane
        spread = jnp.where(in_lane, 1.0, 0.0).astype(jnp.bfloat16)
        parts = []
        for step in range(steps):
            rest = table[2 + step : 3 + step]
            for _ in range(3):
                part = rest.astype(jnp.bfloat16).astype(jnp.float32)
                rest = rest - part
                parts.append(jnp.where(in_row, part, 0.0).astype(jnp.bfloat16))
        product = lax.dot_general(
            jnp.concatenate(parts, axis=0),
            spread,
            (((1,), (1,)), ((), ())),
            preferred_element_type=jnp.float32,
        )
        total = product if total is None else total + product
    for step in range(steps):
        first = 3 * step * rows
        out_ref[step] = (
            total[first : first + rows]
            + total[first + rows : first + 2 * rows]
            + total[first + 2 * rows : first + 3 * rows]
        )


def injection(tables, steps, rows, lanes):
    here = lax.axis_index("tgt").reshape(1)
    return pl.pallas_call(
        functools.partial(inject_kernel, steps),
        out_shape=jax.ShapeDtypeStruct((steps, rows, lanes), jnp.float32),
        in_specs=[pl.BlockSpec(memory_space=pltpu.SMEM)]
        + [pl.BlockSpec(memory_space=pltpu.VMEM)] * len(tables),
        out_specs=pl.BlockSpec(memory_space=pltpu.VMEM),
        cost_estimate=pl.CostEstimate(
            flops=6 * steps * rows * lanes * sum(t.shape[1] for t in tables),
            bytes_accessed=4 * steps * rows * lanes,
            transcendentals=0,
        ),
    )(here, *tables)


def sum_over(value, axis):
    count = lax.axis_size(axis)
    if count & (count - 1):
        return lax.psum(value, axis)
    distance = 1
    while distance < count:
        value = value + lax.ppermute(value, axis, [(i, i ^ distance) for i in range(count)])
        distance *= 2
    return value


def on_device(adjoint_now, adjoint_later, courant, fwd_acc, surf_dest, surf_cell, surf_vals):
    current = adjoint_now[0]
    later_field = adjoint_later[0]
    grid_shape = current.shape
    steps = fwd_acc.shape[1]
    tables = gathered_entries(surf_dest, surf_cell, surf_vals)
    inject = injection(tables, steps, grid_shape[0] * grid_shape[1], grid_shape[2])
    grad_total = jnp.zeros(grid_shape, jnp.float32)
    square = courant * courant
    for step in range(steps):
        low, high = neighbours(current, "tgt")
        padded = jnp.concatenate([low, current, high], axis=0)
        padded = jnp.pad(padded, ((0, 0), (4, 4), (4, 4)))
        fresh = (
            2.0 * current
            - later_field
            + square * laplace(padded)
            + inject[step].reshape(grid_shape)
        )
        grad_total = grad_total + fwd_acc[0, step].astype(jnp.float32) * fresh / courant
        later_field = current
        current = fresh
    return (current[None], sum_over(grad_total, "shot"))


def solution(mesh):
    in_specs = (
        P(("grp", "shot"), "tgt", None, None),
        P(("grp", "shot"), "tgt", None, None),
        P("tgt", None, None),
        P(("grp", "shot"), None, "tgt", None, None),
        P("tgt", None),
        P("tgt"),
        P(("grp", "shot"), None, "tgt"),
    )
    out_specs = (P(("grp", "shot"), "tgt", None, None), P(("grp", "tgt"), None, None))
    return jax.shard_map(
        on_device, mesh=mesh, in_specs=in_specs, out_specs=out_specs, check_vma=False
    )
```

time: 152 us -> 54 us (0.36)
  local copies, waits for them, and re-layouts: 47.1 us -> 4.62 us
  waiting for transfers between devices: 41.9 us -> 14.3 us
  between operations: 14.3 us -> 0.83 us
  other arithmetic: 17.8 us -> 5.62 us
  starting transfers between devices: 30.6 us -> 25.7 us
  Pallas kernels: 0 us -> 2.59 us
    slice x1, local copies, waits for them, and re-layouts: 41.4 us -> 1.13 us  [on_device(): inject[step].reshape(grid_shape)]
    psum x1 -> x0, waiting for transfers between devices: 34.6 us -> none  [on_device(): grad_total = lax.psum(grad_total, 'shot')]
    scatter-add x1 -> x0, other arithmetic: 8.99 us -> none  [inject_by_slots(): jnp.zeros((STEPS, cells), jnp.float32).at[:, where_to]]
    ppermute x8 -> x13, waiting for transfers between devices: 7.35 us -> 14.3 us  [the longest x4 8.84 us: neighbours(): inner = lax.ppermute(slab, axis, swap_pairs(count, 0))]
    all_to_all x1 -> x0, starting transfers between devices: 6.32 us -> none  [inject_by_slots(): lax.all_to_all(packed, 'tgt', split_axis=1, concat_axis=1, tiled=True)]
    scatter x2 -> x0, local copies, waits for them, and re-layouts: 2.61 us -> none  [the longest x1 1.39 us: inject_by_slots(): jnp.full((owners * CAP,), -1.0, jnp.float32).at[position]]
    pallas_call x0 -> x1, Pallas kernels: none -> 2.59 us  [injection(): pl.pallas_call(functools.partial(inject_kernel, steps), out_shape=jax.Sha...]
    unnamed x9 -> x20, local copies, waits for them, and re-layouts: 1.58 us -> 3.41 us
  transfers between devices with their start and end apart: 10 -> 13, of which waited for: 7 -> 5; matrix products, arithmetic and copies ran while one was open for 33% -> 2% of each run, Pallas kernels for 0% -> 5%
where the time goes in v1:
time: 54 us; the launch traced here: 53.6 us
  starting transfers between devices  25.7 us (48%)
  waiting for transfers between devices  14.3 us (26%)
  other arithmetic  5.62 us (10%)
  local copies, waits for them, and re-layouts  4.62 us (9%)
  Pallas kernels  2.59 us (5%)
  between operations  0.83 us (2%)
    ppermute x4, starting transfers between devices, neighbours(): inner = lax.ppermute(slab, axis, swap_pairs(count, 0))  14.9 us
    ppermute x4, waiting for transfers between devices, neighbours(): inner = lax.ppermute(slab, axis, swap_pairs(count, 0))  8.84 us
    ppermute x3, starting transfers between devices, gathered_entries(): tables.append(lax.ppermute(table, 'tgt', route))  5.71 us
    ppermute x2, waiting for transfers between devices, sum_over(): lax.ppermute(value, axis, [(i, i ^ distance) for i in range(count)])  5.41 us
    ppermute x4, starting transfers between devices, neighbours(): outer = lax.ppermute(slab, axis, swap_pairs(count, 1))  3.56 us
    unnamed x20, local copies, waits for them, and re-layouts  3.41 us
    pallas_call x1, Pallas kernels, injection(): pl.pallas_call(functools.partial(inject_kernel, steps), out_shape=jax.Sha...  2.59 us
    add x3, other arithmetic, on_device(): 2.0 * current - later_field + square * laplace(padded)  1.76 us
  transfers between devices with their start and end apart: 13, of which 5 were waited for; matrix products, arithmetic and copies ran while one was open for 2% of the time, Pallas kernels for 5%

profile of v1, /device:TPU:0, one launch (start us, length us, event | category | flops | bytes accessed | tf_op | source)
XLA Modules:
  0.0 53.6 jit_solution(17533703832962442828)
XLA Ops:
  0.6 0.0 copy-start.6
  0.6 0.7 %convert_bitcast_fusion = f32[1,256]{1,0:T(1,128)S(1)} fusion(s32[256,1]{0,1:T(1,128)} %param.11), kind=kLoop, calls=%fused_computation.212 | loop fusion | flops 256 | bytes 2048 | tf_op jit(solution)/shard_map/convert_element_type | solution.py:66
  1.3 0.0 copy-done.6
  1.3 0.0 copy-start.5
  1.3 0.1 pad.41.clone
  1.4 0.6 %copy-done.5 = f32[1,4,256]{2,1,0:T(4,128)S(1)} copy-done((f32[1,4,256]{2,1,0:T(4,128)S(1)}, f32[1,4,256]{2,1,0:T(4,128)}, u32[]{:S(2)}) %copy-start.5) | copy-done | bytes 4120
  2.0 0.1 maximum_maximum_fusion.refs_0_
  2.1 0.0 copy-start.4
  2.1 5.1 %collective-permute-start.4 = (f32[8,256]{1,0:T(8,128)S(1)}, f32[8,256]{1,0:T(8,128)S(1)}, u32[]{:S(2)}, u32[]{:S(2)}) collective-permute-start(f32[8,256]{1,0:T(8,128)S(1)} %maximum_maximum_fusion.refs_0_), channel_id=1, source_target_pairs={{0,12},{4,8},{8,4},{12,0},{1,13},{5,9},{9,5},{13,1},{2,14},{6,10},... | collective-permute-start | bytes 24584 | tf_op jit(solution)/shard_map/ppermute | solution.py:80
  7.2 0.0 collective-permute-start.3
  7.2 0.6 %collective-permute-start.2 = (f32[8,256]{1,0:T(8,128)S(1)}, f32[8,256]{1,0:T(8,128)S(1)}, u32[]{:S(2)}, u32[]{:S(2)}) collective-permute-start(f32[8,256]{1,0:T(8,128)S(1)} %maximum_maximum_fusion.refs_0_), channel_id=1, source_target_pairs={{0,4},{4,0},{8,12},{12,8},{1,5},{5,1},{9,13},{13,9},{2,6},{6,2},{1... | collective-permute-start | bytes 24584 | tf_op jit(solution)/shard_map/ppermute | solution.py:80
  7.8 1.6 %collective-permute-start.1 = (f32[4,32,256]{2,1,0:T(8,128)}, f32[4,32,256]{2,1,0:T(8,128)S(1)}, u32[]{:S(2)}, u32[]{:S(2)}) collective-permute-start(f32[4,32,256]{2,1,0:T(8,128)} %bitcast.28), channel_id=1, source_target_pairs={{0,0},{4,8},{8,4},{12,12},{1,1},{5,9},{9,5},{13,13},{2,2},{6,10},{... | collective-permute-start | bytes 393224 | tf_op jit(solution)/shard_map/ppermute | solution.py:27
  9.4 3.3 %collective-permute-start = (f32[4,32,256]{2,1,0:T(8,128)}, f32[4,32,256]{2,1,0:T(8,128)S(1)}, u32[]{:S(2)}, u32[]{:S(2)}) collective-permute-start(f32[4,32,256]{2,1,0:T(8,128)} %bitcast.29), channel_id=1, source_target_pairs={{0,4},{4,0},{8,12},{12,8},{1,5},{5,1},{9,13},{13,9},{2,6},{6,2},{1... | collective-permute-start | bytes 393224 | tf_op jit(solution)/shard_map/ppermute | solution.py:28
  12.6 0.0 copy-done.4
  12.6 0.0 collective-permute-done.4.refs_3_
  12.6 0.0 copy-start.7
  12.6 0.0 collective-permute-done.3.refs_2_
  12.6 0.0 copy-start.8
  12.6 0.0 collective-permute-done.2.refs_1_
  12.7 0.0 copy-start.9
  12.7 0.6 %copy-done.7 = f32[8,256]{1,0:T(8,128)} copy-done((f32[8,256]{1,0:T(8,128)}, f32[8,256]{1,0:T(8,128)S(1)}, u32[]{:S(2)}) %copy-start.7) | copy-done | bytes 8216
  13.2 0.0 copy-done.8
  13.2 0.0 copy-done.9
  13.3 2.6 %shard_map.86 = f32[4,128,256]{2,1,0:T(8,128)} custom-call(s32[1]{0:T(128)} %bitcast.2.here_ref, f32[8,256]{1,0:T(8,128)} %copy-done.4, f32[8,256]{1,0:T(8,128)} %copy-done.9, f32[8,256]{1,0:T(8,128)} %copy-done.8, f32[8,256]{1,0:T(8,128)} %copy-done.7), custom_call_target="tpu_custom_call" | custom-call | flops 805306368 | bytes 524288 | tf_op jit(solution)/shard_map/pallas_call | solution.py:138
  15.8 1.1 %fusion.115 = (f32[1,128,256]{2,1,0:T(8,128)S(1)}, f32[1,128,256]{2,1,0:T(8,128)S(1)}, f32[1,128,256]{2,1,0:T(8,128)S(1)}, f32[1,128,256]{2,1,0:T(8,128)S(1)}) fusion(f32[4,128,256]{2,1,0:T(8,128)} %shard_map.86), kind=kLoop, calls=%fused_computation.213 | loop fusion | bytes 1048576 | tf_op jit(solution)/shard_map/slice | solution.py:180
  17.0 0.0 copy-start.1
  17.0 0.0 collective-permute-done.1
  17.0 0.0 collective-permute-done
  17.0 0.8 %copy-done.1 = f32[1,4,32,256]{3,2,1,0:T(8,128)S(1)} copy-done((f32[1,4,32,256]{3,2,1,0:T(8,128)S(1)}, f32[1,4,32,256]{3,2,1,0:T(8,128)}, u32[]{:S(2)}) %copy-start.1) | copy-done | bytes 131096
  17.9 0.0 copy-start
  17.9 0.0 copy-start.3
  17.9 0.3 select_maximum_fusion.6
  18.2 0.6 %copy-done = f32[4,32,256]{2,1,0:T(8,128)S(1)} copy-done((f32[4,32,256]{2,1,0:T(8,128)S(1)}, f32[4,32,256]{2,1,0:T(8,128)}, u32[]{:S(2)}) %copy-start) | copy-done | bytes 131096
  18.8 0.1 copy-done.3
  18.9 0.6 %fusion.84 = f32[4,32,256]{2,1,0:T(8,128)S(1)} fusion(f32[4,32,256]{2,1,0:T(8,128)S(1)} %bitcast.35, f32[4,32,256]{2,1,0:T(8,128)S(1)} %get-tuple-element.15, f32[4,32,256]{2,1,0:T(8,128)S(1)} %bitcast.31, f32[4,32,256]{2,1,0:T(8,128)S(1)} %get-tuple-element.14, f32[12,40,264]{2,1,0:T(8,128)S(1)} %select_maximum_fusion.6, ...), kind=kLoop, calls=%fused_computation.128 | loop fusion | flops 1343488 | bytes 3014656 | tf_op jit(solution)/shard_map/add | solution.py:177
  19.4 0.7 %collective-permute-start.6 = (f32[4,32,256]{2,1,0:T(8,128)S(1)}, f32[4,32,256]{2,1,0:T(8,128)S(1)}, u32[]{:S(2)}, u32[]{:S(2)}) collective-permute-start(f32[4,32,256]{2,1,0:T(8,128)S(1)} %fusion.84), channel_id=1, source_target_pairs={{0,0},{4,8},{8,4},{12,12},{1,1},{5,9},{9,5},{13,13},{2,2},{6,10},{... | collective-permute-start | bytes 393224 | tf_op jit(solution)/shard_map/ppermute | solution.py:27
  20.1 2.9 %collective-permute-start.5 = (f32[4,32,256]{2,1,0:T(8,128)S(1)}, f32[4,32,256]{2,1,0:T(8,128)S(1)}, u32[]{:S(2)}, u32[]{:S(2)}) collective-permute-start(f32[4,32,256]{2,1,0:T(8,128)S(1)} %fusion.84), channel_id=1, source_target_pairs={{0,4},{4,0},{8,12},{12,8},{1,5},{5,1},{9,13},{13,9},{2,6},{6,2},{1... | collective-permute-start | bytes 393224 | tf_op jit(solution)/shard_map/ppermute | solution.py:28
  23.1 0.0 collective-permute-done.6
  23.1 2.9 %collective-permute-done.5 = f32[4,32,256]{2,1,0:T(8,128)S(1)} collective-permute-done((f32[4,32,256]{2,1,0:T(8,128)S(1)}, f32[4,32,256]{2,1,0:T(8,128)S(1)}, u32[]{:S(2)}, u32[]{:S(2)}) %collective-permute-start.5) | collective-permute-done | bytes 131104 | tf_op jit(solution)/shard_map/ppermute | solution.py:28
  26.0 0.3 select_maximum_fusion.4
  26.3 0.6 %fusion.61 = f32[4,32,256]{2,1,0:T(8,128)S(1)} fusion(f32[4,32,256]{2,1,0:T(8,128)S(1)} %bitcast.34, f32[4,32,256]{2,1,0:T(8,128)S(1)} %get-tuple-element.13, f32[4,32,256]{2,1,0:T(8,128)S(1)} %fusion.84, f32[4,32,256]{2,1,0:T(8,128)S(1)} %get-tuple-element.12, f32[12,40,264]{2,1,0:T(8,128)S(1)} %select_maximum_fusion.4, f32[4,32,256]{2,1,0:T(8,128)S(1)} %copy-done, ...), kind=kLoop, calls=%fused_computation.105 | loop fusion | flops 1343488 | bytes 3014656 | tf_op jit(solution)/shard_map/add | solution.py:177
  26.9 0.7 %collective-permute-start.8 = (f32[4,32,256]{2,1,0:T(8,128)S(1)}, f32[4,32,256]{2,1,0:T(8,128)S(1)}, u32[]{:S(2)}, u32[]{:S(2)}) collective-permute-start(f32[4,32,256]{2,1,0:T(8,128)S(1)} %fusion.61), channel_id=1, source_target_pairs={{0,0},{4,8},{8,4},{12,12},{1,1},{5,9},{9,5},{13,13},{2,2},{6,10},{... | collective-permute-start | bytes 393224 | tf_op jit(solution)/shard_map/ppermute | solution.py:27
  27.6 3.8 %collective-permute-start.7 = (f32[4,32,256]{2,1,0:T(8,128)S(1)}, f32[4,32,256]{2,1,0:T(8,128)S(1)}, u32[]{:S(2)}, u32[]{:S(2)}) collective-permute-start(f32[4,32,256]{2,1,0:T(8,128)S(1)} %fusion.61), channel_id=1, source_target_pairs={{0,4},{4,0},{8,12},{12,8},{1,5},{5,1},{9,13},{13,9},{2,6},{6,2},{1... | collective-permute-start | bytes 393224 | tf_op jit(solution)/shard_map/ppermute | solution.py:28
  31.4 0.0 collective-permute-done.8
  31.4 2.9 %collective-permute-done.7 = f32[4,32,256]{2,1,0:T(8,128)S(1)} collective-permute-done((f32[4,32,256]{2,1,0:T(8,128)S(1)}, f32[4,32,256]{2,1,0:T(8,128)S(1)}, u32[]{:S(2)}, u32[]{:S(2)}) %collective-permute-start.7) | collective-permute-done | bytes 131104 | tf_op jit(solution)/shard_map/ppermute | solution.py:28
  34.3 0.3 select_maximum_fusion.2
  34.6 0.6 %fusion.38 = f32[4,32,256]{2,1,0:T(8,128)S(1)} fusion(f32[4,32,256]{2,1,0:T(8,128)S(1)} %bitcast.33, f32[4,32,256]{2,1,0:T(8,128)S(1)} %get-tuple-element.11, f32[4,32,256]{2,1,0:T(8,128)S(1)} %fusion.61, f32[4,32,256]{2,1,0:T(8,128)S(1)} %get-tuple-element.10, f32[12,40,264]{2,1,0:T(8,128)S(1)} %select_maximum_fusion.2, f32[4,32,256]{2,1,0:T(8,128)S(1)} %fusion.84, ...), kind=kLoop, calls=%fused_computation.82 | loop fusion | flops 1343488 | bytes 3014656 | tf_op jit(solution)/shard_map/add | solution.py:177
  35.2 0.7 %collective-permute-start.10 = (f32[4,32,256]{2,1,0:T(8,128)S(1)}, f32[4,32,256]{2,1,0:T(8,128)S(1)}, u32[]{:S(2)}, u32[]{:S(2)}) collective-permute-start(f32[4,32,256]{2,1,0:T(8,128)S(1)} %fusion.38), channel_id=1, source_target_pairs={{0,0},{4,8},{8,4},{12,12},{1,1},{5,9},{9,5},{13,13},{2,2},{6,10},{... | collective-permute-start | bytes 393224 | tf_op jit(solution)/shard_map/ppermute | solution.py:27
  35.9 4.9 %collective-permute-start.9 = (f32[4,32,256]{2,1,0:T(8,128)S(1)}, f32[4,32,256]{2,1,0:T(8,128)S(1)}, u32[]{:S(2)}, u32[]{:S(2)}) collective-permute-start(f32[4,32,256]{2,1,0:T(8,128)S(1)} %fusion.38), channel_id=1, source_target_pairs={{0,4},{4,0},{8,12},{12,8},{1,5},{5,1},{9,13},{13,9},{2,6},{6,2},{1... | collective-permute-start | bytes 393224 | tf_op jit(solution)/shard_map/ppermute | solution.py:28
  40.8 0.0 collective-permute-done.10
  40.8 2.9 %collective-permute-done.9 = f32[4,32,256]{2,1,0:T(8,128)S(1)} collective-permute-done((f32[4,32,256]{2,1,0:T(8,128)S(1)}, f32[4,32,256]{2,1,0:T(8,128)S(1)}, u32[]{:S(2)}, u32[]{:S(2)}) %collective-permute-start.9) | collective-permute-done | bytes 131104 | tf_op jit(solution)/shard_map/ppermute | solution.py:28
  43.8 0.0 copy-start.2
  43.8 0.3 select_maximum_fusion
  44.1 0.7 %copy-done.2 = bf16[1,4,4,32,256]{4,3,2,1,0:T(8,128)(2,1)S(1)} copy-done((bf16[1,4,4,32,256]{4,3,2,1,0:T(8,128)(2,1)S(1)}, bf16[1,4,4,32,256]{4,3,2,1,0:T(8,128)(2,1)}, u32[]{:S(2)}) %copy-start.2) | copy-done | bytes 262168
  44.7 1.2 %fusion.108 = (f32[4,32,256]{2,1,0:T(8,128)S(1)}, f32[4,32,256]{2,1,0:T(8,128)}) fusion(f32[4,32,256]{2,1,0:T(8,128)S(1)} %copy-done, f32[4,32,256]{2,1,0:T(8,128)S(1)} %fusion.38, f32[4,32,256]{2,1,0:T(8,128)S(1)} %fusion.61, f32[4,32,256]{2,1,0:T(8,128)S(1)} %fusion.84, bf16[1,4,4,32,256]{4,3,2,1,0:T(8,128)(2,1)S(1)} %copy-done.2, ...), kind=kLoop, calls=%fused_computation.193 | loop fusion | flops 1835008 | bytes 3538944 | tf_op jit(solution)/shard_map/add | solution.py:182
  46.0 0.0 collective-permute-start.11
  46.0 1.3 %collective-permute-done.11 = f32[4,32,256]{2,1,0:T(8,128)S(1)} collective-permute-done((f32[4,32,256]{2,1,0:T(8,128)S(1)}, f32[4,32,256]{2,1,0:T(8,128)S(1)}, u32[]{:S(2)}, u32[]{:S(2)}) %collective-permute-start.11) | collective-permute-done | bytes 131104 | tf_op jit(solution)/shard_map/ppermute | solution.py:158
  47.3 1.6 %collective-permute-start.12 = (f32[4,32,256]{2,1,0:T(8,128)S(1)}, f32[4,32,256]{2,1,0:T(8,128)S(1)}, u32[]{:S(2)}, u32[]{:S(2)}) collective-permute-start(f32[4,32,256]{2,1,0:T(8,128)S(1)} %add.450), channel_id=1, source_target_pairs={{0,2},{1,3},{2,0},{3,1},{4,6},{5,7},{6,4},{7,5},{8,10},{9,11},{10,... | collective-permute-start | bytes 393224 | tf_op jit(solution)/shard_map/ppermute | solution.py:158
  48.9 4.1 %collective-permute-done.12 = f32[4,32,256]{2,1,0:T(8,128)S(1)} collective-permute-done((f32[4,32,256]{2,1,0:T(8,128)S(1)}, f32[4,32,256]{2,1,0:T(8,128)S(1)}, u32[]{:S(2)}, u32[]{:S(2)}) %collective-permute-start.12) | collective-permute-done | bytes 131104 | tf_op jit(solution)/shard_map/ppermute | solution.py:158
  53.0 0.7 %add.451 = f32[4,32,256]{2,1,0:T(8,128)} add(f32[4,32,256]{2,1,0:T(8,128)S(1)} %add.450, f32[4,32,256]{2,1,0:T(8,128)S(1)} %collective-permute-done.12) | non-fusion elementwise | flops 32768 | bytes 393216 | tf_op jit(solution)/shard_map/add | solution.py:158
  (7 shorter events, 0.1 us)
Async XLA Ops:
  0.6 0.7 %copy-start.6 = (s32[256]{0:T(256)S(1)}, s32[256]{0:T(256)}, u32[]{:S(2)}) copy-start(s32[256]{0:T(256)} %param.12) | copy-start | bytes 3076
  1.3 0.7 %copy-start.5 = (f32[1,4,256]{2,1,0:T(4,128)S(1)}, f32[1,4,256]{2,1,0:T(4,128)}, u32[]{:S(2)}) copy-start(f32[1,4,256]{2,1,0:T(4,128)} %param.13) | copy-start | bytes 12292
  2.1 10.5 %copy-start.4 = (f32[8,256]{1,0:T(8,128)}, f32[8,256]{1,0:T(8,128)S(1)}, u32[]{:S(2)}) copy-start(f32[8,256]{1,0:T(8,128)S(1)} %maximum_maximum_fusion.refs_0_) | copy-start | bytes 24580
  2.1 10.5 %collective-permute-start.4 = (f32[8,256]{1,0:T(8,128)S(1)}, f32[8,256]{1,0:T(8,128)S(1)}, u32[]{:S(2)}, u32[]{:S(2)}) collective-permute-start(f32[8,256]{1,0:T(8,128)S(1)} %maximum_maximum_fusion.refs_0_), channel_id=1, source_target_pairs={{0,12},{4,8},{8,4},{12,0},{1,13},{5,9},{9,5},{13,1},{2,14},{6,10},... | collective-permute-start | bytes 24584 | tf_op jit(solution)/shard_map/ppermute | solution.py:80
  7.2 5.5 %collective-permute-start.3 = (f32[8,256]{1,0:T(8,128)S(1)}, f32[8,256]{1,0:T(8,128)S(1)}, u32[]{:S(2)}, u32[]{:S(2)}) collective-permute-start(f32[8,256]{1,0:T(8,128)S(1)} %maximum_maximum_fusion.refs_0_), channel_id=1, source_target_pairs={{0,8},{4,12},{8,0},{12,4},{1,9},{5,13},{9,1},{13,5},{2,10},{6,14},... | collective-permute-start | bytes 24584 | tf_op jit(solution)/shard_map/ppermute | solution.py:80
  7.2 5.5 %collective-permute-start.2 = (f32[8,256]{1,0:T(8,128)S(1)}, f32[8,256]{1,0:T(8,128)S(1)}, u32[]{:S(2)}, u32[]{:S(2)}) collective-permute-start(f32[8,256]{1,0:T(8,128)S(1)} %maximum_maximum_fusion.refs_0_), channel_id=1, source_target_pairs={{0,4},{4,0},{8,12},{12,8},{1,5},{5,1},{9,13},{13,9},{2,6},{6,2},{1... | collective-permute-start | bytes 24584 | tf_op jit(solution)/shard_map/ppermute | solution.py:80
  7.8 9.2 %collective-permute-start.1 = (f32[4,32,256]{2,1,0:T(8,128)}, f32[4,32,256]{2,1,0:T(8,128)S(1)}, u32[]{:S(2)}, u32[]{:S(2)}) collective-permute-start(f32[4,32,256]{2,1,0:T(8,128)} %bitcast.28), channel_id=1, source_target_pairs={{0,0},{4,8},{8,4},{12,12},{1,1},{5,9},{9,5},{13,13},{2,2},{6,10},{... | collective-permute-start | bytes 393224 | tf_op jit(solution)/shard_map/ppermute | solution.py:27
  9.4 7.6 %collective-permute-start = (f32[4,32,256]{2,1,0:T(8,128)}, f32[4,32,256]{2,1,0:T(8,128)S(1)}, u32[]{:S(2)}, u32[]{:S(2)}) collective-permute-start(f32[4,32,256]{2,1,0:T(8,128)} %bitcast.29), channel_id=1, source_target_pairs={{0,4},{4,0},{8,12},{12,8},{1,5},{5,1},{9,13},{13,9},{2,6},{6,2},{1... | collective-permute-start | bytes 393224 | tf_op jit(solution)/shard_map/ppermute | solution.py:28
  12.6 0.6 %copy-start.7 = (f32[8,256]{1,0:T(8,128)}, f32[8,256]{1,0:T(8,128)S(1)}, u32[]{:S(2)}) copy-start(f32[8,256]{1,0:T(8,128)S(1)} %collective-permute-done.4.refs_3_) | copy-start | bytes 24580
  12.6 0.6 %copy-start.8 = (f32[8,256]{1,0:T(8,128)}, f32[8,256]{1,0:T(8,128)S(1)}, u32[]{:S(2)}) copy-start(f32[8,256]{1,0:T(8,128)S(1)} %collective-permute-done.3.refs_2_) | copy-start | bytes 24580
  12.7 0.6 %copy-start.9 = (f32[8,256]{1,0:T(8,128)}, f32[8,256]{1,0:T(8,128)S(1)}, u32[]{:S(2)}) copy-start(f32[8,256]{1,0:T(8,128)S(1)} %collective-permute-done.2.refs_1_) | copy-start | bytes 24580
  17.0 0.9 %copy-start.1 = (f32[1,4,32,256]{3,2,1,0:T(8,128)S(1)}, f32[1,4,32,256]{3,2,1,0:T(8,128)}, u32[]{:S(2)}) copy-start(f32[1,4,32,256]{3,2,1,0:T(8,128)} %param.7) | copy-start | bytes 393220
  17.9 0.9 %copy-start = (f32[4,32,256]{2,1,0:T(8,128)S(1)}, f32[4,32,256]{2,1,0:T(8,128)}, u32[]{:S(2)}) copy-start(f32[4,32,256]{2,1,0:T(8,128)} %param.9) | copy-start | bytes 393220
  17.9 1.0 %copy-start.3 = (f32[1,4,32,256]{3,2,1,0:T(8,128)S(1)}, f32[1,4,32,256]{3,2,1,0:T(8,128)}, u32[]{:S(2)}) copy-start(f32[1,4,32,256]{3,2,1,0:T(8,128)} %param.8) | copy-start | bytes 393220
  19.4 3.6 %collective-permute-start.6 = (f32[4,32,256]{2,1,0:T(8,128)S(1)}, f32[4,32,256]{2,1,0:T(8,128)S(1)}, u32[]{:S(2)}, u32[]{:S(2)}) collective-permute-start(f32[4,32,256]{2,1,0:T(8,128)S(1)} %fusion.84), channel_id=1, source_target_pairs={{0,0},{4,8},{8,4},{12,12},{1,1},{5,9},{9,5},{13,13},{2,2},{6,10},{... | collective-permute-start | bytes 393224 | tf_op jit(solution)/shard_map/ppermute | solution.py:27
  20.1 5.9 %collective-permute-start.5 = (f32[4,32,256]{2,1,0:T(8,128)S(1)}, f32[4,32,256]{2,1,0:T(8,128)S(1)}, u32[]{:S(2)}, u32[]{:S(2)}) collective-permute-start(f32[4,32,256]{2,1,0:T(8,128)S(1)} %fusion.84), channel_id=1, source_target_pairs={{0,4},{4,0},{8,12},{12,8},{1,5},{5,1},{9,13},{13,9},{2,6},{6,2},{1... | collective-permute-start | bytes 393224 | tf_op jit(solution)/shard_map/ppermute | solution.py:28
  26.9 4.5 %collective-permute-start.8 = (f32[4,32,256]{2,1,0:T(8,128)S(1)}, f32[4,32,256]{2,1,0:T(8,128)S(1)}, u32[]{:S(2)}, u32[]{:S(2)}) collective-permute-start(f32[4,32,256]{2,1,0:T(8,128)S(1)} %fusion.61), channel_id=1, source_target_pairs={{0,0},{4,8},{8,4},{12,12},{1,1},{5,9},{9,5},{13,13},{2,2},{6,10},{... | collective-permute-start | bytes 393224 | tf_op jit(solution)/shard_map/ppermute | solution.py:27
  27.6 6.7 %collective-permute-start.7 = (f32[4,32,256]{2,1,0:T(8,128)S(1)}, f32[4,32,256]{2,1,0:T(8,128)S(1)}, u32[]{:S(2)}, u32[]{:S(2)}) collective-permute-start(f32[4,32,256]{2,1,0:T(8,128)S(1)} %fusion.61), channel_id=1, source_target_pairs={{0,4},{4,0},{8,12},{12,8},{1,5},{5,1},{9,13},{13,9},{2,6},{6,2},{1... | collective-permute-start | bytes 393224 | tf_op jit(solution)/shard_map/ppermute | solution.py:28
  35.2 5.6 %collective-permute-start.10 = (f32[4,32,256]{2,1,0:T(8,128)S(1)}, f32[4,32,256]{2,1,0:T(8,128)S(1)}, u32[]{:S(2)}, u32[]{:S(2)}) collective-permute-start(f32[4,32,256]{2,1,0:T(8,128)S(1)} %fusion.38), channel_id=1, source_target_pairs={{0,0},{4,8},{8,4},{12,12},{1,1},{5,9},{9,5},{13,13},{2,2},{6,10},{... | collective-permute-start | bytes 393224 | tf_op jit(solution)/shard_map/ppermute | solution.py:27
  35.9 7.8 %collective-permute-start.9 = (f32[4,32,256]{2,1,0:T(8,128)S(1)}, f32[4,32,256]{2,1,0:T(8,128)S(1)}, u32[]{:S(2)}, u32[]{:S(2)}) collective-permute-start(f32[4,32,256]{2,1,0:T(8,128)S(1)} %fusion.38), channel_id=1, source_target_pairs={{0,4},{4,0},{8,12},{12,8},{1,5},{5,1},{9,13},{13,9},{2,6},{6,2},{1... | collective-permute-start | bytes 393224 | tf_op jit(solution)/shard_map/ppermute | solution.py:28
  43.8 1.0 %copy-start.2 = (bf16[1,4,4,32,256]{4,3,2,1,0:T(8,128)(2,1)S(1)}, bf16[1,4,4,32,256]{4,3,2,1,0:T(8,128)(2,1)}, u32[]{:S(2)}) copy-start(bf16[1,4,4,32,256]{4,3,2,1,0:T(8,128)(2,1)} %param.10) | copy-start | bytes 786436
  46.0 1.3 %collective-permute-start.11 = (f32[4,32,256]{2,1,0:T(8,128)S(1)}, f32[4,32,256]{2,1,0:T(8,128)S(1)}, u32[]{:S(2)}, u32[]{:S(2)}) collective-permute-start(f32[4,32,256]{2,1,0:T(8,128)S(1)} %get-tuple-element.2), channel_id=1, source_target_pairs={{0,1},{1,0},{2,3},{3,2},{4,5},{5,4},{6,7},{7,6},{8,9},{9,8},{10,11... | collective-permute-start | bytes 393224 | tf_op jit(solution)/shard_map/ppermute | solution.py:158
  47.3 5.6 %collective-permute-start.12 = (f32[4,32,256]{2,1,0:T(8,128)S(1)}, f32[4,32,256]{2,1,0:T(8,128)S(1)}, u32[]{:S(2)}, u32[]{:S(2)}) collective-permute-start(f32[4,32,256]{2,1,0:T(8,128)S(1)} %add.450), channel_id=1, source_target_pairs={{0,2},{1,3},{2,0},{3,1},{4,6},{5,7},{6,4},{7,5},{8,10},{9,11},{10,... | collective-permute-start | bytes 393224 | tf_op jit(solution)/shard_map/ppermute | solution.py:158

commit v2 on v1

v2 whole, which is shorter than its diff:
```python
import functools

import jax
import jax.numpy as jnp
from jax import lax
from jax.experimental import pallas as pl
from jax.experimental.pallas import tpu as pltpu
from jax.sharding import PartitionSpec as P

CAP = 128
GATHER_LIMIT = 4096
REACH = 4
PIECES = 3

COEFFS = (-205.0 / 72.0, 8.0 / 5.0, -1.0 / 5.0, 8.0 / 315.0, -1.0 / 560.0)


def on_chip(kernel, outs, *args, flops=0):
    scalar = [a.dtype == jnp.int32 and a.ndim == 1 for a in args]
    results = pl.pallas_call(
        kernel,
        out_shape=[pltpu.VMEM(shape, jnp.float32) for shape in outs],
        in_specs=[
            pl.BlockSpec(memory_space=pltpu.SMEM if s else pltpu.VMEM) for s in scalar
        ],
        out_specs=[pl.BlockSpec(memory_space=pltpu.VMEM) for _ in outs],
        cost_estimate=pl.CostEstimate(
            flops=flops,
            bytes_accessed=sum(a.size * a.dtype.itemsize for a in args),
            transcendentals=0,
        ),
    )(
        *[
            a if s else pltpu.with_memory_space_constraint(a, pltpu.VMEM)
            for a, s in zip(args, scalar)
        ]
    )
    return list(results)


def swap_pairs(count, first):
    partner = list(range(count))
    for left in range(first, count - 1, 2):
        partner[left], partner[left + 1] = left + 1, left
    return list(enumerate(partner))


def exchange(slab):
    count = lax.axis_size("tgt")
    outer = lax.ppermute(slab, "tgt", swap_pairs(count, 1))
    inner = lax.ppermute(slab, "tgt", swap_pairs(count, 0))
    return inner, outer


def gathered_entries(surf_dest, surf_cell, surf_vals):
    steps = surf_vals.shape[1]
    owners = lax.axis_size("tgt")
    count = surf_cell.shape[0]
    pad = -(2 + steps) % 8
    table = jnp.concatenate(
        [
            surf_dest.reshape(1, count).astype(jnp.float32),
            surf_cell.reshape(1, count).astype(jnp.float32),
            surf_vals[0],
            jnp.zeros((pad, count), jnp.float32),
        ],
        axis=0,
    )
    if owners * count <= GATHER_LIMIT:
        tables = [table]
        for shift in range(1, owners):
            if owners & (owners - 1) == 0:
                route = [(i, i ^ shift) for i in range(owners)]
            else:
                route = [(i, (i + shift) % owners) for i in range(owners)]
            tables.append(lax.ppermute(table, "tgt", route))
        return tables, True
    target = surf_dest[:, 0]
    onehot_table = (target[:, None] == jnp.arange(owners, dtype=jnp.int32)[None, :]).astype(
        jnp.int32
    )
    ranks = jnp.sum((jnp.cumsum(onehot_table, axis=0) - 1) * onehot_table, axis=1)
    position = target * CAP + ranks
    slots = jnp.full((table.shape[0], owners * CAP), -1.0, jnp.float32)
    slots = slots.at[:, position].set(table)
    arrived = lax.all_to_all(
        slots.reshape(-1, owners, CAP), "tgt", split_axis=1, concat_axis=1, tiled=True
    )
    flat = arrived.reshape(-1, owners * CAP)
    chunk = 1024 if owners * CAP % 1024 == 0 else CAP
    return [flat[:, i : i + chunk] for i in range(0, owners * CAP, chunk)], False


def inject_kernel(steps, table_count, with_halo, here_ref, *refs):
    table_refs, out_refs = refs[:table_count], refs[table_count:]
    planes, cells_y, lanes = out_refs[0].shape
    rows = planes * cells_y
    here = here_ref[0].astype(jnp.float32)
    left, right = [], []
    for table_ref in table_refs:
        table = table_ref[...]
        count = table.shape[1]
        slab = table[0:1]
        cell = table[1:2].astype(jnp.int32)
        row, lane = cell // lanes, cell % lanes
        in_lane = lax.broadcasted_iota(jnp.int32, (lanes, count), 0) == lane
        spread = jnp.where(in_lane, 1.0, 0.0).astype(jnp.bfloat16)
        each_row = lax.broadcasted_iota(jnp.int32, (rows, count), 0)
        in_row = [each_row == jnp.where(slab == here, row, -1)]
        if with_halo:
            in_row.append(each_row == jnp.where(slab == here - 1.0, row, -1))
            in_row.append(each_row == jnp.where(slab == here + 1.0, row, -1))
        rest = [table[2 + step : 3 + step] for step in range(steps)]
        for _ in range(PIECES):
            part = [r.astype(jnp.bfloat16).astype(jnp.float32) for r in rest]
            rest = [r - p for r, p in zip(rest, part)]
            picks = [(in_row[0], p) for p in part] + [(m, part[0]) for m in in_row[1:]]
            left.append(
                jnp.concatenate(
                    [jnp.where(m, p, 0.0).astype(jnp.bfloat16) for m, p in picks], axis=0
                )
            )
            right.append(spread)
    total = lax.dot_general(
        jnp.concatenate(left, axis=1),
        jnp.concatenate(right, axis=1),
        (((1,), (1,)), ((), ())),
        preferred_element_type=jnp.float32,
    )
    for i, out_ref in enumerate(out_refs):
        out_ref[...] = total[i * rows : (i + 1) * rows].reshape(out_ref.shape)


def injection(here, tables, steps, grid_shape, with_halo):
    outs = [grid_shape] * (steps + 2 * with_halo)
    entries = sum(t.shape[1] for t in tables)
    cells = grid_shape[0] * grid_shape[1] * grid_shape[2]
    return on_chip(
        functools.partial(inject_kernel, steps, len(tables), with_halo),
        outs,
        here,
        *tables,
        flops=2 * PIECES * len(outs) * cells * entries,
    )


def plane_stencil(plane):
    cells_y, lanes = plane.shape
    at_y = lax.broadcasted_iota(jnp.int32, plane.shape, 0)
    at_z = lax.broadcasted_iota(jnp.int32, plane.shape, 1)
    total = 3.0 * COEFFS[0] * plane
    for k in range(1, REACH + 1):
        pairs = (
            jnp.where(at_y >= k, pltpu.roll(plane, k, 0), 0.0)
            + jnp.where(at_y < cells_y - k, pltpu.roll(plane, cells_y - k, 0), 0.0)
            + jnp.where(at_z >= k, pltpu.roll(plane, k, 1), 0.0)
            + jnp.where(at_z < lanes - k, pltpu.roll(plane, lanes - k, 1), 0.0)
        )
        total = total + COEFFS[k] * pairs
    return total


def own_kernel(step, has_inject, fix_inject, last, *refs):
    refs = list(refs)
    current_ref, later_ref, courant_ref = refs[:3]
    refs = refs[3:]
    inject_ref = refs.pop(0) if has_inject else None
    fix_ref = refs.pop(0) if fix_inject else None
    fwd_ref = refs.pop(0) if step else None
    grad_in_ref = refs.pop(0) if step > 1 else None
    part_ref = refs.pop(0)
    fixed_ref = refs.pop(0) if fix_inject else None
    grad_ref = refs.pop(0) if step else None
    weight_ref = refs.pop(0) if last else None
    planes = current_ref.shape[0]
    current = [current_ref[p] for p in range(planes)]
    if fix_inject:
        current = [current[p] + fix_ref[p] for p in range(planes)]
        for p in range(planes):
            fixed_ref[p] = current[p]
    for p in range(planes):
        total = plane_stencil(current[p])
        for k in range(1, REACH + 1):
            for q in (p - k, p + k):
                if 0 <= q < planes:
                    total = total + COEFFS[k] * current[q]
        courant = courant_ref[p]
        part = 2.0 * current[p] - later_ref[p] + courant * courant * total
        if has_inject:
            part = part + inject_ref[p]
        part_ref[p] = part
        if step:
            grad = fwd_ref[step - 1, p].astype(jnp.float32) * current[p]
            if step > 1:
                grad = grad + grad_in_ref[p]
            if last:
                inverse = 1.0 / courant
                grad = grad * inverse
                weight_ref[p] = fwd_ref[step, p].astype(jnp.float32) * inverse
            grad_ref[p] = grad


def halo_kernel(slabs, fix_inject, last, here_ref, *refs):
    refs = list(refs)
    inner_ref, outer_ref, part_ref, courant_ref = refs[:4]
    refs = refs[4:]
    fix_refs = (refs.pop(0), refs.pop(0)) if fix_inject else None
    weight_ref, grad_in_ref = (refs.pop(0), refs.pop(0)) if last else (None, None)
    fresh_ref = refs.pop(0)
    grad_ref = refs.pop(0) if last else None
    here = here_ref[0]
    even = here % 2 == 0
    planes = inner_ref.shape[0]
    low, high = {}, {}
    for p in range(planes - REACH, planes):
        plane = jnp.where(even, outer_ref[p], inner_ref[p])
        if fix_inject:
            plane = plane + fix_refs[0][p]
        low[p - planes] = jnp.where(here == 0, 0.0, plane)
    for p in range(REACH):
        plane = jnp.where(even, inner_ref[p], outer_ref[p])
        if fix_inject:
            plane = plane + fix_refs[1][p]
        high[p + planes] = jnp.where(here == slabs - 1, 0.0, plane)
    for p in range(planes):
        terms = []
        for k in range(1, REACH + 1):
            if p - k < 0:
                terms.append(COEFFS[k] * low[p - k])
            if p + k >= planes:
                terms.append(COEFFS[k] * high[p + k])
        courant = courant_ref[p]
        fresh = part_ref[p] + courant * courant * sum(terms[1:], terms[0])
        fresh_ref[p] = fresh
        if last:
            grad_ref[p] = grad_in_ref[p] + weight_ref[p] * fresh


def sum_over(value, axis):
    count = lax.axis_size(axis)
    if count & (count - 1):
        return lax.psum(value, axis)
    distance = 1
    while distance < count:
        value = value + lax.ppermute(value, axis, [(i, i ^ distance) for i in range(count)])
        distance *= 2
    return value


def on_device(adjoint_now, adjoint_later, courant, fwd_acc, surf_dest, surf_cell, surf_vals):
    current = adjoint_now[0]
    later_field = adjoint_later[0]
    fwd = fwd_acc[0]
    shape = current.shape
    steps = fwd.shape[0]
    slabs = lax.axis_size("tgt")
    here = lax.axis_index("tgt").reshape(1)
    tables, everywhere = gathered_entries(surf_dest, surf_cell, surf_vals)
    inject = injection(here, tables, steps, shape, everywhere)
    grad = None
    for step in range(steps):
        last = step == steps - 1
        received = exchange(current)
        fix = everywhere and step == 1
        has_inject = step > 0 or not everywhere
        args, outs = [current, later_field, courant], [shape]
        if has_inject:
            args.append(inject[step])
        if fix:
            args.append(inject[0])
            outs.append(shape)
        if step:
            args.append(fwd)
            outs.append(shape)
        if step > 1:
            args.append(grad)
        if last:
            outs.append(shape)
        results = on_chip(
            functools.partial(own_kernel, step, has_inject, fix, last),
            outs,
            *args,
            flops=40 * current.size,
        )
        part = results.pop(0)
        if fix:
            current = results.pop(0)
        if step:
            grad = results.pop(0)
        args, outs = [here, *received, part, courant], [shape]
        if fix:
            args += inject[steps:]
        if last:
            args += [results.pop(0), grad]
            outs.append(shape)
        results = on_chip(
            functools.partial(halo_kernel, slabs, fix, last), outs, *args, flops=10 * current.size
        )
        later_field, current = current, results[0]
        if last:
            grad = results[1]
    return (current[None], sum_over(grad, "shot"))


def solution(mesh):
    in_specs = (
        P(("grp", "shot"), "tgt", None, None),
        P(("grp", "shot"), "tgt", None, None),
        P("tgt", None, None),
        P(("grp", "shot"), None, "tgt", None, None),
        P("tgt", None),
        P("tgt"),
        P(("grp", "shot"), None, "tgt"),
    )
    out_specs = (P(("grp", "shot"), "tgt", None, None), P(("grp", "tgt"), None, None))
    return jax.shard_map(
        on_device, mesh=mesh, in_specs=in_specs, out_specs=out_specs, check_vma=False
    )
```

time: 54 us -> 47.2 us (0.87)
  other arithmetic: 5.62 us -> 0.77 us
  starting transfers between devices: 25.7 us -> 22.5 us
  Pallas kernels: 2.59 us -> 3.31 us
    ppermute x3, waiting for transfers between devices: 0.01 us -> 3.79 us  [gathered_entries(): tables.append(lax.ppermute(table, 'tgt', route))]
    add x4 -> x0, other arithmetic: 3.01 us -> none  [the longest x3 1.76 us: on_device(): 2.0 * current - later_field + square * laplace(padded)]
    ppermute x8, waiting for transfers between devices: 8.85 us -> 6.32 us  [the longest x4 6.31 us: exchange(): inner = lax.ppermute(slab, 'tgt', swap_pairs(count, 0))]
    ppermute x8, starting transfers between devices: 18.4 us -> 16.4 us  [the longest x4 12.8 us: exchange(): inner = lax.ppermute(slab, 'tgt', swap_pairs(count, 0))]
    ppermute x3, starting transfers between devices: 5.71 us -> 4.49 us  [gathered_entries(): tables.append(lax.ppermute(table, 'tgt', route))]
    unnamed x20 -> x19, local copies, waits for them, and re-layouts: 3.41 us -> 4.58 us
    slice x1 -> x0, local copies, waits for them, and re-layouts: 1.13 us -> none  [on_device(): inject[step].reshape(grid_shape)]
    concatenate x4 -> x0, other arithmetic: 1.08 us -> none  [on_device(): padded = jnp.concatenate([low, current, high], axis=0)]
  transfers between devices with their start and end apart: 13 -> 13, of which waited for: 5 -> 6; matrix products, arithmetic and copies ran while one was open for 2% -> 2% of each run, Pallas kernels for 5% -> 6%
where the time goes in v2:
time: 47.2 us; the launch traced here: 46.9 us
  starting transfers between devices  22.5 us (48%)
  waiting for transfers between devices  14.8 us (31%)
  local copies, waits for them, and re-layouts  4.65 us (10%)
  Pallas kernels  3.31 us (7%)
  between operations  0.79 us (2%)
  other arithmetic  0.77 us (2%)
    ppermute x4, starting transfers between devices, exchange(): inner = lax.ppermute(slab, 'tgt', swap_pairs(count, 0))  12.8 us
    ppermute x4, waiting for transfers between devices, exchange(): inner = lax.ppermute(slab, 'tgt', swap_pairs(count, 0))  6.31 us
    ppermute x2, waiting for transfers between devices, sum_over(): lax.ppermute(value, axis, [(i, i ^ distance) for i in range(count)])  4.73 us
    unnamed x19, local copies, waits for them, and re-layouts  4.58 us
    ppermute x3, starting transfers between devices, gathered_entries(): tables.append(lax.ppermute(table, 'tgt', route))  4.49 us
    ppermute x3, waiting for transfers between devices, gathered_entries(): tables.append(lax.ppermute(table, 'tgt', route))  3.79 us
    ppermute x4, starting transfers between devices, exchange(): outer = lax.ppermute(slab, 'tgt', swap_pairs(count, 1))  3.53 us
    pallas_call x9, Pallas kernels, on_chip(): pl.pallas_call(kernel, out_shape=[pltpu.VMEM(shape, jnp.float32) for shap...  3.31 us
  transfers between devices with their start and end apart: 13, of which 6 were waited for; matrix products, arithmetic and copies ran while one was open for 2% of the time, Pallas kernels for 6%

profile of v2, /device:TPU:0, one launch (start us, length us, event | category | flops | bytes accessed | tf_op | source)
XLA Modules:
  0.0 46.9 jit_solution(7914780677061083251)
XLA Ops:
  0.6 3.1 %collective-permute-start = (f32[4,32,256]{2,1,0:T(8,128)}, f32[4,32,256]{2,1,0:T(8,128)S(1)}, u32[]{:S(2)}, u32[]{:S(2)}) collective-permute-start(f32[4,32,256]{2,1,0:T(8,128)} %bitcast.13), channel_id=1, source_target_pairs={{0,4},{4,0},{8,12},{12,8},{1,5},{5,1},{9,13},{13,9},{2,6},{6,2},{1... | collective-permute-start | bytes 393224 | tf_op jit(solution)/shard_map/ppermute | solution.py:51
  3.7 1.6 %collective-permute-start.1 = (f32[4,32,256]{2,1,0:T(8,128)}, f32[4,32,256]{2,1,0:T(8,128)S(1)}, u32[]{:S(2)}, u32[]{:S(2)}) collective-permute-start(f32[4,32,256]{2,1,0:T(8,128)} %bitcast.14), channel_id=1, source_target_pairs={{0,0},{4,8},{8,4},{12,12},{1,1},{5,9},{9,5},{13,13},{2,2},{6,10},{... | collective-permute-start | bytes 393224 | tf_op jit(solution)/shard_map/ppermute | solution.py:50
  5.3 0.0 copy-start.7
  5.3 0.7 %copy-done.7 = s32[256]{0:T(256)S(1)} copy-done((s32[256]{0:T(256)S(1)}, s32[256]{0:T(256)}, u32[]{:S(2)}) %copy-start.7) | copy-done | bytes 1048
  6.0 0.1 pad.3.clone
  6.0 0.0 copy-start
  6.0 0.9 %copy-done = f32[4,32,256]{2,1,0:T(8,128)S(1)} copy-done((f32[4,32,256]{2,1,0:T(8,128)S(1)}, f32[4,32,256]{2,1,0:T(8,128)}, u32[]{:S(2)}) %copy-start) | copy-done | bytes 131096
  6.9 0.0 copy-start.3
  6.9 0.9 %copy-done.3 = f32[1,4,32,256]{3,2,1,0:T(8,128)S(1)} copy-done((f32[1,4,32,256]{3,2,1,0:T(8,128)S(1)}, f32[1,4,32,256]{3,2,1,0:T(8,128)}, u32[]{:S(2)}) %copy-start.3) | copy-done | bytes 131096
  7.8 0.0 copy-start.5
  7.8 0.9 %copy-done.5 = f32[1,4,32,256]{3,2,1,0:T(8,128)S(1)} copy-done((f32[1,4,32,256]{3,2,1,0:T(8,128)S(1)}, f32[1,4,32,256]{3,2,1,0:T(8,128)}, u32[]{:S(2)}) %copy-start.5) | copy-done | bytes 131096
  8.7 0.0 copy-start.8
  8.7 0.0 copy-start.1
  8.8 0.4 shard_map.86.refs_2_
  9.1 0.3 copy-done.8
  9.4 0.0 collective-permute-done.refs_0_
  9.4 0.0 collective-permute-done.1.refs_1_
  9.4 0.2 copy-done.1
  9.7 0.0 copy-start.6
  9.7 0.1 shard_map.87.refs_0_
  9.8 3.6 %collective-permute-start.2 = (f32[4,32,256]{2,1,0:T(8,128)S(1)}, f32[4,32,256]{2,1,0:T(8,128)S(1)}, u32[]{:S(2)}, u32[]{:S(2)}) collective-permute-start(f32[4,32,256]{2,1,0:T(8,128)S(1)} %shard_map.87.refs_0_), channel_id=1, source_target_pairs={{0,4},{4,0},{8,12},{12,8},{1,5},{5,1},{9,13},{13,9},{2,6},{6,2},{1... | collective-permute-start | bytes 393224 | tf_op jit(solution)/shard_map/ppermute | solution.py:51
  13.3 0.7 %collective-permute-start.3 = (f32[4,32,256]{2,1,0:T(8,128)S(1)}, f32[4,32,256]{2,1,0:T(8,128)S(1)}, u32[]{:S(2)}, u32[]{:S(2)}) collective-permute-start(f32[4,32,256]{2,1,0:T(8,128)S(1)} %shard_map.87.refs_0_), channel_id=1, source_target_pairs={{0,0},{4,8},{8,4},{12,12},{1,1},{5,9},{9,5},{13,13},{2,2},{6,10},{... | collective-permute-start | bytes 393224 | tf_op jit(solution)/shard_map/ppermute | solution.py:50
  14.0 0.0 copy-done.6
  14.0 0.1 maximum_maximum_fusion.refs_0_
  14.1 0.0 copy-start.2
  14.1 0.0 copy-start.4
  14.1 2.1 %collective-permute-start.4 = (f32[8,256]{1,0:T(8,128)S(1)}, f32[8,256]{1,0:T(8,128)S(1)}, u32[]{:S(2)}, u32[]{:S(2)}) collective-permute-start(f32[8,256]{1,0:T(8,128)S(1)} %maximum_maximum_fusion.refs_0_), channel_id=1, source_target_pairs={{0,4},{4,0},{8,12},{12,8},{1,5},{5,1},{9,13},{13,9},{2,6},{6,2},{1... | collective-permute-start | bytes 24584 | tf_op jit(solution)/shard_map/ppermute | solution.py:76
  16.1 0.8 %collective-permute-start.5 = (f32[8,256]{1,0:T(8,128)S(1)}, f32[8,256]{1,0:T(8,128)S(1)}, u32[]{:S(2)}, u32[]{:S(2)}) collective-permute-start(f32[8,256]{1,0:T(8,128)S(1)} %maximum_maximum_fusion.refs_0_), channel_id=1, source_target_pairs={{0,8},{4,12},{8,0},{12,4},{1,9},{5,13},{9,1},{13,5},{2,10},{6,14},... | collective-permute-start | bytes 24584 | tf_op jit(solution)/shard_map/ppermute | solution.py:76
  16.9 1.7 %collective-permute-start.6 = (f32[8,256]{1,0:T(8,128)S(1)}, f32[8,256]{1,0:T(8,128)S(1)}, u32[]{:S(2)}, u32[]{:S(2)}) collective-permute-start(f32[8,256]{1,0:T(8,128)S(1)} %maximum_maximum_fusion.refs_0_), channel_id=1, source_target_pairs={{0,12},{4,8},{8,4},{12,0},{1,13},{5,9},{9,5},{13,1},{2,14},{6,10},... | collective-permute-start | bytes 24584 | tf_op jit(solution)/shard_map/ppermute | solution.py:76
  18.6 0.0 collective-permute-done.4.refs_1_
  18.6 2.1 %collective-permute-done.5.refs_2_ = f32[8,256]{1,0:T(8,128)S(1)} collective-permute-done((f32[8,256]{1,0:T(8,128)S(1)}, f32[8,256]{1,0:T(8,128)S(1)}, u32[]{:S(2)}, u32[]{:S(2)}) %collective-permute-start.5) | collective-permute-done | bytes 8224 | tf_op jit(solution)/shard_map/ppermute | solution.py:76
  20.7 1.7 %collective-permute-done.6.refs_3_ = f32[8,256]{1,0:T(8,128)S(1)} collective-permute-done((f32[8,256]{1,0:T(8,128)S(1)}, f32[8,256]{1,0:T(8,128)S(1)}, u32[]{:S(2)}, u32[]{:S(2)}) %collective-permute-start.6) | collective-permute-done | bytes 8224 | tf_op jit(solution)/shard_map/ppermute | solution.py:76
  22.4 1.4 %shard_map.88 = (f32[4,32,256]{2,1,0:T(8,128)S(1)}, f32[4,32,256]{2,1,0:T(8,128)S(1)}, f32[4,32,256]{2,1,0:T(8,128)S(1)}, f32[4,32,256]{2,1,0:T(8,128)S(1)}, f32...) custom-call(s32[1]{0:T(128)} %bitcast.here_ref, f32[8,256]{1,0:T(8,128)S(1)} %maximum_maximum_fusion.refs_0_, ...), custom_call_target="tpu_custom_call" | custom-call | flops 1207959552 | bytes 32772 | tf_op jit(solution)/shard_map/pallas_call | solution.py:20
  23.8 0.0 copy-done.2
  23.8 0.0 copy-done.4
  23.8 0.4 shard_map.89
  24.2 0.0 collective-permute-done.2.refs_0_
  24.2 0.0 collective-permute-done.3.refs_1_
  24.2 0.1 shard_map.90.refs_0_.refs_1_
  24.3 0.2 collective-permute-start.7
  24.6 0.7 %collective-permute-start.8 = (f32[4,32,256]{2,1,0:T(8,128)S(1)}, f32[4,32,256]{2,1,0:T(8,128)S(1)}, u32[]{:S(2)}, u32[]{:S(2)}) collective-permute-start(f32[4,32,256]{2,1,0:T(8,128)S(1)} %shard_map.90.refs_0_.refs_1_), channel_id=1, source_target_pairs={{0,0},{4,8},{8,4},{12,12},{1,1},{5,9},{9,5},{13,13},{2,2},{6,10},{... | collective-permute-start | bytes 393224 | tf_op jit(solution)/shard_map/ppermute | solution.py:50
  25.2 0.4 shard_map.91
  25.6 3.8 %collective-permute-done.7.refs_0_ = f32[4,32,256]{2,1,0:T(8,128)S(1)} collective-permute-done((f32[4,32,256]{2,1,0:T(8,128)S(1)}, f32[4,32,256]{2,1,0:T(8,128)S(1)}, u32[]{:S(2)}, u32[]{:S(2)}) %collective-permute-start.7) | collective-permute-done | bytes 131104 | tf_op jit(solution)/shard_map/ppermute | solution.py:51
  29.4 0.0 collective-permute-done.8.refs_1_
  29.4 0.1 shard_map.92.refs_0_
  29.5 0.7 %collective-permute-start.10 = (f32[4,32,256]{2,1,0:T(8,128)S(1)}, f32[4,32,256]{2,1,0:T(8,128)S(1)}, u32[]{:S(2)}, u32[]{:S(2)}) collective-permute-start(f32[4,32,256]{2,1,0:T(8,128)S(1)} %shard_map.92.refs_0_), channel_id=1, source_target_pairs={{0,0},{4,8},{8,4},{12,12},{1,1},{5,9},{9,5},{13,13},{2,2},{6,10},{... | collective-permute-start | bytes 393224 | tf_op jit(solution)/shard_map/ppermute | solution.py:50
  30.1 6.0 %collective-permute-start.9 = (f32[4,32,256]{2,1,0:T(8,128)S(1)}, f32[4,32,256]{2,1,0:T(8,128)S(1)}, u32[]{:S(2)}, u32[]{:S(2)}) collective-permute-start(f32[4,32,256]{2,1,0:T(8,128)S(1)} %shard_map.92.refs_0_), channel_id=1, source_target_pairs={{0,4},{4,0},{8,12},{12,8},{1,5},{5,1},{9,13},{13,9},{2,6},{6,2},{1... | collective-permute-start | bytes 393224 | tf_op jit(solution)/shard_map/ppermute | solution.py:51
  36.1 0.4 shard_map.93
  36.5 0.0 collective-permute-done.10.refs_1_
  36.5 2.5 %collective-permute-done.9.refs_0_ = f32[4,32,256]{2,1,0:T(8,128)S(1)} collective-permute-done((f32[4,32,256]{2,1,0:T(8,128)S(1)}, f32[4,32,256]{2,1,0:T(8,128)S(1)}, u32[]{:S(2)}, u32[]{:S(2)}) %collective-permute-start.9) | collective-permute-done | bytes 131104 | tf_op jit(solution)/shard_map/ppermute | solution.py:51
  39.1 0.1 shard_map.94
  39.1 0.1 collective-permute-start.11
  39.2 1.3 %collective-permute-done.11 = f32[4,32,256]{2,1,0:T(8,128)S(1)} collective-permute-done((f32[4,32,256]{2,1,0:T(8,128)S(1)}, f32[4,32,256]{2,1,0:T(8,128)S(1)}, u32[]{:S(2)}, u32[]{:S(2)}) %collective-permute-start.11) | collective-permute-done | bytes 131104 | tf_op jit(solution)/shard_map/ppermute | solution.py:245
  40.6 1.6 %collective-permute-start.12 = (f32[4,32,256]{2,1,0:T(8,128)S(1)}, f32[4,32,256]{2,1,0:T(8,128)S(1)}, u32[]{:S(2)}, u32[]{:S(2)}) collective-permute-start(f32[4,32,256]{2,1,0:T(8,128)S(1)} %add.6), channel_id=1, source_target_pairs={{0,2},{1,3},{2,0},{3,1},{4,6},{5,7},{6,4},{7,5},{8,10},{9,11},{10,... | collective-permute-start | bytes 393224 | tf_op jit(solution)/shard_map/ppermute | solution.py:245
  42.1 0.7 %copy.9 = f32[1,4,32,256]{3,2,1,0:T(8,128)} copy(f32[1,4,32,256]{3,2,1,0:T(8,128)S(1)} %bitcast.9) | data formatting | bytes 262144
  42.8 3.4 %collective-permute-done.12 = f32[4,32,256]{2,1,0:T(8,128)S(1)} collective-permute-done((f32[4,32,256]{2,1,0:T(8,128)S(1)}, f32[4,32,256]{2,1,0:T(8,128)S(1)}, u32[]{:S(2)}, u32[]{:S(2)}) %collective-permute-start.12) | collective-permute-done | bytes 131104 | tf_op jit(solution)/shard_map/ppermute | solution.py:245
  46.2 0.7 %add.7 = f32[4,32,256]{2,1,0:T(8,128)} add(f32[4,32,256]{2,1,0:T(8,128)S(1)} %add.6, f32[4,32,256]{2,1,0:T(8,128)S(1)} %collective-permute-done.12) | non-fusion elementwise | flops 32768 | bytes 393216 | tf_op jit(solution)/shard_map/add | solution.py:245
  (4 shorter events, 0.0 us)
Async XLA Ops:
  0.6 8.8 %collective-permute-start = (f32[4,32,256]{2,1,0:T(8,128)}, f32[4,32,256]{2,1,0:T(8,128)S(1)}, u32[]{:S(2)}, u32[]{:S(2)}) collective-permute-start(f32[4,32,256]{2,1,0:T(8,128)} %bitcast.13), channel_id=1, source_target_pairs={{0,4},{4,0},{8,12},{12,8},{1,5},{5,1},{9,13},{13,9},{2,6},{6,2},{1... | collective-permute-start | bytes 393224 | tf_op jit(solution)/shard_map/ppermute | solution.py:51
  3.7 5.7 %collective-permute-start.1 = (f32[4,32,256]{2,1,0:T(8,128)}, f32[4,32,256]{2,1,0:T(8,128)S(1)}, u32[]{:S(2)}, u32[]{:S(2)}) collective-permute-start(f32[4,32,256]{2,1,0:T(8,128)} %bitcast.14), channel_id=1, source_target_pairs={{0,0},{4,8},{8,4},{12,12},{1,1},{5,9},{9,5},{13,13},{2,2},{6,10},{... | collective-permute-start | bytes 393224 | tf_op jit(solution)/shard_map/ppermute | solution.py:50
  5.3 0.7 %copy-start.7 = (s32[256]{0:T(256)S(1)}, s32[256]{0:T(256)}, u32[]{:S(2)}) copy-start(s32[256]{0:T(256)} %param.12) | copy-start | bytes 3076
  6.0 0.9 %copy-start = (f32[4,32,256]{2,1,0:T(8,128)S(1)}, f32[4,32,256]{2,1,0:T(8,128)}, u32[]{:S(2)}) copy-start(f32[4,32,256]{2,1,0:T(8,128)} %refs_3_.7) | copy-start | bytes 393220
  6.9 0.9 %copy-start.3 = (f32[1,4,32,256]{3,2,1,0:T(8,128)S(1)}, f32[1,4,32,256]{3,2,1,0:T(8,128)}, u32[]{:S(2)}) copy-start(f32[1,4,32,256]{3,2,1,0:T(8,128)} %param.7) | copy-start | bytes 393220
  7.8 0.9 %copy-start.5 = (f32[1,4,32,256]{3,2,1,0:T(8,128)S(1)}, f32[1,4,32,256]{3,2,1,0:T(8,128)}, u32[]{:S(2)}) copy-start(f32[1,4,32,256]{3,2,1,0:T(8,128)} %param.8) | copy-start | bytes 393220
  8.7 0.7 %copy-start.8 = (s32[256,1]{0,1:T(1,128)S(1)}, s32[256,1]{0,1:T(1,128)}, u32[]{:S(2)}) copy-start(s32[256,1]{0,1:T(1,128)} %param.11) | copy-start | bytes 3076
  8.7 0.9 %copy-start.1 = (f32[4,32,256]{2,1,0:T(8,128)S(1)}, f32[4,32,256]{2,1,0:T(8,128)}, u32[]{:S(2)}) copy-start(f32[4,32,256]{2,1,0:T(8,128)} %refs_3_.7) | copy-start | bytes 393220
  9.7 4.3 %copy-start.6 = (f32[1,4,256]{2,1,0:T(4,128)S(1)}, f32[1,4,256]{2,1,0:T(4,128)}, u32[]{:S(2)}) copy-start(f32[1,4,256]{2,1,0:T(4,128)} %param.13) | copy-start | bytes 12292
  9.8 14.5 %collective-permute-start.2 = (f32[4,32,256]{2,1,0:T(8,128)S(1)}, f32[4,32,256]{2,1,0:T(8,128)S(1)}, u32[]{:S(2)}, u32[]{:S(2)}) collective-permute-start(f32[4,32,256]{2,1,0:T(8,128)S(1)} %shard_map.87.refs_0_), channel_id=1, source_target_pairs={{0,4},{4,0},{8,12},{12,8},{1,5},{5,1},{9,13},{13,9},{2,6},{6,2},{1... | collective-permute-start | bytes 393224 | tf_op jit(solution)/shard_map/ppermute | solution.py:51
  13.3 10.9 %collective-permute-start.3 = (f32[4,32,256]{2,1,0:T(8,128)S(1)}, f32[4,32,256]{2,1,0:T(8,128)S(1)}, u32[]{:S(2)}, u32[]{:S(2)}) collective-permute-start(f32[4,32,256]{2,1,0:T(8,128)S(1)} %shard_map.87.refs_0_), channel_id=1, source_target_pairs={{0,0},{4,8},{8,4},{12,12},{1,1},{5,9},{9,5},{13,13},{2,2},{6,10},{... | collective-permute-start | bytes 393224 | tf_op jit(solution)/shard_map/ppermute | solution.py:50
  14.1 9.7 %copy-start.2 = (bf16[1,4,4,32,256]{4,3,2,1,0:T(8,128)(2,1)S(1)}, bf16[1,4,4,32,256]{4,3,2,1,0:T(8,128)(2,1)}, u32[]{:S(2)}) copy-start(bf16[1,4,4,32,256]{4,3,2,1,0:T(8,128)(2,1)} %param.10) | copy-start | bytes 786436
  14.1 9.7 %copy-start.4 = (f32[1,4,32,256]{3,2,1,0:T(8,128)S(1)}, f32[1,4,32,256]{3,2,1,0:T(8,128)}, u32[]{:S(2)}) copy-start(f32[1,4,32,256]{3,2,1,0:T(8,128)} %param.7) | copy-start | bytes 393220
  14.1 4.5 %collective-permute-start.4 = (f32[8,256]{1,0:T(8,128)S(1)}, f32[8,256]{1,0:T(8,128)S(1)}, u32[]{:S(2)}, u32[]{:S(2)}) collective-permute-start(f32[8,256]{1,0:T(8,128)S(1)} %maximum_maximum_fusion.refs_0_), channel_id=1, source_target_pairs={{0,4},{4,0},{8,12},{12,8},{1,5},{5,1},{9,13},{13,9},{2,6},{6,2},{1... | collective-permute-start | bytes 24584 | tf_op jit(solution)/shard_map/ppermute | solution.py:76
  16.1 4.5 %collective-permute-start.5 = (f32[8,256]{1,0:T(8,128)S(1)}, f32[8,256]{1,0:T(8,128)S(1)}, u32[]{:S(2)}, u32[]{:S(2)}) collective-permute-start(f32[8,256]{1,0:T(8,128)S(1)} %maximum_maximum_fusion.refs_0_), channel_id=1, source_target_pairs={{0,8},{4,12},{8,0},{12,4},{1,9},{5,13},{9,1},{13,5},{2,10},{6,14},... | collective-permute-start | bytes 24584 | tf_op jit(solution)/shard_map/ppermute | solution.py:76
  16.9 5.4 %collective-permute-start.6 = (f32[8,256]{1,0:T(8,128)S(1)}, f32[8,256]{1,0:T(8,128)S(1)}, u32[]{:S(2)}, u32[]{:S(2)}) collective-permute-start(f32[8,256]{1,0:T(8,128)S(1)} %maximum_maximum_fusion.refs_0_), channel_id=1, source_target_pairs={{0,12},{4,8},{8,4},{12,0},{1,13},{5,9},{9,5},{13,1},{2,14},{6,10},... | collective-permute-start | bytes 24584 | tf_op jit(solution)/shard_map/ppermute | solution.py:76
  24.3 5.0 %collective-permute-start.7 = (f32[4,32,256]{2,1,0:T(8,128)S(1)}, f32[4,32,256]{2,1,0:T(8,128)S(1)}, u32[]{:S(2)}, u32[]{:S(2)}) collective-permute-start(f32[4,32,256]{2,1,0:T(8,128)S(1)} %shard_map.90.refs_0_.refs_1_), channel_id=1, source_target_pairs={{0,4},{4,0},{8,12},{12,8},{1,5},{5,1},{9,13},{13,9},{2,6},{6,2},{1... | collective-permute-start | bytes 393224 | tf_op jit(solution)/shard_map/ppermute | solution.py:51
  24.6 4.8 %collective-permute-start.8 = (f32[4,32,256]{2,1,0:T(8,128)S(1)}, f32[4,32,256]{2,1,0:T(8,128)S(1)}, u32[]{:S(2)}, u32[]{:S(2)}) collective-permute-start(f32[4,32,256]{2,1,0:T(8,128)S(1)} %shard_map.90.refs_0_.refs_1_), channel_id=1, source_target_pairs={{0,0},{4,8},{8,4},{12,12},{1,1},{5,9},{9,5},{13,13},{2,2},{6,10},{... | collective-permute-start | bytes 393224 | tf_op jit(solution)/shard_map/ppermute | solution.py:50
  29.5 7.0 %collective-permute-start.10 = (f32[4,32,256]{2,1,0:T(8,128)S(1)}, f32[4,32,256]{2,1,0:T(8,128)S(1)}, u32[]{:S(2)}, u32[]{:S(2)}) collective-permute-start(f32[4,32,256]{2,1,0:T(8,128)S(1)} %shard_map.92.refs_0_), channel_id=1, source_target_pairs={{0,0},{4,8},{8,4},{12,12},{1,1},{5,9},{9,5},{13,13},{2,2},{6,10},{... | collective-permute-start | bytes 393224 | tf_op jit(solution)/shard_map/ppermute | solution.py:50
  30.1 8.9 %collective-permute-start.9 = (f32[4,32,256]{2,1,0:T(8,128)S(1)}, f32[4,32,256]{2,1,0:T(8,128)S(1)}, u32[]{:S(2)}, u32[]{:S(2)}) collective-permute-start(f32[4,32,256]{2,1,0:T(8,128)S(1)} %shard_map.92.refs_0_), channel_id=1, source_target_pairs={{0,4},{4,0},{8,12},{12,8},{1,5},{5,1},{9,13},{13,9},{2,6},{6,2},{1... | collective-permute-start | bytes 393224 | tf_op jit(solution)/shard_map/ppermute | solution.py:51
  39.1 1.4 %collective-permute-start.11 = (f32[4,32,256]{2,1,0:T(8,128)S(1)}, f32[4,32,256]{2,1,0:T(8,128)S(1)}, u32[]{:S(2)}, u32[]{:S(2)}) collective-permute-start(f32[4,32,256]{2,1,0:T(8,128)S(1)} %get-tuple-element.33), channel_id=1, source_target_pairs={{0,1},{1,0},{2,3},{3,2},{4,5},{5,4},{6,7},{7,6},{8,9},{9,8},{10,11... | collective-permute-start | bytes 393224 | tf_op jit(solution)/shard_map/ppermute | solution.py:245
  40.6 5.6 %collective-permute-start.12 = (f32[4,32,256]{2,1,0:T(8,128)S(1)}, f32[4,32,256]{2,1,0:T(8,128)S(1)}, u32[]{:S(2)}, u32[]{:S(2)}) collective-permute-start(f32[4,32,256]{2,1,0:T(8,128)S(1)} %add.6), channel_id=1, source_target_pairs={{0,2},{1,3},{2,0},{3,1},{4,6},{5,7},{6,4},{7,5},{8,10},{9,11},{10,... | collective-permute-start | bytes 393224 | tf_op jit(solution)/shard_map/ppermute | solution.py:245

commit v3 on v2

v3 whole, which is shorter than its diff:
```python
import functools

import jax
import jax.numpy as jnp
from jax import lax
from jax.experimental import pallas as pl
from jax.experimental.pallas import tpu as pltpu
from jax.sharding import PartitionSpec as P

CAP = 128
GATHER_LIMIT = 4096
REACH = 4
PIECES = 3

COEFFS = (-205.0 / 72.0, 8.0 / 5.0, -1.0 / 5.0, 8.0 / 315.0, -1.0 / 560.0)


def on_chip(kernel, outs, *args, flops=0, scratch=(), in_hbm=()):
    spaces = [pltpu.SMEM if a.ndim == 1 else pltpu.VMEM for a in args]
    for i in in_hbm:
        spaces[i] = pltpu.HBM
    results = pl.pallas_call(
        kernel,
        out_shape=[pltpu.VMEM(shape, dtype) for shape, dtype in outs],
        in_specs=[pl.BlockSpec(memory_space=s) for s in spaces],
        out_specs=[pl.BlockSpec(memory_space=pltpu.VMEM) for _ in outs],
        scratch_shapes=list(scratch),
        cost_estimate=pl.CostEstimate(
            flops=flops,
            bytes_accessed=sum(a.size * a.dtype.itemsize for a in args),
            transcendentals=0,
        ),
    )(
        *[
            a if s is pltpu.SMEM else pltpu.with_memory_space_constraint(a, s)
            for a, s in zip(args, spaces)
        ]
    )
    return list(results)


def swap_pairs(count, first):
    partner = list(range(count))
    for left in range(first, count - 1, 2):
        partner[left], partner[left + 1] = left + 1, left
    return list(enumerate(partner))


def exchange(to_inner, to_outer):
    count = lax.axis_size("tgt")
    outer = lax.ppermute(to_outer, "tgt", swap_pairs(count, 1))
    inner = lax.ppermute(to_inner, "tgt", swap_pairs(count, 0))
    return inner, outer


def slotted_tables(table, surf_dest, owners):
    target = surf_dest[:, 0]
    onehot_table = (target[:, None] == jnp.arange(owners, dtype=jnp.int32)[None, :]).astype(
        jnp.int32
    )
    ranks = jnp.sum((jnp.cumsum(onehot_table, axis=0) - 1) * onehot_table, axis=1)
    position = target * CAP + ranks
    slots = jnp.full((table.shape[0], owners * CAP), -1.0, jnp.float32)
    slots = slots.at[:, position].set(table)
    arrived = lax.all_to_all(
        slots.reshape(-1, owners, CAP), "tgt", split_axis=1, concat_axis=1, tiled=True
    )
    flat = arrived.reshape(-1, owners * CAP)
    chunk = 1024 if owners * CAP % 1024 == 0 else CAP
    return [flat[:, i : i + chunk] for i in range(0, owners * CAP, chunk)]


def inject_kernel(steps, first_rows, with_halo, here_ref, *refs):
    table_refs, out_refs = refs[: len(first_rows)], refs[len(first_rows) :]
    rows, lanes = out_refs[0].shape
    here = here_ref[0].astype(jnp.float32)
    left, right = [], []
    for table_ref, firsts in zip(table_refs, first_rows):
        for first in firsts:
            table = table_ref[first : first + 2 + steps]
            count = table.shape[1]
            slab = table[0:1]
            cell = table[1:2].astype(jnp.int32)
            row, lane = cell // lanes, cell % lanes
            in_lane = lax.broadcasted_iota(jnp.int32, (lanes, count), 0) == lane
            spread = jnp.where(in_lane, 1.0, 0.0).astype(jnp.bfloat16)
            each_row = lax.broadcasted_iota(jnp.int32, (rows, count), 0)
            in_row = [each_row == jnp.where(slab == here, row, -1)]
            if with_halo:
                in_row.append(each_row == jnp.where(slab == here - 1.0, row, -1))
                in_row.append(each_row == jnp.where(slab == here + 1.0, row, -1))
            rest = [table[2 + step : 3 + step] for step in range(steps)]
            for _ in range(PIECES):
                part = [r.astype(jnp.bfloat16).astype(jnp.float32) for r in rest]
                rest = [r - p for r, p in zip(rest, part)]
                picks = [(in_row[0], p) for p in part] + [(m, part[0]) for m in in_row[1:]]
                left.append(
                    jnp.concatenate(
                        [jnp.where(m, p, 0.0).astype(jnp.bfloat16) for m, p in picks], axis=0
                    )
                )
                right.append(spread)
    total = lax.dot_general(
        jnp.concatenate(left, axis=1),
        jnp.concatenate(right, axis=1),
        (((1,), (1,)), ((), ())),
        preferred_element_type=jnp.float32,
    )
    for i, out_ref in enumerate(out_refs):
        out_ref[...] = total[i * rows : (i + 1) * rows]


def injection(here, tables, first_rows, steps, shape, with_halo):
    count = steps + 2 * with_halo
    entries = sum(t.shape[1] * len(f) for t, f in zip(tables, first_rows))
    return on_chip(
        functools.partial(inject_kernel, steps, first_rows, with_halo),
        [(shape, jnp.float32)] * count,
        here,
        *tables,
        flops=2 * PIECES * count * shape[0] * shape[1] * entries,
    )


def plane_stencil(plane):
    cells_y, lanes = plane.shape
    at_y = lax.broadcasted_iota(jnp.int32, plane.shape, 0)
    at_z = lax.broadcasted_iota(jnp.int32, plane.shape, 1)
    total = 3.0 * COEFFS[0] * plane
    for k in range(1, REACH + 1):
        pairs = (
            jnp.where(at_y >= k, pltpu.roll(plane, k, 0), 0.0)
            + jnp.where(at_y < cells_y - k, pltpu.roll(plane, cells_y - k, 0), 0.0)
            + jnp.where(at_z >= k, pltpu.roll(plane, k, 1), 0.0)
            + jnp.where(at_z < lanes - k, pltpu.roll(plane, lanes - k, 1), 0.0)
        )
        total = total + COEFFS[k] * pairs
    return total


def own_part(current, p, later, courant):
    total = plane_stencil(current[p])
    for k in range(1, REACH + 1):
        for q in (p - k, p + k):
            if 0 <= q < len(current):
                total = total + COEFFS[k] * current[q]
    return 2.0 * current[p] - later + courant * courant * total


def first_kernel(planes, table_rows, *refs):
    refs = list(refs)
    now_hbm, later_hbm, courant_hbm, fwd_hbm, dest_hbm, cell_hbm, vals_hbm = refs[:7]
    part_ref, table_ref, now_ref, courant_ref, fwd_ref = refs[7:12]
    later_ref, dest_ref, cell_ref, vals_ref, sems = refs[12:]
    pairs = [
        (dest_hbm, dest_ref),
        (cell_hbm, cell_ref),
        (vals_hbm, vals_ref),
        (now_hbm, now_ref),
        (later_hbm, later_ref),
        (courant_hbm, courant_ref),
        (fwd_hbm, fwd_ref),
    ]
    copies = [pltpu.make_async_copy(a, b, sems.at[i]) for i, (a, b) in enumerate(pairs)]
    for copy in copies:
        copy.start()
    for copy in copies[:3]:
        copy.wait()
    table_ref[...] = jnp.zeros_like(table_ref)
    table_ref[0:1] = dest_ref[...].astype(jnp.float32)
    table_ref[1:2] = cell_ref[...].astype(jnp.float32)
    table_ref[2 : 2 + vals_ref.shape[0]] = vals_ref[...]
    for copy in copies[3:6]:
        copy.wait()
    cells_y = now_ref.shape[0] // planes
    at = [slice(p * cells_y, (p + 1) * cells_y) for p in range(planes)]
    current = [now_ref[s] for s in at]
    for p, s in enumerate(at):
        part_ref[s] = own_part(current, p, later_ref[s], courant_ref[s])
    copies[6].wait()


def own_kernel(planes, step, fix_inject, last, *refs):
    refs = list(refs)
    current_ref, later_ref, courant_ref, fwd_ref, inject_ref = refs[:5]
    refs = refs[5:]
    fix_ref = refs.pop(0) if fix_inject else None
    grad_in_ref = refs.pop(0) if step > 1 else None
    part_ref = refs.pop(0)
    grad_ref = refs.pop(0)
    fixed_ref = refs.pop(0) if fix_inject else None
    weight_ref = refs.pop(0) if last else None
    cells_y = current_ref.shape[0] // planes
    at = [slice(p * cells_y, (p + 1) * cells_y) for p in range(planes)]
    current = [current_ref[s] for s in at]
    if fix_inject:
        current = [c + fix_ref[s] for c, s in zip(current, at)]
        for c, s in zip(current, at):
            fixed_ref[s] = c
    for p, s in enumerate(at):
        courant = courant_ref[s]
        part_ref[s] = own_part(current, p, later_ref[s], courant) + inject_ref[s]
        grad = fwd_ref[step - 1, s].astype(jnp.float32) * current[p]
        if step > 1:
            grad = grad + grad_in_ref[s]
        if last:
            inverse = 1.0 / courant
            grad = grad * inverse
            weight_ref[s] = fwd_ref[step, s].astype(jnp.float32) * inverse
        grad_ref[s] = grad


def halo_kernel(planes, slabs, fix_inject, last, tables, here_ref, *refs):
    refs = list(refs)
    inner_ref, outer_ref, part_ref, courant_ref = refs[:4]
    refs = refs[4:]
    fix_refs = (refs.pop(0), refs.pop(0)) if fix_inject else None
    weight_ref, grad_in_ref = (refs.pop(0), refs.pop(0)) if last else (None, None)
    table_refs = [refs.pop(0) for _ in range(tables)]
    fresh_ref = refs.pop(0)
    other_ref = refs.pop(0) if last or tables else None
    here = here_ref[0]
    even = here % 2 == 0
    rows = part_ref.shape[0]
    cells_y = rows // planes
    at = [slice(p * cells_y, (p + 1) * cells_y) for p in range(planes)]
    low, high = {}, {}
    for p in range(planes - REACH, planes):
        plane = jnp.where(even, outer_ref[at[p]], inner_ref[at[p]])
        if fix_inject:
            plane = plane + fix_refs[0][at[p]]
        low[p - planes] = jnp.where(here == 0, 0.0, plane)
    for p in range(REACH):
        plane = jnp.where(even, inner_ref[at[p]], outer_ref[at[p]])
        if fix_inject:
            plane = plane + fix_refs[1][at[p]]
        high[p + planes] = jnp.where(here == slabs - 1, 0.0, plane)
    for p, s in enumerate(at):
        terms = []
        for k in range(1, REACH + 1):
            if p - k < 0:
                terms.append(COEFFS[k] * low[p - k])
            if p + k >= planes:
                terms.append(COEFFS[k] * high[p + k])
        courant = courant_ref[s]
        fresh = part_ref[s] + courant * courant * sum(terms[1:], terms[0])
        fresh_ref[s] = fresh
        if last:
            other_ref[s] = grad_in_ref[s] + weight_ref[s] * fresh
        if tables:
            other_ref[s] = fresh
    for i, table_ref in enumerate(table_refs):
        first = rows + i * table_ref.shape[0]
        other_ref[first : first + table_ref.shape[0]] = table_ref[...]


def sum_over(value, axis):
    count = lax.axis_size(axis)
    if count & (count - 1):
        return lax.psum(value, axis)
    distance = 1
    while distance < count:
        value = value + lax.ppermute(value, axis, [(i, i ^ distance) for i in range(count)])
        distance *= 2
    return value


def on_device(adjoint_now, adjoint_later, courant, fwd_acc, surf_dest, surf_cell, surf_vals):
    planes, cells_y, lanes = courant.shape
    steps = fwd_acc.shape[1]
    rows = planes * cells_y
    shape = (rows, lanes)
    entries = surf_cell.shape[0]
    slabs = lax.axis_size("tgt")
    here = lax.axis_index("tgt").reshape(1)
    now = adjoint_now.reshape(shape)
    table_rows = -(-(2 + steps) // 8) * 8
    everywhere = (
        slabs & (slabs - 1) == 0 and slabs * entries <= GATHER_LIMIT and entries == lanes
    )

    received = exchange(now, now)
    f32 = jnp.float32
    part, table, current, courant_here, fwd = on_chip(
        functools.partial(first_kernel, planes, table_rows),
        [
            (shape, f32),
            ((table_rows, entries), f32),
            (shape, f32),
            (shape, f32),
            ((steps, rows, lanes), fwd_acc.dtype),
        ],
        now,
        adjoint_later.reshape(shape),
        courant.reshape(shape),
        fwd_acc.reshape(steps, rows, lanes),
        surf_dest.reshape(1, entries),
        surf_cell.reshape(1, entries),
        surf_vals.reshape(steps, entries),
        flops=40 * rows * lanes,
        scratch=[
            pltpu.VMEM(shape, f32),
            pltpu.VMEM((1, entries), surf_dest.dtype),
            pltpu.VMEM((1, entries), surf_cell.dtype),
            pltpu.VMEM((steps, entries), f32),
            pltpu.SemaphoreType.DMA((7,)),
        ],
        in_hbm=range(7),
    )
    if everywhere:
        tables = [table] + [
            lax.ppermute(table, "tgt", [(i, i ^ far) for i in range(slabs)])
            for far in range(2, slabs, 2)
        ]
        inject = None
    else:
        tables = slotted_tables(table, surf_dest, slabs)
        inject = injection(here, tables, [[0]] * len(tables), steps, shape, False)
        part = part + inject[0]
        tables = []

    fixes, extra, later_field, grad = [], [], None, None
    for step in range(steps):
        last = step == steps - 1
        fix = everywhere and step == 1
        if step:
            outs = [(shape, f32)] * (2 + fix + last)
            args = [current, later_field, courant_here, fwd, inject[step]]
            args += [inject[0]] if fix else []
            args += [grad] if step > 1 else []
            part, grad, *extra = on_chip(
                functools.partial(own_kernel, planes, step, fix, last),
                outs,
                *args,
                flops=40 * rows * lanes,
            )
            if fix:
                current = extra.pop(0)
        carried = tables if step == 0 else []
        args = [here, *received, part, courant_here, *fixes]
        args += [*extra, grad] if last else []
        outs = [(shape, f32)] + ([(shape, f32)] if last else [])
        if carried:
            outs.append(((rows + len(carried) * table_rows, lanes), f32))
        fresh, *other = on_chip(
            functools.partial(halo_kernel, planes, slabs, fix, last, len(carried)),
            outs,
            *args,
            *carried,
            flops=10 * rows * lanes,
        )
        later_field, current, fixes = current, fresh, []
        if not last:
            received = exchange(other[0] if carried else fresh, fresh)
        if carried:
            places = [rows + i * table_rows for i in range(len(carried))]
            first_rows = [[0]] * len(carried) + [places]
            inject = injection(here, [*tables, received[0]], first_rows, steps, shape, True)
            fixes = inject[steps:]
    grad = sum_over(other[0], "shot")
    return (current.reshape(adjoint_now.shape), grad.reshape(courant.shape))


def solution(mesh):
    in_specs = (
        P(("grp", "shot"), "tgt", None, None),
        P(("grp", "shot"), "tgt", None, None),
        P("tgt", None, None),
        P(("grp", "shot"), None, "tgt", None, None),
        P("tgt", None),
        P("tgt"),
        P(("grp", "shot"), None, "tgt"),
    )
    out_specs = (P(("grp", "shot"), "tgt", None, None), P(("grp", "tgt"), None, None))
    return jax.shard_map(
        on_device, mesh=mesh, in_specs=in_specs, out_specs=out_specs, check_vma=False
    )
```

time: 47.2 us -> 41.1 us (0.87)
  the two profiles are of different devices: /device:TPU:0 before, /device:TPU:8 now
where the time goes in v3:
time: 41.1 us; the launch traced here: 40.9 us
  waiting for transfers between devices  19.5 us (47%)
  starting transfers between devices  14.9 us (36%)
  Pallas kernels  4.47 us (11%)
  between operations  0.79 us (2%)
  other arithmetic  0.69 us (2%)
  local copies, waits for them, and re-layouts  0.65 us (2%)
    ppermute x4, starting transfers between devices, exchange(): outer = lax.ppermute(to_outer, 'tgt', swap_pairs(count, 1))  12.9 us
    ppermute x4, waiting for transfers between devices, exchange(): inner = lax.ppermute(to_inner, 'tgt', swap_pairs(count, 0))  6.38 us
    ppermute x2, waiting for transfers between devices, sum_over(): lax.ppermute(value, axis, [(i, i ^ distance) for i in range(count)])  4.74 us
    ppermute x1, waiting for transfers between devices, on_device(): lax.ppermute(table, 'tgt', [(i, i ^ far) for i in range(slabs)])  4.53 us
    pallas_call x9, Pallas kernels, on_chip(): pl.pallas_call(kernel, out_shape=[pltpu.VMEM(shape, dtype) for shape, dty...  4.47 us
    ppermute x4, waiting for transfers between devices, exchange(): outer = lax.ppermute(to_outer, 'tgt', swap_pairs(count, 1))  3.82 us
    ppermute x2, starting transfers between devices, sum_over(): lax.ppermute(value, axis, [(i, i ^ distance) for i in range(count)])  1.63 us
  transfers between devices with their start and end apart: 11, of which 8 were waited for; matrix products, arithmetic and copies ran while one was open for 2% of the time, Pallas kernels for 10%

profile of v3, /device:TPU:8, one launch (start us, length us, event | category | flops | bytes accessed | tf_op | source)
XLA Modules:
  0.0 40.9 jit_solution(11302005964080156188)
XLA Ops:
  0.6 0.1 collective-permute-start
  0.7 5.0 %collective-permute-start.1 = (f32[128,256]{1,0:T(8,128)}, f32[128,256]{1,0:T(8,128)S(1)}, u32[]{:S(2)}, u32[]{:S(2)}) collective-permute-start(f32[128,256]{1,0:T(8,128)} %bitcast.15), channel_id=1, source_target_pairs={{0,0},{4,8},{8,4},{12,12},{1,1},{5,9},{9,5},{13,13},{2,2},{6,10},{... | collective-permute-start | bytes 393224 | tf_op jit(solution)/shard_map/ppermute | solution.py:51
  5.8 1.5 %shard_map.86 = (f32[128,256]{1,0:T(8,128)S(1)}, f32[8,256]{1,0:T(8,128)S(1)}, f32[128,256]{1,0:T(8,128)S(1)}, f32[128,256]{1,0:T(8,128)S(1)}, bf16[4,128,256]{2,1,0:T(8,128)(2,1)S(1)}) custom-call(f32[128,256]{1,0:T(8,128)} %bitcast.16, f32[128,256]{1,0:T(8,128)} %bitcast.12, f32[128,256]{1,0:T(8,128)} %bitcast.13, bf16[4,128,256]{2,1,0:T(8,128)(2,1)} %bitcast.11, ...), custom_call_target="tpu_custom_call" | custom-call | flops 1310720 | bytes 661504 | tf_op jit(solution)/shard_map/pallas_call | solution.py:22
  7.3 0.1 collective-permute-start.2
  7.4 4.5 %collective-permute-done.2.refs_5_.refs_1_ = f32[8,256]{1,0:T(8,128)S(1)} collective-permute-done((f32[8,256]{1,0:T(8,128)S(1)}, f32[8,256]{1,0:T(8,128)S(1)}, u32[]{:S(2)}, u32[]{:S(2)}) %collective-permute-start.2) | collective-permute-done | bytes 8224 | tf_op jit(solution)/shard_map/ppermute | solution.py:312
  11.9 0.0 collective-permute-done.refs_0_
  11.9 0.0 collective-permute-done.1.refs_1_
  11.9 0.1 shard_map.87
  12.0 0.1 collective-permute-start.3
  12.1 2.6 %collective-permute-start.4 = (f32[128,256]{1,0:T(8,128)S(1)}, f32[128,256]{1,0:T(8,128)S(1)}, u32[]{:S(2)}, u32[]{:S(2)}) collective-permute-start(f32[128,256]{1,0:T(8,128)S(1)} %get-tuple-element.29.refs_0_), channel_id=1, source_target_pairs={{0,0},{4,8},{8,4},{12,12},{1,1},{5,9},{9,5},{13,13},{2,2},{6,10},{... | collective-permute-start | bytes 393224 | tf_op jit(solution)/shard_map/ppermute | solution.py:51
  14.7 2.5 %collective-permute-done.3.refs_2_.refs_0_ = f32[144,256]{1,0:T(8,128)S(1)} collective-permute-done((f32[144,256]{1,0:T(8,128)S(1)}, f32[144,256]{1,0:T(8,128)S(1)}, u32[]{:S(2)}, u32[]{:S(2)}) %collective-permute-start.3) | collective-permute-done | bytes 147488 | tf_op jit(solution)/shard_map/ppermute | solution.py:52
  17.2 1.4 %shard_map.88 = (f32[128,256]{1,0:T(8,128)S(1)}, f32[128,256]{1,0:T(8,128)S(1)}, f32[128,256]{1,0:T(8,128)S(1)}, f32[128,256]{1,0:T(8,128)S(1)}, f32[128,256]{1,0:T(8,128)S(1)}, /*index=5*/f32[128,256]{1,0:T(8,128)S(1)}) custom-call(s32[1]{0:T(128)} %bitcast.here_ref, f32[8,256]{1,0:T(8,128)S(1)} %get-tuple-element.27.refs_4_.refs_0_, ...), custom_call_target="tpu_custom_call" | custom-call | flops 1207959552 | bytes 163844 | tf_op jit(solution)/shard_map/pallas_call | solution.py:22
  18.6 0.4 shard_map.89
  19.0 0.0 collective-permute-done.4.refs_1_
  19.0 0.1 shard_map.90.refs_0_.refs_1_
  19.1 0.1 collective-permute-start.5
  19.2 2.6 %collective-permute-start.6 = (f32[128,256]{1,0:T(8,128)S(1)}, f32[128,256]{1,0:T(8,128)S(1)}, u32[]{:S(2)}, u32[]{:S(2)}) collective-permute-start(f32[128,256]{1,0:T(8,128)S(1)} %shard_map.90.refs_0_.refs_1_), channel_id=1, source_target_pairs={{0,0},{4,8},{8,4},{12,12},{1,1},{5,9},{9,5},{13,13},{2,2},{6,10},{... | collective-permute-start | bytes 393224 | tf_op jit(solution)/shard_map/ppermute | solution.py:51
  21.9 0.4 shard_map.91
  22.2 1.9 %collective-permute-done.5.refs_0_ = f32[128,256]{1,0:T(8,128)S(1)} collective-permute-done((f32[128,256]{1,0:T(8,128)S(1)}, f32[128,256]{1,0:T(8,128)S(1)}, u32[]{:S(2)}, u32[]{:S(2)}) %collective-permute-start.5) | collective-permute-done | bytes 131104 | tf_op jit(solution)/shard_map/ppermute | solution.py:52
  24.2 1.9 %collective-permute-done.6.refs_1_ = f32[128,256]{1,0:T(8,128)S(1)} collective-permute-done((f32[128,256]{1,0:T(8,128)S(1)}, f32[128,256]{1,0:T(8,128)S(1)}, u32[]{:S(2)}, u32[]{:S(2)}) %collective-permute-start.6) | collective-permute-done | bytes 131104 | tf_op jit(solution)/shard_map/ppermute | solution.py:51
  26.1 0.1 shard_map.92.refs_0_
  26.2 0.1 collective-permute-start.7
  26.3 2.6 %collective-permute-start.8 = (f32[128,256]{1,0:T(8,128)S(1)}, f32[128,256]{1,0:T(8,128)S(1)}, u32[]{:S(2)}, u32[]{:S(2)}) collective-permute-start(f32[128,256]{1,0:T(8,128)S(1)} %shard_map.92.refs_0_), channel_id=1, source_target_pairs={{0,0},{4,8},{8,4},{12,12},{1,1},{5,9},{9,5},{13,13},{2,2},{6,10},{... | collective-permute-start | bytes 393224 | tf_op jit(solution)/shard_map/ppermute | solution.py:51
  28.9 0.4 shard_map.93
  29.3 1.9 %collective-permute-done.7.refs_0_ = f32[128,256]{1,0:T(8,128)S(1)} collective-permute-done((f32[128,256]{1,0:T(8,128)S(1)}, f32[128,256]{1,0:T(8,128)S(1)}, u32[]{:S(2)}, u32[]{:S(2)}) %collective-permute-start.7) | collective-permute-done | bytes 131104 | tf_op jit(solution)/shard_map/ppermute | solution.py:52
  31.2 1.9 %collective-permute-done.8.refs_1_ = f32[128,256]{1,0:T(8,128)S(1)} collective-permute-done((f32[128,256]{1,0:T(8,128)S(1)}, f32[128,256]{1,0:T(8,128)S(1)}, u32[]{:S(2)}, u32[]{:S(2)}) %collective-permute-start.8) | collective-permute-done | bytes 131104 | tf_op jit(solution)/shard_map/ppermute | solution.py:51
  33.1 0.1 shard_map.94
  33.2 0.1 collective-permute-start.9
  33.3 1.3 %collective-permute-done.9 = f32[128,256]{1,0:T(8,128)S(1)} collective-permute-done((f32[128,256]{1,0:T(8,128)S(1)}, f32[128,256]{1,0:T(8,128)S(1)}, u32[]{:S(2)}, u32[]{:S(2)}) %collective-permute-start.9) | collective-permute-done | bytes 131104 | tf_op jit(solution)/shard_map/ppermute | solution.py:263
  34.6 1.6 %collective-permute-start.10 = (f32[128,256]{1,0:T(8,128)S(1)}, f32[128,256]{1,0:T(8,128)S(1)}, u32[]{:S(2)}, u32[]{:S(2)}) collective-permute-start(f32[128,256]{1,0:T(8,128)S(1)} %add.6), channel_id=1, source_target_pairs={{0,2},{1,3},{2,0},{3,1},{4,6},{5,7},{6,4},{7,5},{8,10},{9,11},{10,... | collective-permute-start | bytes 393224 | tf_op jit(solution)/shard_map/ppermute | solution.py:263
  36.2 0.7 %copy.9 = f32[1,4,32,256]{3,2,1,0:T(8,128)} copy(f32[1,4,32,256]{3,2,1,0:T(8,128)S(1)} %bitcast.10) | data formatting | bytes 262144
  36.9 3.4 %collective-permute-done.10 = f32[128,256]{1,0:T(8,128)S(1)} collective-permute-done((f32[128,256]{1,0:T(8,128)S(1)}, f32[128,256]{1,0:T(8,128)S(1)}, u32[]{:S(2)}, u32[]{:S(2)}) %collective-permute-start.10) | collective-permute-done | bytes 131104 | tf_op jit(solution)/shard_map/ppermute | solution.py:263
  40.3 0.7 %add.7 = f32[128,256]{1,0:T(8,128)} add(f32[128,256]{1,0:T(8,128)S(1)} %add.6, f32[128,256]{1,0:T(8,128)S(1)} %collective-permute-done.10) | non-fusion elementwise | flops 32768 | bytes 393216 | tf_op jit(solution)/shard_map/add | solution.py:263
  (1 shorter events, 0.0 us)
Async XLA Ops:
  0.6 11.3 %collective-permute-start = (f32[128,256]{1,0:T(8,128)}, f32[128,256]{1,0:T(8,128)S(1)}, u32[]{:S(2)}, u32[]{:S(2)}) collective-permute-start(f32[128,256]{1,0:T(8,128)} %bitcast.14), channel_id=1, source_target_pairs={{0,4},{4,0},{8,12},{12,8},{1,5},{5,1},{9,13},{13,9},{2,6},{6,2},{1... | collective-permute-start | bytes 393224 | tf_op jit(solution)/shard_map/ppermute | solution.py:52
  0.7 11.2 %collective-permute-start.1 = (f32[128,256]{1,0:T(8,128)}, f32[128,256]{1,0:T(8,128)S(1)}, u32[]{:S(2)}, u32[]{:S(2)}) collective-permute-start(f32[128,256]{1,0:T(8,128)} %bitcast.15), channel_id=1, source_target_pairs={{0,0},{4,8},{8,4},{12,12},{1,1},{5,9},{9,5},{13,13},{2,2},{6,10},{... | collective-permute-start | bytes 393224 | tf_op jit(solution)/shard_map/ppermute | solution.py:51
  7.3 4.6 %collective-permute-start.2 = (f32[8,256]{1,0:T(8,128)S(1)}, f32[8,256]{1,0:T(8,128)S(1)}, u32[]{:S(2)}, u32[]{:S(2)}) collective-permute-start(f32[8,256]{1,0:T(8,128)S(1)} %get-tuple-element.27.refs_4_.refs_0_), channel_id=1, source_target_pairs={{0,8},{4,12},{8,0},{12,4},{1,9},{5,13},{9,1},{13,5},{2,10},{6,14},... | collective-permute-start | bytes 24584 | tf_op jit(solution)/shard_map/ppermute | solution.py:312
  12.0 5.2 %collective-permute-start.3 = (f32[144,256]{1,0:T(8,128)S(1)}, f32[144,256]{1,0:T(8,128)S(1)}, u32[]{:S(2)}, u32[]{:S(2)}) collective-permute-start(f32[144,256]{1,0:T(8,128)S(1)} %get-tuple-element.28), channel_id=1, source_target_pairs={{0,4},{4,0},{8,12},{12,8},{1,5},{5,1},{9,13},{13,9},{2,6},{6,2},{1... | collective-permute-start | bytes 442376 | tf_op jit(solution)/shard_map/ppermute | solution.py:52
  12.1 7.0 %collective-permute-start.4 = (f32[128,256]{1,0:T(8,128)S(1)}, f32[128,256]{1,0:T(8,128)S(1)}, u32[]{:S(2)}, u32[]{:S(2)}) collective-permute-start(f32[128,256]{1,0:T(8,128)S(1)} %get-tuple-element.29.refs_0_), channel_id=1, source_target_pairs={{0,0},{4,8},{8,4},{12,12},{1,1},{5,9},{9,5},{13,13},{2,2},{6,10},{... | collective-permute-start | bytes 393224 | tf_op jit(solution)/shard_map/ppermute | solution.py:51
  19.1 5.0 %collective-permute-start.5 = (f32[128,256]{1,0:T(8,128)S(1)}, f32[128,256]{1,0:T(8,128)S(1)}, u32[]{:S(2)}, u32[]{:S(2)}) collective-permute-start(f32[128,256]{1,0:T(8,128)S(1)} %shard_map.90.refs_0_.refs_1_), channel_id=1, source_target_pairs={{0,4},{4,0},{8,12},{12,8},{1,5},{5,1},{9,13},{13,9},{2,6},{6,2},{1... | collective-permute-start | bytes 393224 | tf_op jit(solution)/shard_map/ppermute | solution.py:52
  19.2 6.9 %collective-permute-start.6 = (f32[128,256]{1,0:T(8,128)S(1)}, f32[128,256]{1,0:T(8,128)S(1)}, u32[]{:S(2)}, u32[]{:S(2)}) collective-permute-start(f32[128,256]{1,0:T(8,128)S(1)} %shard_map.90.refs_0_.refs_1_), channel_id=1, source_target_pairs={{0,0},{4,8},{8,4},{12,12},{1,1},{5,9},{9,5},{13,13},{2,2},{6,10},{... | collective-permute-start | bytes 393224 | tf_op jit(solution)/shard_map/ppermute | solution.py:51
  26.2 5.0 %collective-permute-start.7 = (f32[128,256]{1,0:T(8,128)S(1)}, f32[128,256]{1,0:T(8,128)S(1)}, u32[]{:S(2)}, u32[]{:S(2)}) collective-permute-start(f32[128,256]{1,0:T(8,128)S(1)} %shard_map.92.refs_0_), channel_id=1, source_target_pairs={{0,4},{4,0},{8,12},{12,8},{1,5},{5,1},{9,13},{13,9},{2,6},{6,2},{1... | collective-permute-start | bytes 393224 | tf_op jit(solution)/shard_map/ppermute | solution.py:52
  26.3 6.9 %collective-permute-start.8 = (f32[128,256]{1,0:T(8,128)S(1)}, f32[128,256]{1,0:T(8,128)S(1)}, u32[]{:S(2)}, u32[]{:S(2)}) collective-permute-start(f32[128,256]{1,0:T(8,128)S(1)} %shard_map.92.refs_0_), channel_id=1, source_target_pairs={{0,0},{4,8},{8,4},{12,12},{1,1},{5,9},{9,5},{13,13},{2,2},{6,10},{... | collective-permute-start | bytes 393224 | tf_op jit(solution)/shard_map/ppermute | solution.py:51
  33.2 1.4 %collective-permute-start.9 = (f32[128,256]{1,0:T(8,128)S(1)}, f32[128,256]{1,0:T(8,128)S(1)}, u32[]{:S(2)}, u32[]{:S(2)}) collective-permute-start(f32[128,256]{1,0:T(8,128)S(1)} %get-tuple-element.47), channel_id=1, source_target_pairs={{0,1},{1,0},{2,3},{3,2},{4,5},{5,4},{6,7},{7,6},{8,9},{9,8},{10,11... | collective-permute-start | bytes 393224 | tf_op jit(solution)/shard_map/ppermute | solution.py:263
  34.6 5.6 %collective-permute-start.10 = (f32[128,256]{1,0:T(8,128)S(1)}, f32[128,256]{1,0:T(8,128)S(1)}, u32[]{:S(2)}, u32[]{:S(2)}) collective-permute-start(f32[128,256]{1,0:T(8,128)S(1)} %add.6), channel_id=1, source_target_pairs={{0,2},{1,3},{2,0},{3,1},{4,6},{5,7},{6,4},{7,5},{8,10},{9,11},{10,... | collective-permute-start | bytes 393224 | tf_op jit(solution)/shard_map/ppermute | solution.py:263

commit v4 on v3

--- a/solution.py
+++ b/solution.py
@@ -70,8 +70,9 @@
     return [flat[:, i : i + chunk] for i in range(0, owners * CAP, chunk)]
 
 
-def inject_kernel(steps, first_rows, with_halo, here_ref, *refs):
-    table_refs, out_refs = refs[: len(first_rows)], refs[len(first_rows) :]
+def inject_kernel(steps, first_rows, with_halo, more, here_ref, *refs):
+    table_refs, refs = refs[: len(first_rows)], refs[len(first_rows) :]
+    in_refs, out_refs = (refs[: len(refs) // 2], refs[len(refs) // 2 :]) if more else ((), refs)
     rows, lanes = out_refs[0].shape
     here = here_ref[0].astype(jnp.float32)
     left, right = [], []
@@ -107,18 +108,20 @@
         preferred_element_type=jnp.float32,
     )
     for i, out_ref in enumerate(out_refs):
-        out_ref[...] = total[i * rows : (i + 1) * rows]
-
-
-def injection(here, tables, first_rows, steps, shape, with_halo):
+        mine = total[i * rows : (i + 1) * rows]
+        out_ref[...] = in_refs[i][...] + mine if more else mine
+
+
+def injection(here, tables, first_rows, steps, shape, with_halo, before=()):
     count = steps + 2 * with_halo
     entries = sum(t.shape[1] * len(f) for t, f in zip(tables, first_rows))
     return on_chip(
-        functools.partial(inject_kernel, steps, first_rows, with_halo),
+        functools.partial(inject_kernel, steps, first_rows, with_halo, len(before) > 0),
         [(shape, jnp.float32)] * count,
         here,
         *tables,
-        flops=2 * PIECES * count * shape[0] * shape[1] * entries,
+        *before,
+        flops=4 * 2 * PIECES * count * shape[0] * shape[1] * entries,
     )
 
 
@@ -258,10 +261,10 @@
     count = lax.axis_size(axis)
     if count & (count - 1):
         return lax.psum(value, axis)
-    distance = 1
-    while distance < count:
+    distance = count // 2
+    while distance:
         value = value + lax.ppermute(value, axis, [(i, i ^ distance) for i in range(count)])
-        distance *= 2
+        distance //= 2
     return value
 
 
@@ -310,7 +313,7 @@
     if everywhere:
         tables = [table] + [
             lax.ppermute(table, "tgt", [(i, i ^ far) for i in range(slabs)])
-            for far in range(2, slabs, 2)
+            for far in range(2, slabs)
         ]
         inject = None
     else:
@@ -336,7 +339,7 @@
             )
             if fix:
                 current = extra.pop(0)
-        carried = tables if step == 0 else []
+        carried = tables[:1] if step == 0 else []
         args = [here, *received, part, courant_here, *fixes]
         args += [*extra, grad] if last else []
         outs = [(shape, f32)] + ([(shape, f32)] if last else [])
@@ -353,9 +356,8 @@
         if not last:
             received = exchange(other[0] if carried else fresh, fresh)
         if carried:
-            places = [rows + i * table_rows for i in range(len(carried))]
-            first_rows = [[0]] * len(carried) + [places]
-            inject = injection(here, [*tables, received[0]], first_rows, steps, shape, True)
+            inject = injection(here, tables, [[0]] * len(tables), steps, shape, True)
+            inject = injection(here, received[:1], [[rows]], steps, shape, True, inject)
             fixes = inject[steps:]
     grad = sum_over(other[0], "shot")
     return (current.reshape(adjoint_now.shape), grad.reshape(courant.shape))

time: 41.1 us -> 40.6 us (0.988)
  the two profiles are of different devices: /device:TPU:8 before, /device:TPU:9 now
where the time goes in v4:
time: 40.6 us; the launch traced here: 40.4 us
  starting transfers between devices  21.1 us (52%)
  waiting for transfers between devices  12.4 us (31%)
  Pallas kernels  4.76 us (12%)
  between operations  0.8 us (2%)
  other arithmetic  0.69 us (2%)
  local copies, waits for them, and re-layouts  0.65 us (2%)
    ppermute x4, starting transfers between devices, exchange(): outer = lax.ppermute(to_outer, 'tgt', swap_pairs(count, 1))  10.9 us
    ppermute x2, starting transfers between devices, sum_over(): lax.ppermute(value, axis, [(i, i ^ distance) for i in range(count)])  7.72 us
    ppermute x4, waiting for transfers between devices, exchange(): outer = lax.ppermute(to_outer, 'tgt', swap_pairs(count, 1))  6.87 us
    pallas_call x10, Pallas kernels, on_chip(): pl.pallas_call(kernel, out_shape=[pltpu.VMEM(shape, dtype) for shape, dty...  4.76 us
    ppermute x2, waiting for transfers between devices, sum_over(): lax.ppermute(value, axis, [(i, i ^ distance) for i in range(count)])  3.23 us
    ppermute x4, starting transfers between devices, exchange(): inner = lax.ppermute(to_inner, 'tgt', swap_pairs(count, 0))  2.33 us
    ppermute x4, waiting for transfers between devices, exchange(): inner = lax.ppermute(to_inner, 'tgt', swap_pairs(count, 0))  2.33 us
  transfers between devices with their start and end apart: 12, of which 8 were waited for; matrix products, arithmetic and copies ran while one was open for 2% of the time, Pallas kernels for 11%

profile of v4, /device:TPU:9, one launch (start us, length us, event | category | flops | bytes accessed | tf_op | source)
XLA Modules:
  0.0 40.4 jit_solution(12285713965120656653)
XLA Ops:
  0.6 0.1 collective-permute-start
  0.7 4.5 %collective-permute-start.1 = (f32[128,256]{1,0:T(8,128)}, f32[128,256]{1,0:T(8,128)S(1)}, u32[]{:S(2)}, u32[]{:S(2)}) collective-permute-start(f32[128,256]{1,0:T(8,128)} %bitcast.15), channel_id=1, source_target_pairs={{0,0},{4,8},{8,4},{12,12},{1,1},{5,9},{9,5},{13,13},{2,2},{6,10},{... | collective-permute-start | bytes 393224 | tf_op jit(solution)/shard_map/ppermute | solution.py:51
  5.2 1.5 %shard_map.86 = (f32[128,256]{1,0:T(8,128)S(1)}, f32[8,256]{1,0:T(8,128)S(1)}, f32[128,256]{1,0:T(8,128)S(1)}, f32[128,256]{1,0:T(8,128)S(1)}, bf16[4,128,256]{2,1,0:T(8,128)(2,1)S(1)}) custom-call(f32[128,256]{1,0:T(8,128)} %bitcast.16, f32[128,256]{1,0:T(8,128)} %bitcast.12, f32[128,256]{1,0:T(8,128)} %bitcast.13, bf16[4,128,256]{2,1,0:T(8,128)(2,1)} %bitcast.11, ...), custom_call_target="tpu_custom_call" | custom-call | flops 1310720 | bytes 661504 | tf_op jit(solution)/shard_map/pallas_call | solution.py:22
  6.7 0.1 collective-permute-start.4
  6.8 0.1 collective-permute-start.5
  6.9 0.0 collective-permute-done.refs_0_
  6.9 1.4 %collective-permute-done.1.refs_1_ = f32[128,256]{1,0:T(8,128)S(1)} collective-permute-done((f32[128,256]{1,0:T(8,128)}, f32[128,256]{1,0:T(8,128)S(1)}, u32[]{:S(2)}, u32[]{:S(2)}) %collective-permute-start.1) | collective-permute-done | bytes 131104 | tf_op jit(solution)/shard_map/ppermute | solution.py:51
  8.3 0.1 shard_map.87
  8.4 2.1 %collective-permute-start.2 = (f32[136,256]{1,0:T(8,128)S(1)}, f32[136,256]{1,0:T(8,128)S(1)}, u32[]{:S(2)}, u32[]{:S(2)}) collective-permute-start(f32[136,256]{1,0:T(8,128)S(1)} %get-tuple-element.34), channel_id=1, source_target_pairs={{0,4},{4,0},{8,12},{12,8},{1,5},{5,1},{9,13},{13,9},{2,6},{6,2},{1... | collective-permute-start | bytes 417800 | tf_op jit(solution)/shard_map/ppermute | solution.py:52
  10.5 1.9 %collective-permute-start.3 = (f32[128,256]{1,0:T(8,128)S(1)}, f32[128,256]{1,0:T(8,128)S(1)}, u32[]{:S(2)}, u32[]{:S(2)}) collective-permute-start(f32[128,256]{1,0:T(8,128)S(1)} %get-tuple-element.35.refs_0_), channel_id=1, source_target_pairs={{0,0},{4,8},{8,4},{12,12},{1,1},{5,9},{9,5},{13,13},{2,2},{6,10},{... | collective-permute-start | bytes 393224 | tf_op jit(solution)/shard_map/ppermute | solution.py:51
  12.4 0.0 collective-permute-done.4.refs_1_
  12.4 0.0 collective-permute-done.5.refs_2_
  12.4 1.1 %shard_map.88 = (f32[128,256]{1,0:T(8,128)S(1)}, f32[128,256]{1,0:T(8,128)S(1)}, f32[128,256]{1,0:T(8,128)S(1)}, f32[128,256]{1,0:T(8,128)S(1)}, f32[128,256]{1,0:T(8,128)S(1)}, /*index=5*/f32[128,256]{1,0:T(8,128)S(1)}) custom-call(s32[1]{0:T(128)} %bitcast.here_ref, f32[8,256]{1,0:T(8,128)S(1)} %get-tuple-element.33.refs_4_.refs_0_, ...), custom_call_target="tpu_custom_call" | custom-call | flops 3623878656 | bytes 24580 | tf_op jit(solution)/shard_map/pallas_call | solution.py:22
  13.6 0.0 collective-permute-done.2.refs_0_
  13.6 0.5 %shard_map.89 = (f32[128,256]{1,0:T(8,128)S(1)}, f32[128,256]{1,0:T(8,128)S(1)}, f32[128,256]{1,0:T(8,128)S(1)}, f32[128,256]{1,0:T(8,128)S(1)}, f32[128,256]{1,0:T(8,128)S(1)}, /*index=5*/f32[128,256]{1,0:T(8,128)S(1)}) custom-call(s32[1]{0:T(128)} %bitcast.here_ref, f32[136,256]{1,0:T(8,128)S(1)} %collective-permute-done.2.refs_0_, ...), custom_call_target="tpu_custom_call" | custom-call | flops 1207959552 | bytes 925700 | tf_op jit(solution)/shard_map/pallas_call | solution.py:22
  14.1 0.4 shard_map.90
  14.5 1.7 %collective-permute-done.3.refs_1_ = f32[128,256]{1,0:T(8,128)S(1)} collective-permute-done((f32[128,256]{1,0:T(8,128)S(1)}, f32[128,256]{1,0:T(8,128)S(1)}, u32[]{:S(2)}, u32[]{:S(2)}) %collective-permute-start.3) | collective-permute-done | bytes 131104 | tf_op jit(solution)/shard_map/ppermute | solution.py:51
  16.2 0.1 shard_map.91.refs_0_.refs_1_
  16.3 0.1 collective-permute-start.6
  16.4 2.1 %collective-permute-start.7 = (f32[128,256]{1,0:T(8,128)S(1)}, f32[128,256]{1,0:T(8,128)S(1)}, u32[]{:S(2)}, u32[]{:S(2)}) collective-permute-start(f32[128,256]{1,0:T(8,128)S(1)} %shard_map.91.refs_0_.refs_1_), channel_id=1, source_target_pairs={{0,0},{4,8},{8,4},{12,12},{1,1},{5,9},{9,5},{13,13},{2,2},{6,10},{... | collective-permute-start | bytes 393224 | tf_op jit(solution)/shard_map/ppermute | solution.py:51
  18.5 0.4 shard_map.92
  18.9 1.3 %collective-permute-done.6.refs_0_ = f32[128,256]{1,0:T(8,128)S(1)} collective-permute-done((f32[128,256]{1,0:T(8,128)S(1)}, f32[128,256]{1,0:T(8,128)S(1)}, u32[]{:S(2)}, u32[]{:S(2)}) %collective-permute-start.6) | collective-permute-done | bytes 131104 | tf_op jit(solution)/shard_map/ppermute | solution.py:52
  20.2 1.9 %collective-permute-done.7.refs_1_ = f32[128,256]{1,0:T(8,128)S(1)} collective-permute-done((f32[128,256]{1,0:T(8,128)S(1)}, f32[128,256]{1,0:T(8,128)S(1)}, u32[]{:S(2)}, u32[]{:S(2)}) %collective-permute-start.7) | collective-permute-done | bytes 131104 | tf_op jit(solution)/shard_map/ppermute | solution.py:51
  22.1 0.1 shard_map.93.refs_0_
  22.2 0.1 collective-permute-start.8
  22.3 2.4 %collective-permute-start.9 = (f32[128,256]{1,0:T(8,128)S(1)}, f32[128,256]{1,0:T(8,128)S(1)}, u32[]{:S(2)}, u32[]{:S(2)}) collective-permute-start(f32[128,256]{1,0:T(8,128)S(1)} %shard_map.93.refs_0_), channel_id=1, source_target_pairs={{0,0},{4,8},{8,4},{12,12},{1,1},{5,9},{9,5},{13,13},{2,2},{6,10},{... | collective-permute-start | bytes 393224 | tf_op jit(solution)/shard_map/ppermute | solution.py:51
  24.7 0.4 shard_map.94
  25.1 1.0 %collective-permute-done.8.refs_0_ = f32[128,256]{1,0:T(8,128)S(1)} collective-permute-done((f32[128,256]{1,0:T(8,128)S(1)}, f32[128,256]{1,0:T(8,128)S(1)}, u32[]{:S(2)}, u32[]{:S(2)}) %collective-permute-start.8) | collective-permute-done | bytes 131104 | tf_op jit(solution)/shard_map/ppermute | solution.py:52
  26.1 1.9 %collective-permute-done.9.refs_1_ = f32[128,256]{1,0:T(8,128)S(1)} collective-permute-done((f32[128,256]{1,0:T(8,128)S(1)}, f32[128,256]{1,0:T(8,128)S(1)}, u32[]{:S(2)}, u32[]{:S(2)}) %collective-permute-start.9) | collective-permute-done | bytes 131104 | tf_op jit(solution)/shard_map/ppermute | solution.py:51
  28.0 0.1 shard_map.95
  28.1 1.3 %collective-permute-start.10 = (f32[128,256]{1,0:T(8,128)S(1)}, f32[128,256]{1,0:T(8,128)S(1)}, u32[]{:S(2)}, u32[]{:S(2)}) collective-permute-start(f32[128,256]{1,0:T(8,128)S(1)} %get-tuple-element.59), channel_id=1, source_target_pairs={{0,2},{1,3},{2,0},{3,1},{4,6},{5,7},{6,4},{7,5},{8,10},{9,11},{10,... | collective-permute-start | bytes 393224 | tf_op jit(solution)/shard_map/ppermute | solution.py:266
  29.4 2.9 %collective-permute-done.10 = f32[128,256]{1,0:T(8,128)S(1)} collective-permute-done((f32[128,256]{1,0:T(8,128)S(1)}, f32[128,256]{1,0:T(8,128)S(1)}, u32[]{:S(2)}, u32[]{:S(2)}) %collective-permute-start.10) | collective-permute-done | bytes 131104 | tf_op jit(solution)/shard_map/ppermute | solution.py:266
  32.3 6.4 %collective-permute-start.11 = (f32[128,256]{1,0:T(8,128)S(1)}, f32[128,256]{1,0:T(8,128)S(1)}, u32[]{:S(2)}, u32[]{:S(2)}) collective-permute-start(f32[128,256]{1,0:T(8,128)S(1)} %add.6), channel_id=1, source_target_pairs={{0,1},{1,0},{2,3},{3,2},{4,5},{5,4},{6,7},{7,6},{8,9},{9,8},{10,11... | collective-permute-start | bytes 393224 | tf_op jit(solution)/shard_map/ppermute | solution.py:266
  38.7 0.7 %copy.9 = f32[1,4,32,256]{3,2,1,0:T(8,128)} copy(f32[1,4,32,256]{3,2,1,0:T(8,128)S(1)} %bitcast.10) | data formatting | bytes 262144
  39.4 0.3 collective-permute-done.11
  39.7 0.7 %add.7 = f32[128,256]{1,0:T(8,128)} add(f32[128,256]{1,0:T(8,128)S(1)} %add.6, f32[128,256]{1,0:T(8,128)S(1)} %collective-permute-done.11) | non-fusion elementwise | flops 32768 | bytes 393216 | tf_op jit(solution)/shard_map/add | solution.py:266
  (1 shorter events, 0.0 us)
Async XLA Ops:
  0.6 6.3 %collective-permute-start = (f32[128,256]{1,0:T(8,128)}, f32[128,256]{1,0:T(8,128)S(1)}, u32[]{:S(2)}, u32[]{:S(2)}) collective-permute-start(f32[128,256]{1,0:T(8,128)} %bitcast.14), channel_id=1, source_target_pairs={{0,4},{4,0},{8,12},{12,8},{1,5},{5,1},{9,13},{13,9},{2,6},{6,2},{1... | collective-permute-start | bytes 393224 | tf_op jit(solution)/shard_map/ppermute | solution.py:52
  0.7 7.6 %collective-permute-start.1 = (f32[128,256]{1,0:T(8,128)}, f32[128,256]{1,0:T(8,128)S(1)}, u32[]{:S(2)}, u32[]{:S(2)}) collective-permute-start(f32[128,256]{1,0:T(8,128)} %bitcast.15), channel_id=1, source_target_pairs={{0,0},{4,8},{8,4},{12,12},{1,1},{5,9},{9,5},{13,13},{2,2},{6,10},{... | collective-permute-start | bytes 393224 | tf_op jit(solution)/shard_map/ppermute | solution.py:51
  6.7 5.7 %collective-permute-start.4 = (f32[8,256]{1,0:T(8,128)S(1)}, f32[8,256]{1,0:T(8,128)S(1)}, u32[]{:S(2)}, u32[]{:S(2)}) collective-permute-start(f32[8,256]{1,0:T(8,128)S(1)} %get-tuple-element.33.refs_4_.refs_0_), channel_id=1, source_target_pairs={{0,8},{4,12},{8,0},{12,4},{1,9},{5,13},{9,1},{13,5},{2,10},{6,14},... | collective-permute-start | bytes 24584 | tf_op jit(solution)/shard_map/ppermute | solution.py:315
  6.8 5.6 %collective-permute-start.5 = (f32[8,256]{1,0:T(8,128)S(1)}, f32[8,256]{1,0:T(8,128)S(1)}, u32[]{:S(2)}, u32[]{:S(2)}) collective-permute-start(f32[8,256]{1,0:T(8,128)S(1)} %get-tuple-element.33.refs_4_.refs_0_), channel_id=1, source_target_pairs={{0,12},{4,8},{8,4},{12,0},{1,13},{5,9},{9,5},{13,1},{2,14},{6,10},... | collective-permute-start | bytes 24584 | tf_op jit(solution)/shard_map/ppermute | solution.py:315
  8.4 5.2 %collective-permute-start.2 = (f32[136,256]{1,0:T(8,128)S(1)}, f32[136,256]{1,0:T(8,128)S(1)}, u32[]{:S(2)}, u32[]{:S(2)}) collective-permute-start(f32[136,256]{1,0:T(8,128)S(1)} %get-tuple-element.34), channel_id=1, source_target_pairs={{0,4},{4,0},{8,12},{12,8},{1,5},{5,1},{9,13},{13,9},{2,6},{6,2},{1... | collective-permute-start | bytes 417800 | tf_op jit(solution)/shard_map/ppermute | solution.py:52
  10.5 5.7 %collective-permute-start.3 = (f32[128,256]{1,0:T(8,128)S(1)}, f32[128,256]{1,0:T(8,128)S(1)}, u32[]{:S(2)}, u32[]{:S(2)}) collective-permute-start(f32[128,256]{1,0:T(8,128)S(1)} %get-tuple-element.35.refs_0_), channel_id=1, source_target_pairs={{0,0},{4,8},{8,4},{12,12},{1,1},{5,9},{9,5},{13,13},{2,2},{6,10},{... | collective-permute-start | bytes 393224 | tf_op jit(solution)/shard_map/ppermute | solution.py:51
  16.3 3.9 %collective-permute-start.6 = (f32[128,256]{1,0:T(8,128)S(1)}, f32[128,256]{1,0:T(8,128)S(1)}, u32[]{:S(2)}, u32[]{:S(2)}) collective-permute-start(f32[128,256]{1,0:T(8,128)S(1)} %shard_map.91.refs_0_.refs_1_), channel_id=1, source_target_pairs={{0,4},{4,0},{8,12},{12,8},{1,5},{5,1},{9,13},{13,9},{2,6},{6,2},{1... | collective-permute-start | bytes 393224 | tf_op jit(solution)/shard_map/ppermute | solution.py:52
  16.4 5.7 %collective-permute-start.7 = (f32[128,256]{1,0:T(8,128)S(1)}, f32[128,256]{1,0:T(8,128)S(1)}, u32[]{:S(2)}, u32[]{:S(2)}) collective-permute-start(f32[128,256]{1,0:T(8,128)S(1)} %shard_map.91.refs_0_.refs_1_), channel_id=1, source_target_pairs={{0,0},{4,8},{8,4},{12,12},{1,1},{5,9},{9,5},{13,13},{2,2},{6,10},{... | collective-permute-start | bytes 393224 | tf_op jit(solution)/shard_map/ppermute | solution.py:51
  22.2 3.9 %collective-permute-start.8 = (f32[128,256]{1,0:T(8,128)S(1)}, f32[128,256]{1,0:T(8,128)S(1)}, u32[]{:S(2)}, u32[]{:S(2)}) collective-permute-start(f32[128,256]{1,0:T(8,128)S(1)} %shard_map.93.refs_0_), channel_id=1, source_target_pairs={{0,4},{4,0},{8,12},{12,8},{1,5},{5,1},{9,13},{13,9},{2,6},{6,2},{1... | collective-permute-start | bytes 393224 | tf_op jit(solution)/shard_map/ppermute | solution.py:52
  22.3 5.7 %collective-permute-start.9 = (f32[128,256]{1,0:T(8,128)S(1)}, f32[128,256]{1,0:T(8,128)S(1)}, u32[]{:S(2)}, u32[]{:S(2)}) collective-permute-start(f32[128,256]{1,0:T(8,128)S(1)} %shard_map.93.refs_0_), channel_id=1, source_target_pairs={{0,0},{4,8},{8,4},{12,12},{1,1},{5,9},{9,5},{13,13},{2,2},{6,10},{... | collective-permute-start | bytes 393224 | tf_op jit(solution)/shard_map/ppermute | solution.py:51
  28.1 4.2 %collective-permute-start.10 = (f32[128,256]{1,0:T(8,128)S(1)}, f32[128,256]{1,0:T(8,128)S(1)}, u32[]{:S(2)}, u32[]{:S(2)}) collective-permute-start(f32[128,256]{1,0:T(8,128)S(1)} %get-tuple-element.59), channel_id=1, source_target_pairs={{0,2},{1,3},{2,0},{3,1},{4,6},{5,7},{6,4},{7,5},{8,10},{9,11},{10,... | collective-permute-start | bytes 393224 | tf_op jit(solution)/shard_map/ppermute | solution.py:266
  32.3 7.4 %collective-permute-start.11 = (f32[128,256]{1,0:T(8,128)S(1)}, f32[128,256]{1,0:T(8,128)S(1)}, u32[]{:S(2)}, u32[]{:S(2)}) collective-permute-start(f32[128,256]{1,0:T(8,128)S(1)} %add.6), channel_id=1, source_target_pairs={{0,1},{1,0},{2,3},{3,2},{4,5},{5,4},{6,7},{7,6},{8,9},{9,8},{10,11... | collective-permute-start | bytes 393224 | tf_op jit(solution)/shard_map/ppermute | solution.py:266

commit v5 on v4

--- a/solution.py
+++ b/solution.py
@@ -39,17 +39,21 @@
     return list(results)
 
 
-def swap_pairs(count, first):
-    partner = list(range(count))
-    for left in range(first, count - 1, 2):
-        partner[left], partner[left + 1] = left + 1, left
-    return list(enumerate(partner))
+def swap_pairs(count, shots, first):
+    routes = []
+    for slab in range(count):
+        paired = slab >= first and (slab - first) // 2 * 2 + first + 1 < count
+        partner = slab + 1 - 2 * ((slab - first) % 2) if paired else slab
+        for shot in range(shots):
+            other = shot if paired or shots % 2 else shot ^ 1
+            routes.append((slab * shots + shot, partner * shots + other))
+    return routes
 
 
 def exchange(to_inner, to_outer):
-    count = lax.axis_size("tgt")
-    outer = lax.ppermute(to_outer, "tgt", swap_pairs(count, 1))
-    inner = lax.ppermute(to_inner, "tgt", swap_pairs(count, 0))
+    count, shots = lax.axis_size("tgt"), lax.axis_size("shot")
+    outer = lax.ppermute(to_outer, ("tgt", "shot"), swap_pairs(count, shots, 1))
+    inner = lax.ppermute(to_inner, ("tgt", "shot"), swap_pairs(count, shots, 0))
     return inner, outer
 
 

time: 40.6 us -> 34.7 us (0.85)
  the two profiles are of different devices: /device:TPU:9 before, /device:TPU:0 now
where the time goes in v5:
time: 34.7 us; the launch traced here: 34.5 us
  waiting for transfers between devices  14.1 us (41%)
  starting transfers between devices  13.6 us (39%)
  Pallas kernels  4.73 us (14%)
  between operations  0.74 us (2%)
  other arithmetic  0.69 us (2%)
  local copies, waits for them, and re-layouts  0.66 us (2%)
    ppermute x4, waiting for transfers between devices, exchange(): inner = lax.ppermute(to_inner, ('tgt', 'shot'), swap_pairs(count, shots, 0))  7.56 us
    ppermute x4, starting transfers between devices, exchange(): inner = lax.ppermute(to_inner, ('tgt', 'shot'), swap_pairs(count, shots, 0))  6.31 us
    ppermute x2, starting transfers between devices, on_device(): lax.ppermute(table, 'tgt', [(i, i ^ far) for i in range(slabs)])  5.58 us
    pallas_call x10, Pallas kernels, on_chip(): pl.pallas_call(kernel, out_shape=[pltpu.VMEM(shape, dtype) for shape, dty...  4.73 us
    ppermute x2, waiting for transfers between devices, sum_over(): lax.ppermute(value, axis, [(i, i ^ distance) for i in range(count)])  4.14 us
    ppermute x2, waiting for transfers between devices, on_device(): lax.ppermute(table, 'tgt', [(i, i ^ far) for i in range(slabs)])  2.37 us
    ppermute x2, starting transfers between devices, sum_over(): lax.ppermute(value, axis, [(i, i ^ distance) for i in range(count)])  1.64 us
  transfers between devices with their start and end apart: 12, of which 6 were waited for; matrix products, arithmetic and copies ran while one was open for 2% of the time, Pallas kernels for 13%

profile of v5, /device:TPU:0, one launch (start us, length us, event | category | flops | bytes accessed | tf_op | source)
XLA Modules:
  0.0 34.5 jit_solution(18314057742308610258)
XLA Ops:
  0.6 3.1 %collective-permute-start = (f32[128,256]{1,0:T(8,128)}, f32[128,256]{1,0:T(8,128)S(1)}, u32[]{:S(2)}, u32[]{:S(2)}) collective-permute-start(f32[128,256]{1,0:T(8,128)} %bitcast.14), channel_id=1, source_target_pairs={{0,4},{1,5},{2,6},{3,7},{4,0},{5,1},{6,2},{7,3},{8,12},{9,13},{10,... | collective-permute-start | bytes 393224 | tf_op jit(solution)/shard_map/ppermute | solution.py:56
  3.7 0.0 collective-permute-start.1
  3.7 1.5 %shard_map.86 = (f32[128,256]{1,0:T(8,128)S(1)}, f32[8,256]{1,0:T(8,128)S(1)}, f32[128,256]{1,0:T(8,128)S(1)}, f32[128,256]{1,0:T(8,128)S(1)}, bf16[4,128,256]{2,1,0:T(8,128)(2,1)S(1)}) custom-call(f32[128,256]{1,0:T(8,128)} %bitcast.16, f32[128,256]{1,0:T(8,128)} %bitcast.12, f32[128,256]{1,0:T(8,128)} %bitcast.13, bf16[4,128,256]{2,1,0:T(8,128)(2,1)} %bitcast.11, ...), custom_call_target="tpu_custom_call" | custom-call | flops 1310720 | bytes 661504 | tf_op jit(solution)/shard_map/pallas_call | solution.py:22
  5.3 2.7 %collective-permute-start.4 = (f32[8,256]{1,0:T(8,128)S(1)}, f32[8,256]{1,0:T(8,128)S(1)}, u32[]{:S(2)}, u32[]{:S(2)}) collective-permute-start(f32[8,256]{1,0:T(8,128)S(1)} %get-tuple-element.33.refs_4_.refs_0_), channel_id=1, source_target_pairs={{0,8},{4,12},{8,0},{12,4},{1,9},{5,13},{9,1},{13,5},{2,10},{6,14},... | collective-permute-start | bytes 24584 | tf_op jit(solution)/shard_map/ppermute | solution.py:319
  7.9 2.9 %collective-permute-start.5 = (f32[8,256]{1,0:T(8,128)S(1)}, f32[8,256]{1,0:T(8,128)S(1)}, u32[]{:S(2)}, u32[]{:S(2)}) collective-permute-start(f32[8,256]{1,0:T(8,128)S(1)} %get-tuple-element.33.refs_4_.refs_0_), channel_id=1, source_target_pairs={{0,12},{4,8},{8,4},{12,0},{1,13},{5,9},{9,5},{13,1},{2,14},{6,10},... | collective-permute-start | bytes 24584 | tf_op jit(solution)/shard_map/ppermute | solution.py:319
  10.8 0.0 collective-permute-done.refs_0_
  10.8 0.0 collective-permute-done.1.refs_1_
  10.8 0.1 shard_map.87
  10.9 0.1 collective-permute-start.2
  11.0 0.1 collective-permute-start.3
  11.1 0.0 collective-permute-done.4.refs_1_
  11.1 2.4 %collective-permute-done.5.refs_2_ = f32[8,256]{1,0:T(8,128)S(1)} collective-permute-done((f32[8,256]{1,0:T(8,128)S(1)}, f32[8,256]{1,0:T(8,128)S(1)}, u32[]{:S(2)}, u32[]{:S(2)}) %collective-permute-start.5) | collective-permute-done | bytes 8224 | tf_op jit(solution)/shard_map/ppermute | solution.py:319
  13.5 1.1 %shard_map.88 = (f32[128,256]{1,0:T(8,128)S(1)}, f32[128,256]{1,0:T(8,128)S(1)}, f32[128,256]{1,0:T(8,128)S(1)}, f32[128,256]{1,0:T(8,128)S(1)}, f32[128,256]{1,0:T(8,128)S(1)}, /*index=5*/f32[128,256]{1,0:T(8,128)S(1)}) custom-call(s32[1]{0:T(128)} %bitcast.here_ref, f32[8,256]{1,0:T(8,128)S(1)} %get-tuple-element.33.refs_4_.refs_0_, ...), custom_call_target="tpu_custom_call" | custom-call | flops 3623878656 | bytes 24580 | tf_op jit(solution)/shard_map/pallas_call | solution.py:22
  14.6 1.4 %collective-permute-done.2.refs_0_ = f32[136,256]{1,0:T(8,128)S(1)} collective-permute-done((f32[136,256]{1,0:T(8,128)S(1)}, f32[136,256]{1,0:T(8,128)S(1)}, u32[]{:S(2)}, u32[]{:S(2)}) %collective-permute-start.2) | collective-permute-done | bytes 139296 | tf_op jit(solution)/shard_map/ppermute | solution.py:56
  16.1 0.5 %shard_map.89 = (f32[128,256]{1,0:T(8,128)S(1)}, f32[128,256]{1,0:T(8,128)S(1)}, f32[128,256]{1,0:T(8,128)S(1)}, f32[128,256]{1,0:T(8,128)S(1)}, f32[128,256]{1,0:T(8,128)S(1)}, /*index=5*/f32[128,256]{1,0:T(8,128)S(1)}) custom-call(s32[1]{0:T(128)} %bitcast.here_ref, f32[136,256]{1,0:T(8,128)S(1)} %collective-permute-done.2.refs_0_, ...), custom_call_target="tpu_custom_call" | custom-call | flops 1207959552 | bytes 925700 | tf_op jit(solution)/shard_map/pallas_call | solution.py:22
  16.6 0.4 %shard_map.90 = (f32[128,256]{1,0:T(8,128)S(1)}, f32[128,256]{1,0:T(8,128)S(1)}, f32[128,256]{1,0:T(8,128)S(1)}) custom-call(f32[128,256]{1,0:T(8,128)S(1)} %get-tuple-element.35.refs_0_, f32[128,256]{1,0:T(8,128)S(1)} %get-tuple-element.36.refs_1_, f32[128,256]{1,0:T(8,128)S(1)} %get-tuple-element.32.refs_3_.refs_2_, ...), custom_call_target="tpu_custom_call" | custom-call | flops 1310720 | bytes 917504 | tf_op jit(solution)/shard_map/pallas_call | solution.py:22
  17.0 0.0 collective-permute-done.3.refs_1_
  17.0 0.1 shard_map.91.refs_0_.refs_1_
  17.1 1.1 %collective-permute-start.6 = (f32[128,256]{1,0:T(8,128)S(1)}, f32[128,256]{1,0:T(8,128)S(1)}, u32[]{:S(2)}, u32[]{:S(2)}) collective-permute-start(f32[128,256]{1,0:T(8,128)S(1)} %shard_map.91.refs_0_.refs_1_), channel_id=1, source_target_pairs={{0,4},{1,5},{2,6},{3,7},{4,0},{5,1},{6,2},{7,3},{8,12},{9,13},{10,... | collective-permute-start | bytes 393224 | tf_op jit(solution)/shard_map/ppermute | solution.py:56
  18.2 0.0 collective-permute-start.7
  18.2 0.4 %shard_map.92 = (f32[128,256]{1,0:T(8,128)S(1)}, f32[128,256]{1,0:T(8,128)S(1)}) custom-call(f32[128,256]{1,0:T(8,128)S(1)} %shard_map.91.refs_0_.refs_1_, f32[128,256]{1,0:T(8,128)S(1)} %get-tuple-element.49.refs_1_, f32[128,256]{1,0:T(8,128)S(1)} %get-tuple-element.32.refs_3_.refs_2_, bf16[4,128,256]{2,1,0:T(8,128)(2,1)S(1)} %get-tuple-element.37.refs_3_, ...), custom_call_target="tpu_custom_call" | custom-call | flops 1310720 | bytes 917504 | tf_op jit(solution)/shard_map/pallas_call | solution.py:22
  18.6 3.6 %collective-permute-done.6.refs_0_ = f32[128,256]{1,0:T(8,128)S(1)} collective-permute-done((f32[128,256]{1,0:T(8,128)S(1)}, f32[128,256]{1,0:T(8,128)S(1)}, u32[]{:S(2)}, u32[]{:S(2)}) %collective-permute-start.6) | collective-permute-done | bytes 131104 | tf_op jit(solution)/shard_map/ppermute | solution.py:56
  22.1 0.0 collective-permute-done.7.refs_1_
  22.1 0.1 shard_map.93.refs_0_
  22.2 2.1 %collective-permute-start.8 = (f32[128,256]{1,0:T(8,128)S(1)}, f32[128,256]{1,0:T(8,128)S(1)}, u32[]{:S(2)}, u32[]{:S(2)}) collective-permute-start(f32[128,256]{1,0:T(8,128)S(1)} %shard_map.93.refs_0_), channel_id=1, source_target_pairs={{0,4},{1,5},{2,6},{3,7},{4,0},{5,1},{6,2},{7,3},{8,12},{9,13},{10,... | collective-permute-start | bytes 393224 | tf_op jit(solution)/shard_map/ppermute | solution.py:56
  24.3 0.0 collective-permute-start.9
  24.3 0.4 %shard_map.94 = (f32[128,256]{1,0:T(8,128)S(1)}, f32[128,256]{1,0:T(8,128)S(1)}, f32[128,256]{1,0:T(8,128)S(1)}) custom-call(f32[128,256]{1,0:T(8,128)S(1)} %shard_map.93.refs_0_, f32[128,256]{1,0:T(8,128)S(1)} %shard_map.91.refs_0_.refs_1_, f32[128,256]{1,0:T(8,128)S(1)} %get-tuple-element.32.refs_3_.refs_2_, ...), custom_call_target="tpu_custom_call" | custom-call | flops 1310720 | bytes 917504 | tf_op jit(solution)/shard_map/pallas_call | solution.py:22
  24.7 2.5 %collective-permute-done.8.refs_0_ = f32[128,256]{1,0:T(8,128)S(1)} collective-permute-done((f32[128,256]{1,0:T(8,128)S(1)}, f32[128,256]{1,0:T(8,128)S(1)}, u32[]{:S(2)}, u32[]{:S(2)}) %collective-permute-start.8) | collective-permute-done | bytes 131104 | tf_op jit(solution)/shard_map/ppermute | solution.py:56
  27.3 0.0 collective-permute-done.9.refs_1_
  27.3 0.1 shard_map.95
  27.4 1.6 %collective-permute-start.10 = (f32[128,256]{1,0:T(8,128)S(1)}, f32[128,256]{1,0:T(8,128)S(1)}, u32[]{:S(2)}, u32[]{:S(2)}) collective-permute-start(f32[128,256]{1,0:T(8,128)S(1)} %get-tuple-element.59), channel_id=1, source_target_pairs={{0,2},{1,3},{2,0},{3,1},{4,6},{5,7},{6,4},{7,5},{8,10},{9,11},{10,... | collective-permute-start | bytes 393224 | tf_op jit(solution)/shard_map/ppermute | solution.py:270
  28.9 3.5 %collective-permute-done.10 = f32[128,256]{1,0:T(8,128)S(1)} collective-permute-done((f32[128,256]{1,0:T(8,128)S(1)}, f32[128,256]{1,0:T(8,128)S(1)}, u32[]{:S(2)}, u32[]{:S(2)}) %collective-permute-start.10) | collective-permute-done | bytes 131104 | tf_op jit(solution)/shard_map/ppermute | solution.py:270
  32.4 0.1 collective-permute-start.11
  32.5 0.7 %copy.9 = f32[1,4,32,256]{3,2,1,0:T(8,128)} copy(f32[1,4,32,256]{3,2,1,0:T(8,128)S(1)} %bitcast.10) | data formatting | bytes 262144
  33.2 0.7 %collective-permute-done.11 = f32[128,256]{1,0:T(8,128)S(1)} collective-permute-done((f32[128,256]{1,0:T(8,128)S(1)}, f32[128,256]{1,0:T(8,128)S(1)}, u32[]{:S(2)}, u32[]{:S(2)}) %collective-permute-start.11) | collective-permute-done | bytes 131104 | tf_op jit(solution)/shard_map/ppermute | solution.py:270
  33.8 0.7 %add.7 = f32[128,256]{1,0:T(8,128)} add(f32[128,256]{1,0:T(8,128)S(1)} %add.6, f32[128,256]{1,0:T(8,128)S(1)} %collective-permute-done.11) | non-fusion elementwise | flops 32768 | bytes 393216 | tf_op jit(solution)/shard_map/add | solution.py:270
  (1 shorter events, 0.0 us)
Async XLA Ops:
  0.6 10.2 %collective-permute-start = (f32[128,256]{1,0:T(8,128)}, f32[128,256]{1,0:T(8,128)S(1)}, u32[]{:S(2)}, u32[]{:S(2)}) collective-permute-start(f32[128,256]{1,0:T(8,128)} %bitcast.14), channel_id=1, source_target_pairs={{0,4},{1,5},{2,6},{3,7},{4,0},{5,1},{6,2},{7,3},{8,12},{9,13},{10,... | collective-permute-start | bytes 393224 | tf_op jit(solution)/shard_map/ppermute | solution.py:56
  3.7 7.1 %collective-permute-start.1 = (f32[128,256]{1,0:T(8,128)}, f32[128,256]{1,0:T(8,128)S(1)}, u32[]{:S(2)}, u32[]{:S(2)}) collective-permute-start(f32[128,256]{1,0:T(8,128)} %bitcast.15), channel_id=1, source_target_pairs={{0,1},{1,0},{2,3},{3,2},{4,8},{5,9},{6,10},{7,11},{8,4},{9,5},{10,... | collective-permute-start | bytes 393224 | tf_op jit(solution)/shard_map/ppermute | solution.py:55
  5.3 5.8 %collective-permute-start.4 = (f32[8,256]{1,0:T(8,128)S(1)}, f32[8,256]{1,0:T(8,128)S(1)}, u32[]{:S(2)}, u32[]{:S(2)}) collective-permute-start(f32[8,256]{1,0:T(8,128)S(1)} %get-tuple-element.33.refs_4_.refs_0_), channel_id=1, source_target_pairs={{0,8},{4,12},{8,0},{12,4},{1,9},{5,13},{9,1},{13,5},{2,10},{6,14},... | collective-permute-start | bytes 24584 | tf_op jit(solution)/shard_map/ppermute | solution.py:319
  7.9 5.6 %collective-permute-start.5 = (f32[8,256]{1,0:T(8,128)S(1)}, f32[8,256]{1,0:T(8,128)S(1)}, u32[]{:S(2)}, u32[]{:S(2)}) collective-permute-start(f32[8,256]{1,0:T(8,128)S(1)} %get-tuple-element.33.refs_4_.refs_0_), channel_id=1, source_target_pairs={{0,12},{4,8},{8,4},{12,0},{1,13},{5,9},{9,5},{13,1},{2,14},{6,10},... | collective-permute-start | bytes 24584 | tf_op jit(solution)/shard_map/ppermute | solution.py:319
  10.9 5.1 %collective-permute-start.2 = (f32[136,256]{1,0:T(8,128)S(1)}, f32[136,256]{1,0:T(8,128)S(1)}, u32[]{:S(2)}, u32[]{:S(2)}) collective-permute-start(f32[136,256]{1,0:T(8,128)S(1)} %get-tuple-element.34), channel_id=1, source_target_pairs={{0,4},{1,5},{2,6},{3,7},{4,0},{5,1},{6,2},{7,3},{8,12},{9,13},{10,... | collective-permute-start | bytes 417800 | tf_op jit(solution)/shard_map/ppermute | solution.py:56
  11.0 6.0 %collective-permute-start.3 = (f32[128,256]{1,0:T(8,128)S(1)}, f32[128,256]{1,0:T(8,128)S(1)}, u32[]{:S(2)}, u32[]{:S(2)}) collective-permute-start(f32[128,256]{1,0:T(8,128)S(1)} %get-tuple-element.35.refs_0_), channel_id=1, source_target_pairs={{0,1},{1,0},{2,3},{3,2},{4,8},{5,9},{6,10},{7,11},{8,4},{9,5},{10,... | collective-permute-start | bytes 393224 | tf_op jit(solution)/shard_map/ppermute | solution.py:55
  17.1 5.0 %collective-permute-start.6 = (f32[128,256]{1,0:T(8,128)S(1)}, f32[128,256]{1,0:T(8,128)S(1)}, u32[]{:S(2)}, u32[]{:S(2)}) collective-permute-start(f32[128,256]{1,0:T(8,128)S(1)} %shard_map.91.refs_0_.refs_1_), channel_id=1, source_target_pairs={{0,4},{1,5},{2,6},{3,7},{4,0},{5,1},{6,2},{7,3},{8,12},{9,13},{10,... | collective-permute-start | bytes 393224 | tf_op jit(solution)/shard_map/ppermute | solution.py:56
  18.2 4.0 %collective-permute-start.7 = (f32[128,256]{1,0:T(8,128)S(1)}, f32[128,256]{1,0:T(8,128)S(1)}, u32[]{:S(2)}, u32[]{:S(2)}) collective-permute-start(f32[128,256]{1,0:T(8,128)S(1)} %shard_map.91.refs_0_.refs_1_), channel_id=1, source_target_pairs={{0,1},{1,0},{2,3},{3,2},{4,8},{5,9},{6,10},{7,11},{8,4},{9,5},{10,... | collective-permute-start | bytes 393224 | tf_op jit(solution)/shard_map/ppermute | solution.py:55
  22.2 5.0 %collective-permute-start.8 = (f32[128,256]{1,0:T(8,128)S(1)}, f32[128,256]{1,0:T(8,128)S(1)}, u32[]{:S(2)}, u32[]{:S(2)}) collective-permute-start(f32[128,256]{1,0:T(8,128)S(1)} %shard_map.93.refs_0_), channel_id=1, source_target_pairs={{0,4},{1,5},{2,6},{3,7},{4,0},{5,1},{6,2},{7,3},{8,12},{9,13},{10,... | collective-permute-start | bytes 393224 | tf_op jit(solution)/shard_map/ppermute | solution.py:56
  24.3 3.0 %collective-permute-start.9 = (f32[128,256]{1,0:T(8,128)S(1)}, f32[128,256]{1,0:T(8,128)S(1)}, u32[]{:S(2)}, u32[]{:S(2)}) collective-permute-start(f32[128,256]{1,0:T(8,128)S(1)} %shard_map.93.refs_0_), channel_id=1, source_target_pairs={{0,1},{1,0},{2,3},{3,2},{4,8},{5,9},{6,10},{7,11},{8,4},{9,5},{10,... | collective-permute-start | bytes 393224 | tf_op jit(solution)/shard_map/ppermute | solution.py:55
  27.4 5.0 %collective-permute-start.10 = (f32[128,256]{1,0:T(8,128)S(1)}, f32[128,256]{1,0:T(8,128)S(1)}, u32[]{:S(2)}, u32[]{:S(2)}) collective-permute-start(f32[128,256]{1,0:T(8,128)S(1)} %get-tuple-element.59), channel_id=1, source_target_pairs={{0,2},{1,3},{2,0},{3,1},{4,6},{5,7},{6,4},{7,5},{8,10},{9,11},{10,... | collective-permute-start | bytes 393224 | tf_op jit(solution)/shard_map/ppermute | solution.py:270
  32.4 1.4 %collective-permute-start.11 = (f32[128,256]{1,0:T(8,128)S(1)}, f32[128,256]{1,0:T(8,128)S(1)}, u32[]{:S(2)}, u32[]{:S(2)}) collective-permute-start(f32[128,256]{1,0:T(8,128)S(1)} %add.6), channel_id=1, source_target_pairs={{0,1},{1,0},{2,3},{3,2},{4,5},{5,4},{6,7},{7,6},{8,9},{9,8},{10,11... | collective-permute-start | bytes 393224 | tf_op jit(solution)/shard_map/ppermute | solution.py:270

commit v6 on v5

--- a/solution.py
+++ b/solution.py
@@ -154,15 +154,23 @@
     return 2.0 * current[p] - later + courant * courant * total
 
 
-def first_kernel(planes, table_rows, *refs):
-    refs = list(refs)
-    now_hbm, later_hbm, courant_hbm, fwd_hbm, dest_hbm, cell_hbm, vals_hbm = refs[:7]
-    part_ref, table_ref, now_ref, courant_ref, fwd_ref = refs[7:12]
-    later_ref, dest_ref, cell_ref, vals_ref, sems = refs[12:]
+def pack_kernel(dest_hbm, cell_hbm, vals_hbm, table_ref, dest_ref, cell_ref, vals_ref, sems):
+    pairs = [(dest_hbm, dest_ref), (cell_hbm, cell_ref), (vals_hbm, vals_ref)]
+    copies = [pltpu.make_async_copy(a, b, sems.at[i]) for i, (a, b) in enumerate(pairs)]
+    for copy in copies:
+        copy.start()
+    table_ref[...] = jnp.zeros_like(table_ref)
+    for copy in copies:
+        copy.wait()
+    table_ref[0:1] = dest_ref[...].astype(jnp.float32)
+    table_ref[1:2] = cell_ref[...].astype(jnp.float32)
+    table_ref[2 : 2 + vals_ref.shape[0]] = vals_ref[...]
+
+
+def first_kernel(planes, *refs):
+    now_hbm, later_hbm, courant_hbm, fwd_hbm = refs[:4]
+    part_ref, now_ref, courant_ref, fwd_ref, later_ref, sems = refs[4:]
     pairs = [
-        (dest_hbm, dest_ref),
-        (cell_hbm, cell_ref),
-        (vals_hbm, vals_ref),
         (now_hbm, now_ref),
         (later_hbm, later_ref),
         (courant_hbm, courant_ref),
@@ -173,18 +181,12 @@
         copy.start()
     for copy in copies[:3]:
         copy.wait()
-    table_ref[...] = jnp.zeros_like(table_ref)
-    table_ref[0:1] = dest_ref[...].astype(jnp.float32)
-    table_ref[1:2] = cell_ref[...].astype(jnp.float32)
-    table_ref[2 : 2 + vals_ref.shape[0]] = vals_ref[...]
-    for copy in copies[3:6]:
-        copy.wait()
     cells_y = now_ref.shape[0] // planes
     at = [slice(p * cells_y, (p + 1) * cells_y) for p in range(planes)]
     current = [now_ref[s] for s in at]
     for p, s in enumerate(at):
         part_ref[s] = own_part(current, p, later_ref[s], courant_ref[s])
-    copies[6].wait()
+    copies[3].wait()
 
 
 def own_kernel(planes, step, fix_inject, last, *refs):
@@ -267,7 +269,7 @@
         return lax.psum(value, axis)
     distance = count // 2
     while distance:
-        value = value + lax.ppermute(value, axis, [(i, i ^ distance) for i in range(count)])
+        value = value + lax.ppermute(value, axis, [(i, i ^ (2 * distance - 1)) for i in range(count)])
         distance //= 2
     return value
 
@@ -288,31 +290,30 @@
 
     received = exchange(now, now)
     f32 = jnp.float32
-    part, table, current, courant_here, fwd = on_chip(
-        functools.partial(first_kernel, planes, table_rows),
-        [
-            (shape, f32),
-            ((table_rows, entries), f32),
-            (shape, f32),
-            (shape, f32),
-            ((steps, rows, lanes), fwd_acc.dtype),
+    (table,) = on_chip(
+        pack_kernel,
+        [((table_rows, entries), f32)],
+        surf_dest.reshape(1, entries),
+        surf_cell.reshape(1, entries),
+        surf_vals.reshape(steps, entries),
+        scratch=[
+            pltpu.VMEM((1, entries), surf_dest.dtype),
+            pltpu.VMEM((1, entries), surf_cell.dtype),
+            pltpu.VMEM((steps, entries), f32),
+            pltpu.SemaphoreType.DMA((3,)),
         ],
+        in_hbm=range(3),
+    )
+    part, current, courant_here, fwd = on_chip(
+        functools.partial(first_kernel, planes),
+        [(shape, f32), (shape, f32), (shape, f32), ((steps, rows, lanes), fwd_acc.dtype)],
         now,
         adjoint_later.reshape(shape),
         courant.reshape(shape),
         fwd_acc.reshape(steps, rows, lanes),
-        surf_dest.reshape(1, entries),
-        surf_cell.reshape(1, entries),
-        surf_vals.reshape(steps, entries),
         flops=40 * rows * lanes,
-        scratch=[
-            pltpu.VMEM(shape, f32),
-            pltpu.VMEM((1, entries), surf_dest.dtype),
-            pltpu.VMEM((1, entries), surf_cell.dtype),
-            pltpu.VMEM((steps, entries), f32),
-            pltpu.SemaphoreType.DMA((7,)),
-        ],
-        in_hbm=range(7),
+        scratch=[pltpu.VMEM(shape, f32), pltpu.SemaphoreType.DMA((4,))],
+        in_hbm=range(4),
     )
     if everywhere:
         tables = [table] + [

time: 34.7 us -> 36.2 us (1.043)
  waiting for transfers between devices: 14.1 us -> 16.3 us
  starting transfers between devices: 13.6 us -> 12.2 us
  Pallas kernels: 4.73 us -> 5.41 us
    ppermute x2, waiting for transfers between devices: 4.14 us -> 6.31 us  [sum_over(): lax.ppermute(value, axis, [(i, i ^ 2 * distance - 1) for i in range(count)])]
    ppermute x4, waiting for transfers between devices: 7.56 us -> 9.15 us  [exchange(): inner = lax.ppermute(to_inner, ('tgt', 'shot'), swap_pairs(count, shots, 0))]
    ppermute x2, waiting for transfers between devices: 2.37 us -> 0.79 us  [on_device(): lax.ppermute(table, 'tgt', [(i, i ^ far) for i in range(slabs)])]
    ppermute x2, starting transfers between devices: 1.64 us -> 0.25 us  [sum_over(): lax.ppermute(value, axis, [(i, i ^ 2 * distance - 1) for i in range(count)])]
    pallas_call x10 -> x11, Pallas kernels: 4.73 us -> 5.41 us  [on_chip(): pl.pallas_call(kernel, out_shape=[pltpu.VMEM(shape, dtype) for shape, dty...]
  transfers between devices with their start and end apart: 12 -> 12, of which waited for: 6 -> 6; matrix products, arithmetic and copies ran while one was open for 2% -> 2% of each run, Pallas kernels for 13% -> 14%
where the time goes in v6:
time: 36.2 us; the launch traced here: 36 us
  waiting for transfers between devices  16.3 us (45%)
  starting transfers between devices  12.2 us (34%)
  Pallas kernels  5.41 us (15%)
  between operations  0.76 us (2%)
  other arithmetic  0.69 us (2%)
  local copies, waits for them, and re-layouts  0.65 us (2%)
    ppermute x4, waiting for transfers between devices, exchange(): inner = lax.ppermute(to_inner, ('tgt', 'shot'), swap_pairs(count, shots, 0))  9.15 us
    ppermute x4, starting transfers between devices, exchange(): inner = lax.ppermute(to_inner, ('tgt', 'shot'), swap_pairs(count, shots, 0))  6.31 us
    ppermute x2, waiting for transfers between devices, sum_over(): lax.ppermute(value, axis, [(i, i ^ 2 * distance - 1) for i in range(count)])  6.31 us
    ppermute x2, starting transfers between devices, on_device(): lax.ppermute(table, 'tgt', [(i, i ^ far) for i in range(slabs)])  5.58 us
    pallas_call x11, Pallas kernels, on_chip(): pl.pallas_call(kernel, out_shape=[pltpu.VMEM(shape, dtype) for shape, dty...  5.41 us
    ppermute x2, waiting for transfers between devices, on_device(): lax.ppermute(table, 'tgt', [(i, i ^ far) for i in range(slabs)])  0.79 us
  transfers between devices with their start and end apart: 12, of which 6 were waited for; matrix products, arithmetic and copies ran while one was open for 2% of the time, Pallas kernels for 14%

profile of v6, /device:TPU:0, one launch (start us, length us, event | category | flops | bytes accessed | tf_op | source)
XLA Modules:
  0.0 36.0 jit_solution(16093903389919063242)
XLA Ops:
  0.6 3.1 %collective-permute-start = (f32[128,256]{1,0:T(8,128)}, f32[128,256]{1,0:T(8,128)S(1)}, u32[]{:S(2)}, u32[]{:S(2)}) collective-permute-start(f32[128,256]{1,0:T(8,128)} %bitcast.14), channel_id=1, source_target_pairs={{0,4},{1,5},{2,6},{3,7},{4,0},{5,1},{6,2},{7,3},{8,12},{9,13},{10,... | collective-permute-start | bytes 393224 | tf_op jit(solution)/shard_map/ppermute | solution.py:56
  3.7 0.0 collective-permute-start.1
  3.7 0.7 %shard_map.87.refs_4_.refs_0_ = f32[8,256]{1,0:T(8,128)S(1)} custom-call(s32[1,256]{1,0:T(1,128)} %bitcast.19, s32[1,256]{1,0:T(1,128)} %bitcast.20, f32[4,256]{1,0:T(4,128)} %bitcast.18), custom_call_target="tpu_custom_call" | custom-call | bytes 6144 | tf_op jit(solution)/shard_map/pallas_call | solution.py:22
  4.5 2.7 %collective-permute-start.4 = (f32[8,256]{1,0:T(8,128)S(1)}, f32[8,256]{1,0:T(8,128)S(1)}, u32[]{:S(2)}, u32[]{:S(2)}) collective-permute-start(f32[8,256]{1,0:T(8,128)S(1)} %shard_map.87.refs_4_.refs_0_), channel_id=1, source_target_pairs={{0,8},{4,12},{8,0},{12,4},{1,9},{5,13},{9,1},{13,5},{2,10},{6,14},... | collective-permute-start | bytes 24584 | tf_op jit(solution)/shard_map/ppermute | solution.py:320
  7.1 2.9 %collective-permute-start.5 = (f32[8,256]{1,0:T(8,128)S(1)}, f32[8,256]{1,0:T(8,128)S(1)}, u32[]{:S(2)}, u32[]{:S(2)}) collective-permute-start(f32[8,256]{1,0:T(8,128)S(1)} %shard_map.87.refs_4_.refs_0_), channel_id=1, source_target_pairs={{0,12},{4,8},{8,4},{12,0},{1,13},{5,9},{9,5},{13,1},{2,14},{6,10},... | collective-permute-start | bytes 24584 | tf_op jit(solution)/shard_map/ppermute | solution.py:320
  10.1 1.5 %shard_map.86 = (f32[128,256]{1,0:T(8,128)S(1)}, f32[128,256]{1,0:T(8,128)S(1)}, f32[128,256]{1,0:T(8,128)S(1)}, bf16[4,128,256]{2,1,0:T(8,128)(2,1)S(1)}) custom-call(f32[128,256]{1,0:T(8,128)} %bitcast.16, f32[128,256]{1,0:T(8,128)} %bitcast.12, f32[128,256]{1,0:T(8,128)} %bitcast.13, bf16[4,128,256]{2,1,0:T(8,128)(2,1)} %bitcast.11), custom_call_target="tpu_custom_call" | custom-call | flops 1310720 | bytes 655360 | tf_op jit(solution)/shard_map/pallas_call | solution.py:22
  11.5 0.0 collective-permute-done.refs_0_
  11.5 0.0 collective-permute-done.1.refs_1_
  11.5 0.1 shard_map.88
  11.6 0.1 collective-permute-start.2
  11.7 0.1 collective-permute-start.3
  11.8 0.0 collective-permute-done.4.refs_1_
  11.8 0.8 %collective-permute-done.5.refs_2_ = f32[8,256]{1,0:T(8,128)S(1)} collective-permute-done((f32[8,256]{1,0:T(8,128)S(1)}, f32[8,256]{1,0:T(8,128)S(1)}, u32[]{:S(2)}, u32[]{:S(2)}) %collective-permute-start.5) | collective-permute-done | bytes 8224 | tf_op jit(solution)/shard_map/ppermute | solution.py:320
  12.6 1.1 %shard_map.89 = (f32[128,256]{1,0:T(8,128)S(1)}, f32[128,256]{1,0:T(8,128)S(1)}, f32[128,256]{1,0:T(8,128)S(1)}, f32[128,256]{1,0:T(8,128)S(1)}, f32[128,256]{1,0:T(8,128)S(1)}, /*index=5*/f32[128,256]{1,0:T(8,128)S(1)}) custom-call(s32[1]{0:T(128)} %bitcast.here_ref, f32[8,256]{1,0:T(8,128)S(1)} %shard_map.87.refs_4_.refs_0_, ...), custom_call_target="tpu_custom_call" | custom-call | flops 3623878656 | bytes 24580 | tf_op jit(solution)/shard_map/pallas_call | solution.py:22
  13.7 3.0 %collective-permute-done.2.refs_0_ = f32[136,256]{1,0:T(8,128)S(1)} collective-permute-done((f32[136,256]{1,0:T(8,128)S(1)}, f32[136,256]{1,0:T(8,128)S(1)}, u32[]{:S(2)}, u32[]{:S(2)}) %collective-permute-start.2) | collective-permute-done | bytes 139296 | tf_op jit(solution)/shard_map/ppermute | solution.py:56
  16.8 0.5 %shard_map.90 = (f32[128,256]{1,0:T(8,128)S(1)}, f32[128,256]{1,0:T(8,128)S(1)}, f32[128,256]{1,0:T(8,128)S(1)}, f32[128,256]{1,0:T(8,128)S(1)}, f32[128,256]{1,0:T(8,128)S(1)}, /*index=5*/f32[128,256]{1,0:T(8,128)S(1)}) custom-call(s32[1]{0:T(128)} %bitcast.here_ref, f32[136,256]{1,0:T(8,128)S(1)} %collective-permute-done.2.refs_0_, ...), custom_call_target="tpu_custom_call" | custom-call | flops 1207959552 | bytes 925700 | tf_op jit(solution)/shard_map/pallas_call | solution.py:22
  17.3 0.4 %shard_map.91 = (f32[128,256]{1,0:T(8,128)S(1)}, f32[128,256]{1,0:T(8,128)S(1)}, f32[128,256]{1,0:T(8,128)S(1)}) custom-call(f32[128,256]{1,0:T(8,128)S(1)} %get-tuple-element.33.refs_0_, f32[128,256]{1,0:T(8,128)S(1)} %get-tuple-element.34.refs_1_, f32[128,256]{1,0:T(8,128)S(1)} %get-tuple-element.31.refs_3_.refs_2_, ...), custom_call_target="tpu_custom_call" | custom-call | flops 1310720 | bytes 917504 | tf_op jit(solution)/shard_map/pallas_call | solution.py:22
  17.7 0.0 collective-permute-done.3.refs_1_
  17.7 0.1 shard_map.92.refs_0_.refs_1_
  17.8 1.1 %collective-permute-start.6 = (f32[128,256]{1,0:T(8,128)S(1)}, f32[128,256]{1,0:T(8,128)S(1)}, u32[]{:S(2)}, u32[]{:S(2)}) collective-permute-start(f32[128,256]{1,0:T(8,128)S(1)} %shard_map.92.refs_0_.refs_1_), channel_id=1, source_target_pairs={{0,4},{1,5},{2,6},{3,7},{4,0},{5,1},{6,2},{7,3},{8,12},{9,13},{10,... | collective-permute-start | bytes 393224 | tf_op jit(solution)/shard_map/ppermute | solution.py:56
  18.9 0.0 collective-permute-start.7
  18.9 0.4 %shard_map.93 = (f32[128,256]{1,0:T(8,128)S(1)}, f32[128,256]{1,0:T(8,128)S(1)}) custom-call(f32[128,256]{1,0:T(8,128)S(1)} %shard_map.92.refs_0_.refs_1_, f32[128,256]{1,0:T(8,128)S(1)} %get-tuple-element.47.refs_1_, f32[128,256]{1,0:T(8,128)S(1)} %get-tuple-element.31.refs_3_.refs_2_, bf16[4,128,256]{2,1,0:T(8,128)(2,1)S(1)} %get-tuple-element.35.refs_3_, ...), custom_call_target="tpu_custom_call" | custom-call | flops 1310720 | bytes 917504 | tf_op jit(solution)/shard_map/pallas_call | solution.py:22
  19.3 3.6 %collective-permute-done.6.refs_0_ = f32[128,256]{1,0:T(8,128)S(1)} collective-permute-done((f32[128,256]{1,0:T(8,128)S(1)}, f32[128,256]{1,0:T(8,128)S(1)}, u32[]{:S(2)}, u32[]{:S(2)}) %collective-permute-start.6) | collective-permute-done | bytes 131104 | tf_op jit(solution)/shard_map/ppermute | solution.py:56
  22.8 0.0 collective-permute-done.7.refs_1_
  22.8 0.1 shard_map.94.refs_0_
  22.9 2.1 %collective-permute-start.8 = (f32[128,256]{1,0:T(8,128)S(1)}, f32[128,256]{1,0:T(8,128)S(1)}, u32[]{:S(2)}, u32[]{:S(2)}) collective-permute-start(f32[128,256]{1,0:T(8,128)S(1)} %shard_map.94.refs_0_), channel_id=1, source_target_pairs={{0,4},{1,5},{2,6},{3,7},{4,0},{5,1},{6,2},{7,3},{8,12},{9,13},{10,... | collective-permute-start | bytes 393224 | tf_op jit(solution)/shard_map/ppermute | solution.py:56
  25.0 0.0 collective-permute-start.9
  25.0 0.4 %shard_map.95 = (f32[128,256]{1,0:T(8,128)S(1)}, f32[128,256]{1,0:T(8,128)S(1)}, f32[128,256]{1,0:T(8,128)S(1)}) custom-call(f32[128,256]{1,0:T(8,128)S(1)} %shard_map.94.refs_0_, f32[128,256]{1,0:T(8,128)S(1)} %shard_map.92.refs_0_.refs_1_, f32[128,256]{1,0:T(8,128)S(1)} %get-tuple-element.31.refs_3_.refs_2_, ...), custom_call_target="tpu_custom_call" | custom-call | flops 1310720 | bytes 917504 | tf_op jit(solution)/shard_map/pallas_call | solution.py:22
  25.4 2.5 %collective-permute-done.8.refs_0_ = f32[128,256]{1,0:T(8,128)S(1)} collective-permute-done((f32[128,256]{1,0:T(8,128)S(1)}, f32[128,256]{1,0:T(8,128)S(1)}, u32[]{:S(2)}, u32[]{:S(2)}) %collective-permute-start.8) | collective-permute-done | bytes 131104 | tf_op jit(solution)/shard_map/ppermute | solution.py:56
  28.0 0.0 collective-permute-done.9.refs_1_
  28.0 0.1 shard_map.96
  28.1 0.1 collective-permute-start.10
  28.1 5.7 %collective-permute-done.10 = f32[128,256]{1,0:T(8,128)S(1)} collective-permute-done((f32[128,256]{1,0:T(8,128)S(1)}, f32[128,256]{1,0:T(8,128)S(1)}, u32[]{:S(2)}, u32[]{:S(2)}) %collective-permute-start.10) | collective-permute-done | bytes 131104 | tf_op jit(solution)/shard_map/ppermute | solution.py:272
  33.9 0.2 collective-permute-start.11
  34.1 0.7 %copy.9 = f32[1,4,32,256]{3,2,1,0:T(8,128)} copy(f32[1,4,32,256]{3,2,1,0:T(8,128)S(1)} %bitcast.10) | data formatting | bytes 262144
  34.7 0.6 %collective-permute-done.11 = f32[128,256]{1,0:T(8,128)S(1)} collective-permute-done((f32[128,256]{1,0:T(8,128)S(1)}, f32[128,256]{1,0:T(8,128)S(1)}, u32[]{:S(2)}, u32[]{:S(2)}) %collective-permute-start.11) | collective-permute-done | bytes 131104 | tf_op jit(solution)/shard_map/ppermute | solution.py:272
  35.3 0.7 %add.7 = f32[128,256]{1,0:T(8,128)} add(f32[128,256]{1,0:T(8,128)S(1)} %add.6, f32[128,256]{1,0:T(8,128)S(1)} %collective-permute-done.11) | non-fusion elementwise | flops 32768 | bytes 393216 | tf_op jit(solution)/shard_map/add | solution.py:272
  (1 shorter events, 0.0 us)
Async XLA Ops:
  0.6 10.9 %collective-permute-start = (f32[128,256]{1,0:T(8,128)}, f32[128,256]{1,0:T(8,128)S(1)}, u32[]{:S(2)}, u32[]{:S(2)}) collective-permute-start(f32[128,256]{1,0:T(8,128)} %bitcast.14), channel_id=1, source_target_pairs={{0,4},{1,5},{2,6},{3,7},{4,0},{5,1},{6,2},{7,3},{8,12},{9,13},{10,... | collective-permute-start | bytes 393224 | tf_op jit(solution)/shard_map/ppermute | solution.py:56
  3.7 7.8 %collective-permute-start.1 = (f32[128,256]{1,0:T(8,128)}, f32[128,256]{1,0:T(8,128)S(1)}, u32[]{:S(2)}, u32[]{:S(2)}) collective-permute-start(f32[128,256]{1,0:T(8,128)} %bitcast.15), channel_id=1, source_target_pairs={{0,1},{1,0},{2,3},{3,2},{4,8},{5,9},{6,10},{7,11},{8,4},{9,5},{10,... | collective-permute-start | bytes 393224 | tf_op jit(solution)/shard_map/ppermute | solution.py:55
  4.5 7.3 %collective-permute-start.4 = (f32[8,256]{1,0:T(8,128)S(1)}, f32[8,256]{1,0:T(8,128)S(1)}, u32[]{:S(2)}, u32[]{:S(2)}) collective-permute-start(f32[8,256]{1,0:T(8,128)S(1)} %shard_map.87.refs_4_.refs_0_), channel_id=1, source_target_pairs={{0,8},{4,12},{8,0},{12,4},{1,9},{5,13},{9,1},{13,5},{2,10},{6,14},... | collective-permute-start | bytes 24584 | tf_op jit(solution)/shard_map/ppermute | solution.py:320
  7.1 5.4 %collective-permute-start.5 = (f32[8,256]{1,0:T(8,128)S(1)}, f32[8,256]{1,0:T(8,128)S(1)}, u32[]{:S(2)}, u32[]{:S(2)}) collective-permute-start(f32[8,256]{1,0:T(8,128)S(1)} %shard_map.87.refs_4_.refs_0_), channel_id=1, source_target_pairs={{0,12},{4,8},{8,4},{12,0},{1,13},{5,9},{9,5},{13,1},{2,14},{6,10},... | collective-permute-start | bytes 24584 | tf_op jit(solution)/shard_map/ppermute | solution.py:320
  11.6 5.1 %collective-permute-start.2 = (f32[136,256]{1,0:T(8,128)S(1)}, f32[136,256]{1,0:T(8,128)S(1)}, u32[]{:S(2)}, u32[]{:S(2)}) collective-permute-start(f32[136,256]{1,0:T(8,128)S(1)} %get-tuple-element.32), channel_id=1, source_target_pairs={{0,4},{1,5},{2,6},{3,7},{4,0},{5,1},{6,2},{7,3},{8,12},{9,13},{10,... | collective-permute-start | bytes 417800 | tf_op jit(solution)/shard_map/ppermute | solution.py:56
  11.7 6.0 %collective-permute-start.3 = (f32[128,256]{1,0:T(8,128)S(1)}, f32[128,256]{1,0:T(8,128)S(1)}, u32[]{:S(2)}, u32[]{:S(2)}) collective-permute-start(f32[128,256]{1,0:T(8,128)S(1)} %get-tuple-element.33.refs_0_), channel_id=1, source_target_pairs={{0,1},{1,0},{2,3},{3,2},{4,8},{5,9},{6,10},{7,11},{8,4},{9,5},{10,... | collective-permute-start | bytes 393224 | tf_op jit(solution)/shard_map/ppermute | solution.py:55
  17.8 5.0 %collective-permute-start.6 = (f32[128,256]{1,0:T(8,128)S(1)}, f32[128,256]{1,0:T(8,128)S(1)}, u32[]{:S(2)}, u32[]{:S(2)}) collective-permute-start(f32[128,256]{1,0:T(8,128)S(1)} %shard_map.92.refs_0_.refs_1_), channel_id=1, source_target_pairs={{0,4},{1,5},{2,6},{3,7},{4,0},{5,1},{6,2},{7,3},{8,12},{9,13},{10,... | collective-permute-start | bytes 393224 | tf_op jit(solution)/shard_map/ppermute | solution.py:56
  18.9 4.0 %collective-permute-start.7 = (f32[128,256]{1,0:T(8,128)S(1)}, f32[128,256]{1,0:T(8,128)S(1)}, u32[]{:S(2)}, u32[]{:S(2)}) collective-permute-start(f32[128,256]{1,0:T(8,128)S(1)} %shard_map.92.refs_0_.refs_1_), channel_id=1, source_target_pairs={{0,1},{1,0},{2,3},{3,2},{4,8},{5,9},{6,10},{7,11},{8,4},{9,5},{10,... | collective-permute-start | bytes 393224 | tf_op jit(solution)/shard_map/ppermute | solution.py:55
  22.9 5.0 %collective-permute-start.8 = (f32[128,256]{1,0:T(8,128)S(1)}, f32[128,256]{1,0:T(8,128)S(1)}, u32[]{:S(2)}, u32[]{:S(2)}) collective-permute-start(f32[128,256]{1,0:T(8,128)S(1)} %shard_map.94.refs_0_), channel_id=1, source_target_pairs={{0,4},{1,5},{2,6},{3,7},{4,0},{5,1},{6,2},{7,3},{8,12},{9,13},{10,... | collective-permute-start | bytes 393224 | tf_op jit(solution)/shard_map/ppermute | solution.py:56
  25.0 3.0 %collective-permute-start.9 = (f32[128,256]{1,0:T(8,128)S(1)}, f32[128,256]{1,0:T(8,128)S(1)}, u32[]{:S(2)}, u32[]{:S(2)}) collective-permute-start(f32[128,256]{1,0:T(8,128)S(1)} %shard_map.94.refs_0_), channel_id=1, source_target_pairs={{0,1},{1,0},{2,3},{3,2},{4,8},{5,9},{6,10},{7,11},{8,4},{9,5},{10,... | collective-permute-start | bytes 393224 | tf_op jit(solution)/shard_map/ppermute | solution.py:55
  28.1 5.8 %collective-permute-start.10 = (f32[128,256]{1,0:T(8,128)S(1)}, f32[128,256]{1,0:T(8,128)S(1)}, u32[]{:S(2)}, u32[]{:S(2)}) collective-permute-start(f32[128,256]{1,0:T(8,128)S(1)} %get-tuple-element.57), channel_id=1, source_target_pairs={{0,3},{1,2},{2,1},{3,0},{4,7},{5,6},{6,5},{7,4},{8,11},{9,10},{10,... | collective-permute-start | bytes 393224 | tf_op jit(solution)/shard_map/ppermute | solution.py:272
  33.9 1.4 %collective-permute-start.11 = (f32[128,256]{1,0:T(8,128)S(1)}, f32[128,256]{1,0:T(8,128)S(1)}, u32[]{:S(2)}, u32[]{:S(2)}) collective-permute-start(f32[128,256]{1,0:T(8,128)S(1)} %add.6), channel_id=1, source_target_pairs={{0,1},{1,0},{2,3},{3,2},{4,5},{5,4},{6,7},{7,6},{8,9},{9,8},{10,11... | collective-permute-start | bytes 393224 | tf_op jit(solution)/shard_map/ppermute | solution.py:272

commit v7 on v5

--- a/solution.py
+++ b/solution.py
@@ -317,7 +317,7 @@
     if everywhere:
         tables = [table] + [
             lax.ppermute(table, "tgt", [(i, i ^ far) for i in range(slabs)])
-            for far in range(2, slabs)
+            for far in reversed(range(2, slabs))
         ]
         inject = None
     else:

time: 34.7 us -> 33.8 us (0.974)
  starting transfers between devices: 13.6 us -> 13 us
    ppermute x2, starting transfers between devices: 5.58 us -> 4.68 us  [on_device(): lax.ppermute(table, 'tgt', [(i, i ^ far) for i in range(slabs)])]
    ppermute x2, waiting for transfers between devices: 2.37 us -> 1.96 us  [on_device(): lax.ppermute(table, 'tgt', [(i, i ^ far) for i in range(slabs)])]
    ppermute x4, starting transfers between devices: 6.31 us -> 6.68 us  [exchange(): inner = lax.ppermute(to_inner, ('tgt', 'shot'), swap_pairs(count, shots, 0))]
  transfers between devices with their start and end apart: 12 -> 12, of which waited for: 6 -> 7; matrix products, arithmetic and copies ran while one was open for 2% -> 2% of each run, Pallas kernels for 13% -> 13%
where the time goes in v7:
time: 33.8 us; the launch traced here: 33.6 us
  waiting for transfers between devices  13.8 us (41%)
  starting transfers between devices  13 us (38%)
  Pallas kernels  4.74 us (14%)
  between operations  0.72 us (2%)
  other arithmetic  0.69 us (2%)
  local copies, waits for them, and re-layouts  0.66 us (2%)
    ppermute x4, waiting for transfers between devices, exchange(): inner = lax.ppermute(to_inner, ('tgt', 'shot'), swap_pairs(count, shots, 0))  7.69 us
    ppermute x4, starting transfers between devices, exchange(): inner = lax.ppermute(to_inner, ('tgt', 'shot'), swap_pairs(count, shots, 0))  6.68 us
    pallas_call x10, Pallas kernels, on_chip(): pl.pallas_call(kernel, out_shape=[pltpu.VMEM(shape, dtype) for shape, dty...  4.74 us
    ppermute x2, starting transfers between devices, on_device(): lax.ppermute(table, 'tgt', [(i, i ^ far) for i in range(slabs)])  4.68 us
    ppermute x2, waiting for transfers between devices, sum_over(): lax.ppermute(value, axis, [(i, i ^ distance) for i in range(count)])  4.15 us
    ppermute x2, waiting for transfers between devices, on_device(): lax.ppermute(table, 'tgt', [(i, i ^ far) for i in range(slabs)])  1.96 us
    ppermute x2, starting transfers between devices, sum_over(): lax.ppermute(value, axis, [(i, i ^ distance) for i in range(count)])  1.63 us
    add x2, other arithmetic, sum_over(): value + lax.ppermute(value, axis, [(i, i ^ distance) for i in range(count)])  0.69 us
  transfers between devices with their start and end apart: 12, of which 7 were waited for; matrix products, arithmetic and copies ran while one was open for 2% of the time, Pallas kernels for 13%

profile of v7, /device:TPU:0, one launch (start us, length us, event | category | flops | bytes accessed | tf_op | source)
XLA Modules:
  0.0 33.6 jit_solution(3281313894614167897)
XLA Ops:
  0.6 3.1 %collective-permute-start = (f32[128,256]{1,0:T(8,128)}, f32[128,256]{1,0:T(8,128)S(1)}, u32[]{:S(2)}, u32[]{:S(2)}) collective-permute-start(f32[128,256]{1,0:T(8,128)} %bitcast.14), channel_id=1, source_target_pairs={{0,4},{1,5},{2,6},{3,7},{4,0},{5,1},{6,2},{7,3},{8,12},{9,13},{10,... | collective-permute-start | bytes 393224 | tf_op jit(solution)/shard_map/ppermute | solution.py:56
  3.7 0.0 collective-permute-start.1
  3.7 1.5 %shard_map.86 = (f32[128,256]{1,0:T(8,128)S(1)}, f32[8,256]{1,0:T(8,128)S(1)}, f32[128,256]{1,0:T(8,128)S(1)}, f32[128,256]{1,0:T(8,128)S(1)}, bf16[4,128,256]{2,1,0:T(8,128)(2,1)S(1)}) custom-call(f32[128,256]{1,0:T(8,128)} %bitcast.16, f32[128,256]{1,0:T(8,128)} %bitcast.12, f32[128,256]{1,0:T(8,128)} %bitcast.13, bf16[4,128,256]{2,1,0:T(8,128)(2,1)} %bitcast.11, ...), custom_call_target="tpu_custom_call" | custom-call | flops 1310720 | bytes 661504 | tf_op jit(solution)/shard_map/pallas_call | solution.py:22
  5.3 2.5 %collective-permute-start.4 = (f32[8,256]{1,0:T(8,128)S(1)}, f32[8,256]{1,0:T(8,128)S(1)}, u32[]{:S(2)}, u32[]{:S(2)}) collective-permute-start(f32[8,256]{1,0:T(8,128)S(1)} %get-tuple-element.33.refs_4_.refs_0_), channel_id=1, source_target_pairs={{0,12},{4,8},{8,4},{12,0},{1,13},{5,9},{9,5},{13,1},{2,14},{6,10},... | collective-permute-start | bytes 24584 | tf_op jit(solution)/shard_map/ppermute | solution.py:319
  7.8 2.1 %collective-permute-start.5 = (f32[8,256]{1,0:T(8,128)S(1)}, f32[8,256]{1,0:T(8,128)S(1)}, u32[]{:S(2)}, u32[]{:S(2)}) collective-permute-start(f32[8,256]{1,0:T(8,128)S(1)} %get-tuple-element.33.refs_4_.refs_0_), channel_id=1, source_target_pairs={{0,8},{4,12},{8,0},{12,4},{1,9},{5,13},{9,1},{13,5},{2,10},{6,14},... | collective-permute-start | bytes 24584 | tf_op jit(solution)/shard_map/ppermute | solution.py:319
  9.9 0.0 collective-permute-done.refs_0_
  9.9 0.0 collective-permute-done.1.refs_1_
  9.9 0.1 shard_map.87
  10.0 0.5 %collective-permute-start.2 = (f32[136,256]{1,0:T(8,128)S(1)}, f32[136,256]{1,0:T(8,128)S(1)}, u32[]{:S(2)}, u32[]{:S(2)}) collective-permute-start(f32[136,256]{1,0:T(8,128)S(1)} %get-tuple-element.34), channel_id=1, source_target_pairs={{0,4},{1,5},{2,6},{3,7},{4,0},{5,1},{6,2},{7,3},{8,12},{9,13},{10,... | collective-permute-start | bytes 417800 | tf_op jit(solution)/shard_map/ppermute | solution.py:56
  10.5 0.0 collective-permute-start.3
  10.5 0.3 collective-permute-done.4.refs_1_
  10.8 1.7 %collective-permute-done.5.refs_2_ = f32[8,256]{1,0:T(8,128)S(1)} collective-permute-done((f32[8,256]{1,0:T(8,128)S(1)}, f32[8,256]{1,0:T(8,128)S(1)}, u32[]{:S(2)}, u32[]{:S(2)}) %collective-permute-start.5) | collective-permute-done | bytes 8224 | tf_op jit(solution)/shard_map/ppermute | solution.py:319
  12.5 1.1 %shard_map.88 = (f32[128,256]{1,0:T(8,128)S(1)}, f32[128,256]{1,0:T(8,128)S(1)}, f32[128,256]{1,0:T(8,128)S(1)}, f32[128,256]{1,0:T(8,128)S(1)}, f32[128,256]{1,0:T(8,128)S(1)}, /*index=5*/f32[128,256]{1,0:T(8,128)S(1)}) custom-call(s32[1]{0:T(128)} %bitcast.here_ref, f32[8,256]{1,0:T(8,128)S(1)} %get-tuple-element.33.refs_4_.refs_0_, ...), custom_call_target="tpu_custom_call" | custom-call | flops 3623878656 | bytes 24580 | tf_op jit(solution)/shard_map/pallas_call | solution.py:22
  13.6 1.6 %collective-permute-done.2.refs_0_ = f32[136,256]{1,0:T(8,128)S(1)} collective-permute-done((f32[136,256]{1,0:T(8,128)S(1)}, f32[136,256]{1,0:T(8,128)S(1)}, u32[]{:S(2)}, u32[]{:S(2)}) %collective-permute-start.2) | collective-permute-done | bytes 139296 | tf_op jit(solution)/shard_map/ppermute | solution.py:56
  15.2 0.5 %shard_map.89 = (f32[128,256]{1,0:T(8,128)S(1)}, f32[128,256]{1,0:T(8,128)S(1)}, f32[128,256]{1,0:T(8,128)S(1)}, f32[128,256]{1,0:T(8,128)S(1)}, f32[128,256]{1,0:T(8,128)S(1)}, /*index=5*/f32[128,256]{1,0:T(8,128)S(1)}) custom-call(s32[1]{0:T(128)} %bitcast.here_ref, f32[136,256]{1,0:T(8,128)S(1)} %collective-permute-done.2.refs_0_, ...), custom_call_target="tpu_custom_call" | custom-call | flops 1207959552 | bytes 925700 | tf_op jit(solution)/shard_map/pallas_call | solution.py:22
  15.7 0.4 %shard_map.90 = (f32[128,256]{1,0:T(8,128)S(1)}, f32[128,256]{1,0:T(8,128)S(1)}, f32[128,256]{1,0:T(8,128)S(1)}) custom-call(f32[128,256]{1,0:T(8,128)S(1)} %get-tuple-element.35.refs_0_, f32[128,256]{1,0:T(8,128)S(1)} %get-tuple-element.36.refs_1_, f32[128,256]{1,0:T(8,128)S(1)} %get-tuple-element.32.refs_3_.refs_2_, ...), custom_call_target="tpu_custom_call" | custom-call | flops 1310720 | bytes 917504 | tf_op jit(solution)/shard_map/pallas_call | solution.py:22
  16.1 0.0 collective-permute-done.3.refs_1_
  16.1 0.1 shard_map.91.refs_0_.refs_1_
  16.2 1.1 %collective-permute-start.6 = (f32[128,256]{1,0:T(8,128)S(1)}, f32[128,256]{1,0:T(8,128)S(1)}, u32[]{:S(2)}, u32[]{:S(2)}) collective-permute-start(f32[128,256]{1,0:T(8,128)S(1)} %shard_map.91.refs_0_.refs_1_), channel_id=1, source_target_pairs={{0,4},{1,5},{2,6},{3,7},{4,0},{5,1},{6,2},{7,3},{8,12},{9,13},{10,... | collective-permute-start | bytes 393224 | tf_op jit(solution)/shard_map/ppermute | solution.py:56
  17.3 0.0 collective-permute-start.7
  17.3 0.4 %shard_map.92 = (f32[128,256]{1,0:T(8,128)S(1)}, f32[128,256]{1,0:T(8,128)S(1)}) custom-call(f32[128,256]{1,0:T(8,128)S(1)} %shard_map.91.refs_0_.refs_1_, f32[128,256]{1,0:T(8,128)S(1)} %get-tuple-element.49.refs_1_, f32[128,256]{1,0:T(8,128)S(1)} %get-tuple-element.32.refs_3_.refs_2_, bf16[4,128,256]{2,1,0:T(8,128)(2,1)S(1)} %get-tuple-element.37.refs_3_, ...), custom_call_target="tpu_custom_call" | custom-call | flops 1310720 | bytes 917504 | tf_op jit(solution)/shard_map/pallas_call | solution.py:22
  17.7 3.6 %collective-permute-done.6.refs_0_ = f32[128,256]{1,0:T(8,128)S(1)} collective-permute-done((f32[128,256]{1,0:T(8,128)S(1)}, f32[128,256]{1,0:T(8,128)S(1)}, u32[]{:S(2)}, u32[]{:S(2)}) %collective-permute-start.6) | collective-permute-done | bytes 131104 | tf_op jit(solution)/shard_map/ppermute | solution.py:56
  21.2 0.0 collective-permute-done.7.refs_1_
  21.2 0.1 shard_map.93.refs_0_
  21.3 2.1 %collective-permute-start.8 = (f32[128,256]{1,0:T(8,128)S(1)}, f32[128,256]{1,0:T(8,128)S(1)}, u32[]{:S(2)}, u32[]{:S(2)}) collective-permute-start(f32[128,256]{1,0:T(8,128)S(1)} %shard_map.93.refs_0_), channel_id=1, source_target_pairs={{0,4},{1,5},{2,6},{3,7},{4,0},{5,1},{6,2},{7,3},{8,12},{9,13},{10,... | collective-permute-start | bytes 393224 | tf_op jit(solution)/shard_map/ppermute | solution.py:56
  23.4 0.0 collective-permute-start.9
  23.4 0.4 %shard_map.94 = (f32[128,256]{1,0:T(8,128)S(1)}, f32[128,256]{1,0:T(8,128)S(1)}, f32[128,256]{1,0:T(8,128)S(1)}) custom-call(f32[128,256]{1,0:T(8,128)S(1)} %shard_map.93.refs_0_, f32[128,256]{1,0:T(8,128)S(1)} %shard_map.91.refs_0_.refs_1_, f32[128,256]{1,0:T(8,128)S(1)} %get-tuple-element.32.refs_3_.refs_2_, ...), custom_call_target="tpu_custom_call" | custom-call | flops 1310720 | bytes 917504 | tf_op jit(solution)/shard_map/pallas_call | solution.py:22
  23.8 2.5 %collective-permute-done.8.refs_0_ = f32[128,256]{1,0:T(8,128)S(1)} collective-permute-done((f32[128,256]{1,0:T(8,128)S(1)}, f32[128,256]{1,0:T(8,128)S(1)}, u32[]{:S(2)}, u32[]{:S(2)}) %collective-permute-start.8) | collective-permute-done | bytes 131104 | tf_op jit(solution)/shard_map/ppermute | solution.py:56
  26.4 0.0 collective-permute-done.9.refs_1_
  26.4 0.1 shard_map.95
  26.5 1.6 %collective-permute-start.10 = (f32[128,256]{1,0:T(8,128)S(1)}, f32[128,256]{1,0:T(8,128)S(1)}, u32[]{:S(2)}, u32[]{:S(2)}) collective-permute-start(f32[128,256]{1,0:T(8,128)S(1)} %get-tuple-element.59), channel_id=1, source_target_pairs={{0,2},{1,3},{2,0},{3,1},{4,6},{5,7},{6,4},{7,5},{8,10},{9,11},{10,... | collective-permute-start | bytes 393224 | tf_op jit(solution)/shard_map/ppermute | solution.py:270
  28.0 3.5 %collective-permute-done.10 = f32[128,256]{1,0:T(8,128)S(1)} collective-permute-done((f32[128,256]{1,0:T(8,128)S(1)}, f32[128,256]{1,0:T(8,128)S(1)}, u32[]{:S(2)}, u32[]{:S(2)}) %collective-permute-start.10) | collective-permute-done | bytes 131104 | tf_op jit(solution)/shard_map/ppermute | solution.py:270
  31.5 0.1 collective-permute-start.11
  31.6 0.7 %copy.9 = f32[1,4,32,256]{3,2,1,0:T(8,128)} copy(f32[1,4,32,256]{3,2,1,0:T(8,128)S(1)} %bitcast.10) | data formatting | bytes 262144
  32.3 0.7 %collective-permute-done.11 = f32[128,256]{1,0:T(8,128)S(1)} collective-permute-done((f32[128,256]{1,0:T(8,128)S(1)}, f32[128,256]{1,0:T(8,128)S(1)}, u32[]{:S(2)}, u32[]{:S(2)}) %collective-permute-start.11) | collective-permute-done | bytes 131104 | tf_op jit(solution)/shard_map/ppermute | solution.py:270
  32.9 0.7 %add.7 = f32[128,256]{1,0:T(8,128)} add(f32[128,256]{1,0:T(8,128)S(1)} %add.6, f32[128,256]{1,0:T(8,128)S(1)} %collective-permute-done.11) | non-fusion elementwise | flops 32768 | bytes 393216 | tf_op jit(solution)/shard_map/add | solution.py:270
  (1 shorter events, 0.0 us)
Async XLA Ops:
  0.6 9.3 %collective-permute-start = (f32[128,256]{1,0:T(8,128)}, f32[128,256]{1,0:T(8,128)S(1)}, u32[]{:S(2)}, u32[]{:S(2)}) collective-permute-start(f32[128,256]{1,0:T(8,128)} %bitcast.14), channel_id=1, source_target_pairs={{0,4},{1,5},{2,6},{3,7},{4,0},{5,1},{6,2},{7,3},{8,12},{9,13},{10,... | collective-permute-start | bytes 393224 | tf_op jit(solution)/shard_map/ppermute | solution.py:56
  3.7 6.2 %collective-permute-start.1 = (f32[128,256]{1,0:T(8,128)}, f32[128,256]{1,0:T(8,128)S(1)}, u32[]{:S(2)}, u32[]{:S(2)}) collective-permute-start(f32[128,256]{1,0:T(8,128)} %bitcast.15), channel_id=1, source_target_pairs={{0,1},{1,0},{2,3},{3,2},{4,8},{5,9},{6,10},{7,11},{8,4},{9,5},{10,... | collective-permute-start | bytes 393224 | tf_op jit(solution)/shard_map/ppermute | solution.py:55
  5.3 5.5 %collective-permute-start.4 = (f32[8,256]{1,0:T(8,128)S(1)}, f32[8,256]{1,0:T(8,128)S(1)}, u32[]{:S(2)}, u32[]{:S(2)}) collective-permute-start(f32[8,256]{1,0:T(8,128)S(1)} %get-tuple-element.33.refs_4_.refs_0_), channel_id=1, source_target_pairs={{0,12},{4,8},{8,4},{12,0},{1,13},{5,9},{9,5},{13,1},{2,14},{6,10},... | collective-permute-start | bytes 24584 | tf_op jit(solution)/shard_map/ppermute | solution.py:319
  7.8 4.7 %collective-permute-start.5 = (f32[8,256]{1,0:T(8,128)S(1)}, f32[8,256]{1,0:T(8,128)S(1)}, u32[]{:S(2)}, u32[]{:S(2)}) collective-permute-start(f32[8,256]{1,0:T(8,128)S(1)} %get-tuple-element.33.refs_4_.refs_0_), channel_id=1, source_target_pairs={{0,8},{4,12},{8,0},{12,4},{1,9},{5,13},{9,1},{13,5},{2,10},{6,14},... | collective-permute-start | bytes 24584 | tf_op jit(solution)/shard_map/ppermute | solution.py:319
  10.0 5.1 %collective-permute-start.2 = (f32[136,256]{1,0:T(8,128)S(1)}, f32[136,256]{1,0:T(8,128)S(1)}, u32[]{:S(2)}, u32[]{:S(2)}) collective-permute-start(f32[136,256]{1,0:T(8,128)S(1)} %get-tuple-element.34), channel_id=1, source_target_pairs={{0,4},{1,5},{2,6},{3,7},{4,0},{5,1},{6,2},{7,3},{8,12},{9,13},{10,... | collective-permute-start | bytes 417800 | tf_op jit(solution)/shard_map/ppermute | solution.py:56
  10.5 5.6 %collective-permute-start.3 = (f32[128,256]{1,0:T(8,128)S(1)}, f32[128,256]{1,0:T(8,128)S(1)}, u32[]{:S(2)}, u32[]{:S(2)}) collective-permute-start(f32[128,256]{1,0:T(8,128)S(1)} %get-tuple-element.35.refs_0_), channel_id=1, source_target_pairs={{0,1},{1,0},{2,3},{3,2},{4,8},{5,9},{6,10},{7,11},{8,4},{9,5},{10,... | collective-permute-start | bytes 393224 | tf_op jit(solution)/shard_map/ppermute | solution.py:55
  16.2 5.0 %collective-permute-start.6 = (f32[128,256]{1,0:T(8,128)S(1)}, f32[128,256]{1,0:T(8,128)S(1)}, u32[]{:S(2)}, u32[]{:S(2)}) collective-permute-start(f32[128,256]{1,0:T(8,128)S(1)} %shard_map.91.refs_0_.refs_1_), channel_id=1, source_target_pairs={{0,4},{1,5},{2,6},{3,7},{4,0},{5,1},{6,2},{7,3},{8,12},{9,13},{10,... | collective-permute-start | bytes 393224 | tf_op jit(solution)/shard_map/ppermute | solution.py:56
  17.3 4.0 %collective-permute-start.7 = (f32[128,256]{1,0:T(8,128)S(1)}, f32[128,256]{1,0:T(8,128)S(1)}, u32[]{:S(2)}, u32[]{:S(2)}) collective-permute-start(f32[128,256]{1,0:T(8,128)S(1)} %shard_map.91.refs_0_.refs_1_), channel_id=1, source_target_pairs={{0,1},{1,0},{2,3},{3,2},{4,8},{5,9},{6,10},{7,11},{8,4},{9,5},{10,... | collective-permute-start | bytes 393224 | tf_op jit(solution)/shard_map/ppermute | solution.py:55
  21.3 5.0 %collective-permute-start.8 = (f32[128,256]{1,0:T(8,128)S(1)}, f32[128,256]{1,0:T(8,128)S(1)}, u32[]{:S(2)}, u32[]{:S(2)}) collective-permute-start(f32[128,256]{1,0:T(8,128)S(1)} %shard_map.93.refs_0_), channel_id=1, source_target_pairs={{0,4},{1,5},{2,6},{3,7},{4,0},{5,1},{6,2},{7,3},{8,12},{9,13},{10,... | collective-permute-start | bytes 393224 | tf_op jit(solution)/shard_map/ppermute | solution.py:56
  23.4 3.0 %collective-permute-start.9 = (f32[128,256]{1,0:T(8,128)S(1)}, f32[128,256]{1,0:T(8,128)S(1)}, u32[]{:S(2)}, u32[]{:S(2)}) collective-permute-start(f32[128,256]{1,0:T(8,128)S(1)} %shard_map.93.refs_0_), channel_id=1, source_target_pairs={{0,1},{1,0},{2,3},{3,2},{4,8},{5,9},{6,10},{7,11},{8,4},{9,5},{10,... | collective-permute-start | bytes 393224 | tf_op jit(solution)/shard_map/ppermute | solution.py:55
  26.5 5.0 %collective-permute-start.10 = (f32[128,256]{1,0:T(8,128)S(1)}, f32[128,256]{1,0:T(8,128)S(1)}, u32[]{:S(2)}, u32[]{:S(2)}) collective-permute-start(f32[128,256]{1,0:T(8,128)S(1)} %get-tuple-element.59), channel_id=1, source_target_pairs={{0,2},{1,3},{2,0},{3,1},{4,6},{5,7},{6,4},{7,5},{8,10},{9,11},{10,... | collective-permute-start | bytes 393224 | tf_op jit(solution)/shard_map/ppermute | solution.py:270
  31.5 1.4 %collective-permute-start.11 = (f32[128,256]{1,0:T(8,128)S(1)}, f32[128,256]{1,0:T(8,128)S(1)}, u32[]{:S(2)}, u32[]{:S(2)}) collective-permute-start(f32[128,256]{1,0:T(8,128)S(1)} %add.6), channel_id=1, source_target_pairs={{0,1},{1,0},{2,3},{3,2},{4,5},{5,4},{6,7},{7,6},{8,9},{9,8},{10,11... | collective-permute-start | bytes 393224 | tf_op jit(solution)/shard_map/ppermute | solution.py:270

commit v8 on v7

--- a/solution.py
+++ b/solution.py
@@ -11,6 +11,7 @@
 GATHER_LIMIT = 4096
 REACH = 4
 PIECES = 3
+EFFORT = 4
 
 COEFFS = (-205.0 / 72.0, 8.0 / 5.0, -1.0 / 5.0, 8.0 / 315.0, -1.0 / 560.0)
 
@@ -50,10 +51,10 @@
     return routes
 
 
-def exchange(to_inner, to_outer):
+def exchange(slab):
     count, shots = lax.axis_size("tgt"), lax.axis_size("shot")
-    outer = lax.ppermute(to_outer, ("tgt", "shot"), swap_pairs(count, shots, 1))
-    inner = lax.ppermute(to_inner, ("tgt", "shot"), swap_pairs(count, shots, 0))
+    outer = lax.ppermute(slab, ("tgt", "shot"), swap_pairs(count, shots, 1))
+    inner = lax.ppermute(slab, ("tgt", "shot"), swap_pairs(count, shots, 0))
     return inner, outer
 
 
@@ -74,37 +75,35 @@
     return [flat[:, i : i + chunk] for i in range(0, owners * CAP, chunk)]
 
 
-def inject_kernel(steps, first_rows, with_halo, more, here_ref, *refs):
-    table_refs, refs = refs[: len(first_rows)], refs[len(first_rows) :]
-    in_refs, out_refs = (refs[: len(refs) // 2], refs[len(refs) // 2 :]) if more else ((), refs)
+def inject_kernel(steps, table_count, with_halo, here_ref, *refs):
+    table_refs, out_refs = refs[:table_count], refs[table_count:]
     rows, lanes = out_refs[0].shape
     here = here_ref[0].astype(jnp.float32)
     left, right = [], []
-    for table_ref, firsts in zip(table_refs, first_rows):
-        for first in firsts:
-            table = table_ref[first : first + 2 + steps]
-            count = table.shape[1]
-            slab = table[0:1]
-            cell = table[1:2].astype(jnp.int32)
-            row, lane = cell // lanes, cell % lanes
-            in_lane = lax.broadcasted_iota(jnp.int32, (lanes, count), 0) == lane
-            spread = jnp.where(in_lane, 1.0, 0.0).astype(jnp.bfloat16)
-            each_row = lax.broadcasted_iota(jnp.int32, (rows, count), 0)
-            in_row = [each_row == jnp.where(slab == here, row, -1)]
-            if with_halo:
-                in_row.append(each_row == jnp.where(slab == here - 1.0, row, -1))
-                in_row.append(each_row == jnp.where(slab == here + 1.0, row, -1))
-            rest = [table[2 + step : 3 + step] for step in range(steps)]
-            for _ in range(PIECES):
-                part = [r.astype(jnp.bfloat16).astype(jnp.float32) for r in rest]
-                rest = [r - p for r, p in zip(rest, part)]
-                picks = [(in_row[0], p) for p in part] + [(m, part[0]) for m in in_row[1:]]
-                left.append(
-                    jnp.concatenate(
-                        [jnp.where(m, p, 0.0).astype(jnp.bfloat16) for m, p in picks], axis=0
-                    )
+    for table_ref in table_refs:
+        table = table_ref[...]
+        count = table.shape[1]
+        slab = table[0:1]
+        cell = table[1:2].astype(jnp.int32)
+        row, lane = cell // lanes, cell % lanes
+        in_lane = lax.broadcasted_iota(jnp.int32, (lanes, count), 0) == lane
+        spread = jnp.where(in_lane, 1.0, 0.0).astype(jnp.bfloat16)
+        each_row = lax.broadcasted_iota(jnp.int32, (rows, count), 0)
+        in_row = [each_row == jnp.where(slab == here, row, -1)]
+        if with_halo:
+            in_row.append(each_row == jnp.where(slab == here - 1.0, row, -1))
+            in_row.append(each_row == jnp.where(slab == here + 1.0, row, -1))
+        rest = [table[2 + step : 3 + step] for step in range(steps)]
+        for _ in range(PIECES):
+            part = [r.astype(jnp.bfloat16).astype(jnp.float32) for r in rest]
+            rest = [r - p for r, p in zip(rest, part)]
+            picks = [(in_row[0], p) for p in part] + [(m, part[0]) for m in in_row[1:]]
+            left.append(
+                jnp.concatenate(
+                    [jnp.where(m, p, 0.0).astype(jnp.bfloat16) for m, p in picks], axis=0
                 )
-                right.append(spread)
+            )
+            right.append(spread)
     total = lax.dot_general(
         jnp.concatenate(left, axis=1),
         jnp.concatenate(right, axis=1),
@@ -112,20 +111,18 @@
         preferred_element_type=jnp.float32,
     )
     for i, out_ref in enumerate(out_refs):
-        mine = total[i * rows : (i + 1) * rows]
-        out_ref[...] = in_refs[i][...] + mine if more else mine
-
-
-def injection(here, tables, first_rows, steps, shape, with_halo, before=()):
+        out_ref[...] = total[i * rows : (i + 1) * rows]
+
+
+def injection(here, tables, steps, shape, with_halo):
     count = steps + 2 * with_halo
-    entries = sum(t.shape[1] * len(f) for t, f in zip(tables, first_rows))
+    entries = sum(t.shape[1] for t in tables)
     return on_chip(
-        functools.partial(inject_kernel, steps, first_rows, with_halo, len(before) > 0),
+        functools.partial(inject_kernel, steps, len(tables), with_halo),
         [(shape, jnp.float32)] * count,
         here,
         *tables,
-        *before,
-        flops=4 * 2 * PIECES * count * shape[0] * shape[1] * entries,
+        flops=EFFORT * 2 * PIECES * count * shape[0] * shape[1] * entries,
     )
 
 
@@ -217,15 +214,16 @@
         grad_ref[s] = grad
 
 
-def halo_kernel(planes, slabs, fix_inject, last, tables, here_ref, *refs):
+def halo_kernel(planes, slabs, fix_inject, last, here_ref, *refs):
     refs = list(refs)
     inner_ref, outer_ref, part_ref, courant_ref = refs[:4]
+    if last:
+        inner_ref, outer_ref = outer_ref, inner_ref
     refs = refs[4:]
     fix_refs = (refs.pop(0), refs.pop(0)) if fix_inject else None
     weight_ref, grad_in_ref = (refs.pop(0), refs.pop(0)) if last else (None, None)
-    table_refs = [refs.pop(0) for _ in range(tables)]
     fresh_ref = refs.pop(0)
-    other_ref = refs.pop(0) if last or tables else None
+    grad_ref = refs.pop(0) if last else None
     here = here_ref[0]
     even = here % 2 == 0
     rows = part_ref.shape[0]
@@ -253,12 +251,7 @@
         fresh = part_ref[s] + courant * courant * sum(terms[1:], terms[0])
         fresh_ref[s] = fresh
         if last:
-            other_ref[s] = grad_in_ref[s] + weight_ref[s] * fresh
-        if tables:
-            other_ref[s] = fresh
-    for i, table_ref in enumerate(table_refs):
-        first = rows + i * table_ref.shape[0]
-        other_ref[first : first + table_ref.shape[0]] = table_ref[...]
+            grad_ref[s] = grad_in_ref[s] + weight_ref[s] * fresh
 
 
 def sum_over(value, axis):
@@ -282,11 +275,9 @@
     here = lax.axis_index("tgt").reshape(1)
     now = adjoint_now.reshape(shape)
     table_rows = -(-(2 + steps) // 8) * 8
-    everywhere = (
-        slabs & (slabs - 1) == 0 and slabs * entries <= GATHER_LIMIT and entries == lanes
-    )
-
-    received = exchange(now, now)
+    everywhere = slabs & (slabs - 1) == 0 and slabs * entries <= GATHER_LIMIT
+
+    received = exchange(now)
     f32 = jnp.float32
     part, table, current, courant_here, fwd = on_chip(
         functools.partial(first_kernel, planes, table_rows),
@@ -317,12 +308,12 @@
     if everywhere:
         tables = [table] + [
             lax.ppermute(table, "tgt", [(i, i ^ far) for i in range(slabs)])
-            for far in reversed(range(2, slabs))
+            for far in [*range(slabs - 1, 2, -1), *range(1, min(slabs, 3))]
         ]
         inject = None
     else:
         tables = slotted_tables(table, surf_dest, slabs)
-        inject = injection(here, tables, [[0]] * len(tables), steps, shape, False)
+        inject = injection(here, tables, steps, shape, False)
         part = part + inject[0]
         tables = []
 
@@ -343,25 +334,19 @@
             )
             if fix:
                 current = extra.pop(0)
-        carried = tables[:1] if step == 0 else []
-        args = [here, *received, part, courant_here, *fixes]
+        args = [here, *(received[::-1] if last else received), part, courant_here, *fixes]
         args += [*extra, grad] if last else []
-        outs = [(shape, f32)] + ([(shape, f32)] if last else [])
-        if carried:
-            outs.append(((rows + len(carried) * table_rows, lanes), f32))
         fresh, *other = on_chip(
-            functools.partial(halo_kernel, planes, slabs, fix, last, len(carried)),
-            outs,
+            functools.partial(halo_kernel, planes, slabs, fix, last),
+            [(shape, f32)] * (1 + last),
             *args,
-            *carried,
             flops=10 * rows * lanes,
         )
         later_field, current, fixes = current, fresh, []
         if not last:
-            received = exchange(other[0] if carried else fresh, fresh)
-        if carried:
-            inject = injection(here, tables, [[0]] * len(tables), steps, shape, True)
-            inject = injection(here, received[:1], [[rows]], steps, shape, True, inject)
+            received = exchange(fresh)
+        if everywhere and step == 0:
+            inject = injection(here, tables, steps, shape, True)
             fixes = inject[steps:]
     grad = sum_over(other[0], "shot")
     return (current.reshape(adjoint_now.shape), grad.reshape(courant.shape))

time: 33.8 us -> 32.9 us (0.973)
  waiting for transfers between devices: 13.8 us -> 10.4 us
  starting transfers between devices: 13 us -> 15.8 us
    ppermute x8, starting transfers between devices: 6.69 us -> 9.51 us  [the longest x4 9.5 us: exchange(): inner = lax.ppermute(slab, ('tgt', 'shot'), swap_pairs(count, shots, 0))]
    ppermute x8, waiting for transfers between devices: 7.7 us -> 5.15 us  [the longest x4 5.14 us: exchange(): inner = lax.ppermute(slab, ('tgt', 'shot'), swap_pairs(count, shots, 0))]
    ppermute x2 -> x3, waiting for transfers between devices: 1.96 us -> 1.08 us  [on_device(): lax.ppermute(table, 'tgt', [(i, i ^ far) for i in range(slabs)])]
    pallas_call x10 -> x9, Pallas kernels: 4.74 us -> 4.45 us  [on_chip(): pl.pallas_call(kernel, out_shape=[pltpu.VMEM(shape, dtype) for shape, dty...]
    ppermute x2 -> x3, starting transfers between devices: 4.68 us -> 4.68 us  [on_device(): lax.ppermute(table, 'tgt', [(i, i ^ far) for i in range(slabs)])]
  transfers between devices with their start and end apart: 12 -> 13, of which waited for: 7 -> 5; matrix products, arithmetic and copies ran while one was open for 2% -> 2% of each run, Pallas kernels for 13% -> 13%
where the time goes in v8:
time: 32.9 us; the launch traced here: 32.7 us
  starting transfers between devices  15.8 us (48%)
  waiting for transfers between devices  10.4 us (32%)
  Pallas kernels  4.45 us (14%)
  between operations  0.71 us (2%)
  other arithmetic  0.69 us (2%)
  local copies, waits for them, and re-layouts  0.66 us (2%)
    ppermute x4, starting transfers between devices, exchange(): inner = lax.ppermute(slab, ('tgt', 'shot'), swap_pairs(count, shots, 0))  9.5 us
    ppermute x4, waiting for transfers between devices, exchange(): inner = lax.ppermute(slab, ('tgt', 'shot'), swap_pairs(count, shots, 0))  5.14 us
    ppermute x3, starting transfers between devices, on_device(): lax.ppermute(table, 'tgt', [(i, i ^ far) for i in range(slabs)])  4.68 us
    pallas_call x9, Pallas kernels, on_chip(): pl.pallas_call(kernel, out_shape=[pltpu.VMEM(shape, dtype) for shape, dty...  4.45 us
    ppermute x2, waiting for transfers between devices, sum_over(): lax.ppermute(value, axis, [(i, i ^ distance) for i in range(count)])  4.15 us
    ppermute x2, starting transfers between devices, sum_over(): lax.ppermute(value, axis, [(i, i ^ distance) for i in range(count)])  1.63 us
    ppermute x3, waiting for transfers between devices, on_device(): lax.ppermute(table, 'tgt', [(i, i ^ far) for i in range(slabs)])  1.08 us
    add x2, other arithmetic, sum_over(): value + lax.ppermute(value, axis, [(i, i ^ distance) for i in range(count)])  0.69 us
  transfers between devices with their start and end apart: 13, of which 5 were waited for; matrix products, arithmetic and copies ran while one was open for 2% of the time, Pallas kernels for 13%

profile of v8, /device:TPU:0, one launch (start us, length us, event | category | flops | bytes accessed | tf_op | source)
XLA Modules:
  0.0 32.7 jit_solution(3342077641009971838)
XLA Ops:
  0.6 3.1 %collective-permute-start = (f32[128,256]{1,0:T(8,128)}, f32[128,256]{1,0:T(8,128)S(1)}, u32[]{:S(2)}, u32[]{:S(2)}) collective-permute-start(f32[128,256]{1,0:T(8,128)} %bitcast.14), channel_id=1, source_target_pairs={{0,4},{1,5},{2,6},{3,7},{4,0},{5,1},{6,2},{7,3},{8,12},{9,13},{10,... | collective-permute-start | bytes 393224 | tf_op jit(solution)/shard_map/ppermute | solution.py:57
  3.7 0.0 collective-permute-start.1
  3.7 1.5 %shard_map.86 = (f32[128,256]{1,0:T(8,128)S(1)}, f32[8,256]{1,0:T(8,128)S(1)}, f32[128,256]{1,0:T(8,128)S(1)}, f32[128,256]{1,0:T(8,128)S(1)}, bf16[4,128,256]{2,1,0:T(8,128)(2,1)S(1)}) custom-call(f32[128,256]{1,0:T(8,128)} %bitcast.16, f32[128,256]{1,0:T(8,128)} %bitcast.12, f32[128,256]{1,0:T(8,128)} %bitcast.13, bf16[4,128,256]{2,1,0:T(8,128)(2,1)} %bitcast.11, ...), custom_call_target="tpu_custom_call" | custom-call | flops 1310720 | bytes 661504 | tf_op jit(solution)/shard_map/pallas_call | solution.py:23
  5.3 2.5 %collective-permute-start.4 = (f32[8,256]{1,0:T(8,128)S(1)}, f32[8,256]{1,0:T(8,128)S(1)}, u32[]{:S(2)}, u32[]{:S(2)}) collective-permute-start(f32[8,256]{1,0:T(8,128)S(1)} %get-tuple-element.27.refs_0_), channel_id=1, source_target_pairs={{0,12},{4,8},{8,4},{12,0},{1,13},{5,9},{9,5},{13,1},{2,14},{6,10},... | collective-permute-start | bytes 24584 | tf_op jit(solution)/shard_map/ppermute | solution.py:310
  7.8 0.8 %collective-permute-start.5 = (f32[8,256]{1,0:T(8,128)S(1)}, f32[8,256]{1,0:T(8,128)S(1)}, u32[]{:S(2)}, u32[]{:S(2)}) collective-permute-start(f32[8,256]{1,0:T(8,128)S(1)} %get-tuple-element.27.refs_0_), channel_id=1, source_target_pairs={{0,4},{4,0},{8,12},{12,8},{1,5},{5,1},{9,13},{13,9},{2,6},{6,2},{1... | collective-permute-start | bytes 24584 | tf_op jit(solution)/shard_map/ppermute | solution.py:310
  8.5 1.4 %collective-permute-start.6 = (f32[8,256]{1,0:T(8,128)S(1)}, f32[8,256]{1,0:T(8,128)S(1)}, u32[]{:S(2)}, u32[]{:S(2)}) collective-permute-start(f32[8,256]{1,0:T(8,128)S(1)} %get-tuple-element.27.refs_0_), channel_id=1, source_target_pairs={{0,8},{4,12},{8,0},{12,4},{1,9},{5,13},{9,1},{13,5},{2,10},{6,14},... | collective-permute-start | bytes 24584 | tf_op jit(solution)/shard_map/ppermute | solution.py:310
  9.9 0.0 collective-permute-done.refs_0_
  9.9 0.0 collective-permute-done.1.refs_1_
  9.9 0.1 shard_map.87.refs_0_
  10.0 2.1 %collective-permute-start.2 = (f32[128,256]{1,0:T(8,128)S(1)}, f32[128,256]{1,0:T(8,128)S(1)}, u32[]{:S(2)}, u32[]{:S(2)}) collective-permute-start(f32[128,256]{1,0:T(8,128)S(1)} %shard_map.87.refs_0_), channel_id=1, source_target_pairs={{0,4},{1,5},{2,6},{3,7},{4,0},{5,1},{6,2},{7,3},{8,12},{9,13},{10,... | collective-permute-start | bytes 393224 | tf_op jit(solution)/shard_map/ppermute | solution.py:57
  12.1 0.0 collective-permute-start.3
  12.1 0.0 collective-permute-done.4.refs_1_
  12.1 0.0 collective-permute-done.5.refs_2_
  12.1 1.1 %collective-permute-done.6.refs_3_ = f32[8,256]{1,0:T(8,128)S(1)} collective-permute-done((f32[8,256]{1,0:T(8,128)S(1)}, f32[8,256]{1,0:T(8,128)S(1)}, u32[]{:S(2)}, u32[]{:S(2)}) %collective-permute-start.6) | collective-permute-done | bytes 8224 | tf_op jit(solution)/shard_map/ppermute | solution.py:310
  13.2 1.4 %shard_map.88 = (f32[128,256]{1,0:T(8,128)S(1)}, f32[128,256]{1,0:T(8,128)S(1)}, f32[128,256]{1,0:T(8,128)S(1)}, f32[128,256]{1,0:T(8,128)S(1)}, f32[128,256]{1,0:T(8,128)S(1)}, /*index=5*/f32[128,256]{1,0:T(8,128)S(1)}) custom-call(s32[1]{0:T(128)} %bitcast.here_ref, f32[8,256]{1,0:T(8,128)S(1)} %get-tuple-element.27.refs_0_, ...), custom_call_target="tpu_custom_call" | custom-call | flops 4831838208 | bytes 32772 | tf_op jit(solution)/shard_map/pallas_call | solution.py:23
  14.6 0.4 %shard_map.89 = (f32[128,256]{1,0:T(8,128)S(1)}, f32[128,256]{1,0:T(8,128)S(1)}, f32[128,256]{1,0:T(8,128)S(1)}) custom-call(f32[128,256]{1,0:T(8,128)S(1)} %shard_map.87.refs_0_, f32[128,256]{1,0:T(8,128)S(1)} %get-tuple-element.25.refs_1_, f32[128,256]{1,0:T(8,128)S(1)} %get-tuple-element.24.refs_3_.refs_2_, ...), custom_call_target="tpu_custom_call" | custom-call | flops 1310720 | bytes 917504 | tf_op jit(solution)/shard_map/pallas_call | solution.py:23
  15.0 0.0 collective-permute-done.2.refs_0_
  15.1 0.0 collective-permute-done.3.refs_1_
  15.1 0.1 shard_map.90.refs_0_.refs_1_
  15.2 2.2 %collective-permute-start.7 = (f32[128,256]{1,0:T(8,128)S(1)}, f32[128,256]{1,0:T(8,128)S(1)}, u32[]{:S(2)}, u32[]{:S(2)}) collective-permute-start(f32[128,256]{1,0:T(8,128)S(1)} %shard_map.90.refs_0_.refs_1_), channel_id=1, source_target_pairs={{0,4},{1,5},{2,6},{3,7},{4,0},{5,1},{6,2},{7,3},{8,12},{9,13},{10,... | collective-permute-start | bytes 393224 | tf_op jit(solution)/shard_map/ppermute | solution.py:57
  17.3 0.0 collective-permute-start.8
  17.3 0.4 %shard_map.91 = (f32[128,256]{1,0:T(8,128)S(1)}, f32[128,256]{1,0:T(8,128)S(1)}) custom-call(f32[128,256]{1,0:T(8,128)S(1)} %shard_map.90.refs_0_.refs_1_, f32[128,256]{1,0:T(8,128)S(1)} %get-tuple-element.33.refs_1_, f32[128,256]{1,0:T(8,128)S(1)} %get-tuple-element.24.refs_3_.refs_2_, bf16[4,128,256]{2,1,0:T(8,128)(2,1)S(1)} %get-tuple-element.26.refs_3_, ...), custom_call_target="tpu_custom_call" | custom-call | flops 1310720 | bytes 917504 | tf_op jit(solution)/shard_map/pallas_call | solution.py:23
  17.7 2.6 %collective-permute-done.7.refs_0_ = f32[128,256]{1,0:T(8,128)S(1)} collective-permute-done((f32[128,256]{1,0:T(8,128)S(1)}, f32[128,256]{1,0:T(8,128)S(1)}, u32[]{:S(2)}, u32[]{:S(2)}) %collective-permute-start.7) | collective-permute-done | bytes 131104 | tf_op jit(solution)/shard_map/ppermute | solution.py:57
  20.3 0.0 collective-permute-done.8.refs_1_
  20.3 0.1 shard_map.92.refs_0_
  20.4 2.2 %collective-permute-start.10 = (f32[128,256]{1,0:T(8,128)S(1)}, f32[128,256]{1,0:T(8,128)S(1)}, u32[]{:S(2)}, u32[]{:S(2)}) collective-permute-start(f32[128,256]{1,0:T(8,128)S(1)} %shard_map.92.refs_0_), channel_id=1, source_target_pairs={{0,4},{1,5},{2,6},{3,7},{4,0},{5,1},{6,2},{7,3},{8,12},{9,13},{10,... | collective-permute-start | bytes 393224 | tf_op jit(solution)/shard_map/ppermute | solution.py:57
  22.5 0.0 collective-permute-start.9
  22.5 0.4 %shard_map.93 = (f32[128,256]{1,0:T(8,128)S(1)}, f32[128,256]{1,0:T(8,128)S(1)}, f32[128,256]{1,0:T(8,128)S(1)}) custom-call(f32[128,256]{1,0:T(8,128)S(1)} %shard_map.92.refs_0_, f32[128,256]{1,0:T(8,128)S(1)} %shard_map.90.refs_0_.refs_1_, f32[128,256]{1,0:T(8,128)S(1)} %get-tuple-element.24.refs_3_.refs_2_, ...), custom_call_target="tpu_custom_call" | custom-call | flops 1310720 | bytes 917504 | tf_op jit(solution)/shard_map/pallas_call | solution.py:23
  22.9 2.6 %collective-permute-done.10.refs_1_ = f32[128,256]{1,0:T(8,128)S(1)} collective-permute-done((f32[128,256]{1,0:T(8,128)S(1)}, f32[128,256]{1,0:T(8,128)S(1)}, u32[]{:S(2)}, u32[]{:S(2)}) %collective-permute-start.10) | collective-permute-done | bytes 131104 | tf_op jit(solution)/shard_map/ppermute | solution.py:57
  25.5 0.0 collective-permute-done.9.refs_0_
  25.5 0.1 shard_map.94
  25.6 1.6 %collective-permute-start.11 = (f32[128,256]{1,0:T(8,128)S(1)}, f32[128,256]{1,0:T(8,128)S(1)}, u32[]{:S(2)}, u32[]{:S(2)}) collective-permute-start(f32[128,256]{1,0:T(8,128)S(1)} %get-tuple-element.43), channel_id=1, source_target_pairs={{0,2},{1,3},{2,0},{3,1},{4,6},{5,7},{6,4},{7,5},{8,10},{9,11},{10,... | collective-permute-start | bytes 393224 | tf_op jit(solution)/shard_map/ppermute | solution.py:263
  27.1 3.5 %collective-permute-done.11 = f32[128,256]{1,0:T(8,128)S(1)} collective-permute-done((f32[128,256]{1,0:T(8,128)S(1)}, f32[128,256]{1,0:T(8,128)S(1)}, u32[]{:S(2)}, u32[]{:S(2)}) %collective-permute-start.11) | collective-permute-done | bytes 131104 | tf_op jit(solution)/shard_map/ppermute | solution.py:263
  30.6 0.1 collective-permute-start.12
  30.7 0.7 %copy.9 = f32[1,4,32,256]{3,2,1,0:T(8,128)} copy(f32[1,4,32,256]{3,2,1,0:T(8,128)S(1)} %bitcast.10) | data formatting | bytes 262144
  31.4 0.7 %collective-permute-done.12 = f32[128,256]{1,0:T(8,128)S(1)} collective-permute-done((f32[128,256]{1,0:T(8,128)S(1)}, f32[128,256]{1,0:T(8,128)S(1)}, u32[]{:S(2)}, u32[]{:S(2)}) %collective-permute-start.12) | collective-permute-done | bytes 131104 | tf_op jit(solution)/shard_map/ppermute | solution.py:263
  32.0 0.7 %add.7 = f32[128,256]{1,0:T(8,128)} add(f32[128,256]{1,0:T(8,128)S(1)} %add.6, f32[128,256]{1,0:T(8,128)S(1)} %collective-permute-done.12) | non-fusion elementwise | flops 32768 | bytes 393216 | tf_op jit(solution)/shard_map/add | solution.py:263
  (1 shorter events, 0.0 us)
Async XLA Ops:
  0.6 9.3 %collective-permute-start = (f32[128,256]{1,0:T(8,128)}, f32[128,256]{1,0:T(8,128)S(1)}, u32[]{:S(2)}, u32[]{:S(2)}) collective-permute-start(f32[128,256]{1,0:T(8,128)} %bitcast.14), channel_id=1, source_target_pairs={{0,4},{1,5},{2,6},{3,7},{4,0},{5,1},{6,2},{7,3},{8,12},{9,13},{10,... | collective-permute-start | bytes 393224 | tf_op jit(solution)/shard_map/ppermute | solution.py:57
  3.7 6.2 %collective-permute-start.1 = (f32[128,256]{1,0:T(8,128)}, f32[128,256]{1,0:T(8,128)S(1)}, u32[]{:S(2)}, u32[]{:S(2)}) collective-permute-start(f32[128,256]{1,0:T(8,128)} %bitcast.15), channel_id=1, source_target_pairs={{0,1},{1,0},{2,3},{3,2},{4,8},{5,9},{6,10},{7,11},{8,4},{9,5},{10,... | collective-permute-start | bytes 393224 | tf_op jit(solution)/shard_map/ppermute | solution.py:56
  5.3 6.9 %collective-permute-start.4 = (f32[8,256]{1,0:T(8,128)S(1)}, f32[8,256]{1,0:T(8,128)S(1)}, u32[]{:S(2)}, u32[]{:S(2)}) collective-permute-start(f32[8,256]{1,0:T(8,128)S(1)} %get-tuple-element.27.refs_0_), channel_id=1, source_target_pairs={{0,12},{4,8},{8,4},{12,0},{1,13},{5,9},{9,5},{13,1},{2,14},{6,10},... | collective-permute-start | bytes 24584 | tf_op jit(solution)/shard_map/ppermute | solution.py:310
  7.8 4.3 %collective-permute-start.5 = (f32[8,256]{1,0:T(8,128)S(1)}, f32[8,256]{1,0:T(8,128)S(1)}, u32[]{:S(2)}, u32[]{:S(2)}) collective-permute-start(f32[8,256]{1,0:T(8,128)S(1)} %get-tuple-element.27.refs_0_), channel_id=1, source_target_pairs={{0,4},{4,0},{8,12},{12,8},{1,5},{5,1},{9,13},{13,9},{2,6},{6,2},{1... | collective-permute-start | bytes 24584 | tf_op jit(solution)/shard_map/ppermute | solution.py:310
  8.5 4.7 %collective-permute-start.6 = (f32[8,256]{1,0:T(8,128)S(1)}, f32[8,256]{1,0:T(8,128)S(1)}, u32[]{:S(2)}, u32[]{:S(2)}) collective-permute-start(f32[8,256]{1,0:T(8,128)S(1)} %get-tuple-element.27.refs_0_), channel_id=1, source_target_pairs={{0,8},{4,12},{8,0},{12,4},{1,9},{5,13},{9,1},{13,5},{2,10},{6,14},... | collective-permute-start | bytes 24584 | tf_op jit(solution)/shard_map/ppermute | solution.py:310
  10.0 5.0 %collective-permute-start.2 = (f32[128,256]{1,0:T(8,128)S(1)}, f32[128,256]{1,0:T(8,128)S(1)}, u32[]{:S(2)}, u32[]{:S(2)}) collective-permute-start(f32[128,256]{1,0:T(8,128)S(1)} %shard_map.87.refs_0_), channel_id=1, source_target_pairs={{0,4},{1,5},{2,6},{3,7},{4,0},{5,1},{6,2},{7,3},{8,12},{9,13},{10,... | collective-permute-start | bytes 393224 | tf_op jit(solution)/shard_map/ppermute | solution.py:57
  12.1 3.0 %collective-permute-start.3 = (f32[128,256]{1,0:T(8,128)S(1)}, f32[128,256]{1,0:T(8,128)S(1)}, u32[]{:S(2)}, u32[]{:S(2)}) collective-permute-start(f32[128,256]{1,0:T(8,128)S(1)} %shard_map.87.refs_0_), channel_id=1, source_target_pairs={{0,1},{1,0},{2,3},{3,2},{4,8},{5,9},{6,10},{7,11},{8,4},{9,5},{10,... | collective-permute-start | bytes 393224 | tf_op jit(solution)/shard_map/ppermute | solution.py:56
  15.2 5.1 %collective-permute-start.7 = (f32[128,256]{1,0:T(8,128)S(1)}, f32[128,256]{1,0:T(8,128)S(1)}, u32[]{:S(2)}, u32[]{:S(2)}) collective-permute-start(f32[128,256]{1,0:T(8,128)S(1)} %shard_map.90.refs_0_.refs_1_), channel_id=1, source_target_pairs={{0,4},{1,5},{2,6},{3,7},{4,0},{5,1},{6,2},{7,3},{8,12},{9,13},{10,... | collective-permute-start | bytes 393224 | tf_op jit(solution)/shard_map/ppermute | solution.py:57
  17.3 3.0 %collective-permute-start.8 = (f32[128,256]{1,0:T(8,128)S(1)}, f32[128,256]{1,0:T(8,128)S(1)}, u32[]{:S(2)}, u32[]{:S(2)}) collective-permute-start(f32[128,256]{1,0:T(8,128)S(1)} %shard_map.90.refs_0_.refs_1_), channel_id=1, source_target_pairs={{0,1},{1,0},{2,3},{3,2},{4,8},{5,9},{6,10},{7,11},{8,4},{9,5},{10,... | collective-permute-start | bytes 393224 | tf_op jit(solution)/shard_map/ppermute | solution.py:56
  20.4 5.1 %collective-permute-start.10 = (f32[128,256]{1,0:T(8,128)S(1)}, f32[128,256]{1,0:T(8,128)S(1)}, u32[]{:S(2)}, u32[]{:S(2)}) collective-permute-start(f32[128,256]{1,0:T(8,128)S(1)} %shard_map.92.refs_0_), channel_id=1, source_target_pairs={{0,4},{1,5},{2,6},{3,7},{4,0},{5,1},{6,2},{7,3},{8,12},{9,13},{10,... | collective-permute-start | bytes 393224 | tf_op jit(solution)/shard_map/ppermute | solution.py:57
  22.5 3.0 %collective-permute-start.9 = (f32[128,256]{1,0:T(8,128)S(1)}, f32[128,256]{1,0:T(8,128)S(1)}, u32[]{:S(2)}, u32[]{:S(2)}) collective-permute-start(f32[128,256]{1,0:T(8,128)S(1)} %shard_map.92.refs_0_), channel_id=1, source_target_pairs={{0,1},{1,0},{2,3},{3,2},{4,8},{5,9},{6,10},{7,11},{8,4},{9,5},{10,... | collective-permute-start | bytes 393224 | tf_op jit(solution)/shard_map/ppermute | solution.py:56
  25.6 5.0 %collective-permute-start.11 = (f32[128,256]{1,0:T(8,128)S(1)}, f32[128,256]{1,0:T(8,128)S(1)}, u32[]{:S(2)}, u32[]{:S(2)}) collective-permute-start(f32[128,256]{1,0:T(8,128)S(1)} %get-tuple-element.43), channel_id=1, source_target_pairs={{0,2},{1,3},{2,0},{3,1},{4,6},{5,7},{6,4},{7,5},{8,10},{9,11},{10,... | collective-permute-start | bytes 393224 | tf_op jit(solution)/shard_map/ppermute | solution.py:263
  30.6 1.4 %collective-permute-start.12 = (f32[128,256]{1,0:T(8,128)S(1)}, f32[128,256]{1,0:T(8,128)S(1)}, u32[]{:S(2)}, u32[]{:S(2)}) collective-permute-start(f32[128,256]{1,0:T(8,128)S(1)} %add.6), channel_id=1, source_target_pairs={{0,1},{1,0},{2,3},{3,2},{4,5},{5,4},{6,7},{7,6},{8,9},{9,8},{10,11... | collective-permute-start | bytes 393224 | tf_op jit(solution)/shard_map/ppermute | solution.py:263

commit v9 on v8

--- a/solution.py
+++ b/solution.py
@@ -51,9 +51,9 @@
     return routes
 
 
-def exchange(slab):
+def exchange(slab, other=None):
     count, shots = lax.axis_size("tgt"), lax.axis_size("shot")
-    outer = lax.ppermute(slab, ("tgt", "shot"), swap_pairs(count, shots, 1))
+    outer = lax.ppermute(slab if other is None else other, ("tgt", "shot"), swap_pairs(count, shots, 1))
     inner = lax.ppermute(slab, ("tgt", "shot"), swap_pairs(count, shots, 0))
     return inner, outer
 
@@ -75,13 +75,13 @@
     return [flat[:, i : i + chunk] for i in range(0, owners * CAP, chunk)]
 
 
-def inject_kernel(steps, table_count, with_halo, here_ref, *refs):
+def inject_kernel(steps, table_count, table_rows, with_halo, here_ref, *refs):
     table_refs, out_refs = refs[:table_count], refs[table_count:]
     rows, lanes = out_refs[0].shape
     here = here_ref[0].astype(jnp.float32)
     left, right = [], []
     for table_ref in table_refs:
-        table = table_ref[...]
+        table = table_ref[table_ref.shape[0] - table_rows :]
         count = table.shape[1]
         slab = table[0:1]
         cell = table[1:2].astype(jnp.int32)
@@ -118,7 +118,7 @@
     count = steps + 2 * with_halo
     entries = sum(t.shape[1] for t in tables)
     return on_chip(
-        functools.partial(inject_kernel, steps, len(tables), with_halo),
+        functools.partial(inject_kernel, steps, len(tables), tables[0].shape[0], with_halo),
         [(shape, jnp.float32)] * count,
         here,
         *tables,
@@ -151,11 +151,10 @@
     return 2.0 * current[p] - later + courant * courant * total
 
 
-def first_kernel(planes, table_rows, *refs):
-    refs = list(refs)
-    now_hbm, later_hbm, courant_hbm, fwd_hbm, dest_hbm, cell_hbm, vals_hbm = refs[:7]
-    part_ref, table_ref, now_ref, courant_ref, fwd_ref = refs[7:12]
-    later_ref, dest_ref, cell_ref, vals_ref, sems = refs[12:]
+def first_kernel(carry, *refs):
+    now_hbm, later_hbm, courant_hbm, dest_hbm, cell_hbm, vals_hbm = refs[:6]
+    later_ref, table_ref, now_ref, courant_ref = refs[6:10]
+    dest_ref, cell_ref, vals_ref, sems = refs[-4:]
     pairs = [
         (dest_hbm, dest_ref),
         (cell_hbm, cell_ref),
@@ -163,7 +162,6 @@
         (now_hbm, now_ref),
         (later_hbm, later_ref),
         (courant_hbm, courant_ref),
-        (fwd_hbm, fwd_ref),
     ]
     copies = [pltpu.make_async_copy(a, b, sems.at[i]) for i, (a, b) in enumerate(pairs)]
     for copy in copies:
@@ -176,12 +174,18 @@
     table_ref[2 : 2 + vals_ref.shape[0]] = vals_ref[...]
     for copy in copies[3:6]:
         copy.wait()
+    if carry:
+        message_ref = refs[10]
+        message_ref[0 : now_ref.shape[0]] = now_ref[...]
+        message_ref[now_ref.shape[0] :] = table_ref[...]
+
+
+def start_kernel(planes, now_ref, later_ref, courant_ref, part_ref):
     cells_y = now_ref.shape[0] // planes
     at = [slice(p * cells_y, (p + 1) * cells_y) for p in range(planes)]
     current = [now_ref[s] for s in at]
     for p, s in enumerate(at):
         part_ref[s] = own_part(current, p, later_ref[s], courant_ref[s])
-    copies[6].wait()
 
 
 def own_kernel(planes, step, fix_inject, last, *refs):
@@ -217,8 +221,6 @@
 def halo_kernel(planes, slabs, fix_inject, last, here_ref, *refs):
     refs = list(refs)
     inner_ref, outer_ref, part_ref, courant_ref = refs[:4]
-    if last:
-        inner_ref, outer_ref = outer_ref, inner_ref
     refs = refs[4:]
     fix_refs = (refs.pop(0), refs.pop(0)) if fix_inject else None
     weight_ref, grad_in_ref = (refs.pop(0), refs.pop(0)) if last else (None, None)
@@ -275,47 +277,55 @@
     here = lax.axis_index("tgt").reshape(1)
     now = adjoint_now.reshape(shape)
     table_rows = -(-(2 + steps) // 8) * 8
-    everywhere = slabs & (slabs - 1) == 0 and slabs * entries <= GATHER_LIMIT
-
-    received = exchange(now)
+    everywhere = (
+        1 < slabs == slabs & -slabs and slabs * entries <= GATHER_LIMIT and entries == lanes
+    )
+
     f32 = jnp.float32
-    part, table, current, courant_here, fwd = on_chip(
-        functools.partial(first_kernel, planes, table_rows),
+    fwd = fwd_acc.reshape(steps, rows, lanes)
+    later_here, table, current, courant_here, *message = on_chip(
+        functools.partial(first_kernel, everywhere),
         [
             (shape, f32),
             ((table_rows, entries), f32),
             (shape, f32),
             (shape, f32),
-            ((steps, rows, lanes), fwd_acc.dtype),
-        ],
+        ]
+        + [((rows + table_rows, lanes), f32)] * everywhere,
         now,
         adjoint_later.reshape(shape),
         courant.reshape(shape),
-        fwd_acc.reshape(steps, rows, lanes),
         surf_dest.reshape(1, entries),
         surf_cell.reshape(1, entries),
         surf_vals.reshape(steps, entries),
         flops=40 * rows * lanes,
         scratch=[
-            pltpu.VMEM(shape, f32),
             pltpu.VMEM((1, entries), surf_dest.dtype),
             pltpu.VMEM((1, entries), surf_cell.dtype),
             pltpu.VMEM((steps, entries), f32),
-            pltpu.SemaphoreType.DMA((7,)),
+            pltpu.SemaphoreType.DMA((6,)),
         ],
-        in_hbm=range(7),
+        in_hbm=range(6),
+    )
+    received = exchange(*message, current) if everywhere else exchange(current)
+    (part,) = on_chip(
+        functools.partial(start_kernel, planes),
+        [(shape, f32)],
+        current,
+        later_here,
+        courant_here,
+        flops=40 * rows * lanes,
     )
     if everywhere:
-        tables = [table] + [
+        tables = [table, received[0]] + [
             lax.ppermute(table, "tgt", [(i, i ^ far) for i in range(slabs)])
-            for far in [*range(slabs - 1, 2, -1), *range(1, min(slabs, 3))]
+            for far in range(slabs - 1, 1, -1)
         ]
         inject = None
     else:
         tables = slotted_tables(table, surf_dest, slabs)
         inject = injection(here, tables, steps, shape, False)
         part = part + inject[0]
-        tables = []
 
     fixes, extra, later_field, grad = [], [], None, None
     for step in range(steps):
@@ -334,7 +344,7 @@
             )
             if fix:
                 current = extra.pop(0)
-        args = [here, *(received[::-1] if last else received), part, courant_here, *fixes]
+        args = [here, *received, part, courant_here, *fixes]
         args += [*extra, grad] if last else []
         fresh, *other = on_chip(
             functools.partial(halo_kernel, planes, slabs, fix, last),

time: 32.9 us -> 32.8 us (level)
  starting transfers between devices: 15.8 us -> 15.3 us
    ppermute x4, waiting for transfers between devices: 5.14 us -> 6.29 us  [exchange(): inner = lax.ppermute(slab, ('tgt', 'shot'), swap_pairs(count, shots, 0))]
    ppermute x3 -> x2, waiting for transfers between devices: 1.08 us -> 0.25 us  [on_device(): lax.ppermute(table, 'tgt', [(i, i ^ far) for i in range(slabs)])]
    ppermute x4, starting transfers between devices: 9.5 us -> 9.09 us  [exchange(): inner = lax.ppermute(slab, ('tgt', 'shot'), swap_pairs(count, shots, 0))]
    ppermute x3 -> x2, starting transfers between devices: 4.68 us -> 4.61 us  [on_device(): lax.ppermute(table, 'tgt', [(i, i ^ far) for i in range(slabs)])]
    pallas_call x9 -> x10, Pallas kernels: 4.45 us -> 4.46 us  [on_chip(): pl.pallas_call(kernel, out_shape=[pltpu.VMEM(shape, dtype) for shape, dty...]
    unnamed x1 -> x3, local copies, waits for them, and re-layouts: 0.66 us -> 0.66 us
  transfers between devices with their start and end apart: 13 -> 12, of which waited for: 5 -> 6; matrix products, arithmetic and copies ran while one was open for 2% -> 2% of each run, Pallas kernels for 13% -> 9%
where the time goes in v9:
time: 32.8 us; the launch traced here: 32.6 us
  starting transfers between devices  15.3 us (47%)
  waiting for transfers between devices  10.7 us (33%)
  Pallas kernels  4.46 us (14%)
  between operations  0.75 us (2%)
  other arithmetic  0.69 us (2%)
  local copies, waits for them, and re-layouts  0.66 us (2%)
    ppermute x4, starting transfers between devices, exchange(): inner = lax.ppermute(slab, ('tgt', 'shot'), swap_pairs(count, shots, 0))  9.09 us
    ppermute x4, waiting for transfers between devices, exchange(): inner = lax.ppermute(slab, ('tgt', 'shot'), swap_pairs(count, shots, 0))  6.29 us
    ppermute x2, starting transfers between devices, on_device(): lax.ppermute(table, 'tgt', [(i, i ^ far) for i in range(slabs)])  4.61 us
    pallas_call x10, Pallas kernels, on_chip(): pl.pallas_call(kernel, out_shape=[pltpu.VMEM(shape, dtype) for shape, dty...  4.46 us
    ppermute x2, waiting for transfers between devices, sum_over(): lax.ppermute(value, axis, [(i, i ^ distance) for i in range(count)])  4.15 us
    ppermute x2, starting transfers between devices, sum_over(): lax.ppermute(value, axis, [(i, i ^ distance) for i in range(count)])  1.63 us
    add x2, other arithmetic, sum_over(): value + lax.ppermute(value, axis, [(i, i ^ distance) for i in range(count)])  0.69 us
    unnamed x3, local copies, waits for them, and re-layouts  0.66 us
  transfers between devices with their start and end apart: 12, of which 6 were waited for; matrix products, arithmetic and copies ran while one was open for 2% of the time, Pallas kernels for 9%

profile of v9, /device:TPU:0, one launch (start us, length us, event | category | flops | bytes accessed | tf_op | source)
XLA Modules:
  0.0 32.6 jit_solution(15901967298502777514)
XLA Ops:
  0.6 1.1 %shard_map.86 = (f32[128,256]{1,0:T(8,128)S(1)}, f32[8,256]{1,0:T(8,128)S(1)}, f32[128,256]{1,0:T(8,128)S(1)}, f32[128,256]{1,0:T(8,128)S(1)}, f32[136,256]{1,0:T(8,128)S(1)}) custom-call(f32[128,256]{1,0:T(8,128)} %bitcast.14, f32[128,256]{1,0:T(8,128)} %bitcast.15, f32[128,256]{1,0:T(8,128)} %bitcast.16, s32[1,256]{1,0:T(1,128)} %bitcast.19, ...), custom_call_target="tpu_custom_call" | custom-call | flops 1310720 | bytes 399360 | tf_op jit(solution)/shard_map/pallas_call | solution.py:23
  1.8 3.1 %collective-permute-start = (f32[136,256]{1,0:T(8,128)S(1)}, f32[136,256]{1,0:T(8,128)S(1)}, u32[]{:S(2)}, u32[]{:S(2)}) collective-permute-start(f32[136,256]{1,0:T(8,128)S(1)} %get-tuple-element.23), channel_id=1, source_target_pairs={{0,4},{1,5},{2,6},{3,7},{4,0},{5,1},{6,2},{7,3},{8,12},{9,13},{10,... | collective-permute-start | bytes 417800 | tf_op jit(solution)/shard_map/ppermute | solution.py:57
  4.9 0.0 collective-permute-start.1
  4.9 2.5 %collective-permute-start.4 = (f32[8,256]{1,0:T(8,128)S(1)}, f32[8,256]{1,0:T(8,128)S(1)}, u32[]{:S(2)}, u32[]{:S(2)}) collective-permute-start(f32[8,256]{1,0:T(8,128)S(1)} %get-tuple-element.27.refs_0_), channel_id=1, source_target_pairs={{0,12},{4,8},{8,4},{12,0},{1,13},{5,9},{9,5},{13,1},{2,14},{6,10},... | collective-permute-start | bytes 24584 | tf_op jit(solution)/shard_map/ppermute | solution.py:321
  7.3 2.1 %collective-permute-start.5 = (f32[8,256]{1,0:T(8,128)S(1)}, f32[8,256]{1,0:T(8,128)S(1)}, u32[]{:S(2)}, u32[]{:S(2)}) collective-permute-start(f32[8,256]{1,0:T(8,128)S(1)} %get-tuple-element.27.refs_0_), channel_id=1, source_target_pairs={{0,8},{4,12},{8,0},{12,4},{1,9},{5,13},{9,1},{13,5},{2,10},{6,14},... | collective-permute-start | bytes 24584 | tf_op jit(solution)/shard_map/ppermute | solution.py:321
  9.5 0.4 %shard_map.87.refs_2_ = f32[128,256]{1,0:T(8,128)S(1)} custom-call(f32[128,256]{1,0:T(8,128)S(1)} %get-tuple-element.24.now_ref.refs_1_, f32[128,256]{1,0:T(8,128)S(1)} %get-tuple-element.25.later_ref, f32[128,256]{1,0:T(8,128)S(1)} %get-tuple-element.26.courant_ref.refs_3_.refs_2_), custom_call_target="tpu_custom_call" | custom-call | flops 1310720 | bytes 393216 | tf_op jit(solution)/shard_map/pallas_call | solution.py:23
  9.9 0.0 collective-permute-done.1.refs_1_
  9.9 0.0 collective-permute-done.refs_0_.refs_1_
  9.9 0.1 shard_map.88.refs_0_
  10.0 0.0 copy-start
  10.0 1.8 %collective-permute-start.2 = (f32[128,256]{1,0:T(8,128)S(1)}, f32[128,256]{1,0:T(8,128)S(1)}, u32[]{:S(2)}, u32[]{:S(2)}) collective-permute-start(f32[128,256]{1,0:T(8,128)S(1)} %shard_map.88.refs_0_), channel_id=1, source_target_pairs={{0,4},{1,5},{2,6},{3,7},{4,0},{5,1},{6,2},{7,3},{8,12},{9,13},{10,... | collective-permute-start | bytes 393224 | tf_op jit(solution)/shard_map/ppermute | solution.py:57
  11.8 0.0 collective-permute-start.3
  11.8 0.0 collective-permute-done.4.refs_2_
  11.8 0.2 collective-permute-done.5.refs_3_
  12.0 1.4 %shard_map.89 = (f32[128,256]{1,0:T(8,128)S(1)}, f32[128,256]{1,0:T(8,128)S(1)}, f32[128,256]{1,0:T(8,128)S(1)}, f32[128,256]{1,0:T(8,128)S(1)}, f32[128,256]{1,0:T(8,128)S(1)}, /*index=5*/f32[128,256]{1,0:T(8,128)S(1)}) custom-call(s32[1]{0:T(128)} %bitcast.here_ref, f32[8,256]{1,0:T(8,128)S(1)} %get-tuple-element.27.refs_0_, ...), custom_call_target="tpu_custom_call" | custom-call | flops 4831838208 | bytes 163844 | tf_op jit(solution)/shard_map/pallas_call | solution.py:23
  13.4 0.0 copy-done
  13.4 0.4 %shard_map.90 = (f32[128,256]{1,0:T(8,128)S(1)}, f32[128,256]{1,0:T(8,128)S(1)}, f32[128,256]{1,0:T(8,128)S(1)}) custom-call(f32[128,256]{1,0:T(8,128)S(1)} %shard_map.88.refs_0_, f32[128,256]{1,0:T(8,128)S(1)} %get-tuple-element.24.now_ref.refs_1_, f32[128,256]{1,0:T(8,128)S(1)} %get-tuple-element.26.courant_ref.refs_3_.refs_2_, ...), custom_call_target="tpu_custom_call" | custom-call | flops 1310720 | bytes 917504 | tf_op jit(solution)/shard_map/pallas_call | solution.py:23
  13.9 1.2 %collective-permute-done.2.refs_0_ = f32[128,256]{1,0:T(8,128)S(1)} collective-permute-done((f32[128,256]{1,0:T(8,128)S(1)}, f32[128,256]{1,0:T(8,128)S(1)}, u32[]{:S(2)}, u32[]{:S(2)}) %collective-permute-start.2) | collective-permute-done | bytes 131104 | tf_op jit(solution)/shard_map/ppermute | solution.py:57
  15.0 0.0 collective-permute-done.3.refs_1_
  15.0 0.1 shard_map.91.refs_0_.refs_1_
  15.1 2.1 %collective-permute-start.6 = (f32[128,256]{1,0:T(8,128)S(1)}, f32[128,256]{1,0:T(8,128)S(1)}, u32[]{:S(2)}, u32[]{:S(2)}) collective-permute-start(f32[128,256]{1,0:T(8,128)S(1)} %shard_map.91.refs_0_.refs_1_), channel_id=1, source_target_pairs={{0,4},{1,5},{2,6},{3,7},{4,0},{5,1},{6,2},{7,3},{8,12},{9,13},{10,... | collective-permute-start | bytes 393224 | tf_op jit(solution)/shard_map/ppermute | solution.py:57
  17.2 0.0 collective-permute-start.7
  17.2 0.4 %shard_map.92 = (f32[128,256]{1,0:T(8,128)S(1)}, f32[128,256]{1,0:T(8,128)S(1)}) custom-call(f32[128,256]{1,0:T(8,128)S(1)} %shard_map.91.refs_0_.refs_1_, f32[128,256]{1,0:T(8,128)S(1)} %get-tuple-element.33.refs_1_, f32[128,256]{1,0:T(8,128)S(1)} %get-tuple-element.26.courant_ref.refs_3_.refs_2_, bf16[4,128,256]{2,1,0:T(8,128)(2,1)S(1)} %bitcast.12, ...), custom_call_target="tpu_custom_call" | custom-call | flops 1310720 | bytes 917504 | tf_op jit(solution)/shard_map/pallas_call | solution.py:23
  17.6 2.6 %collective-permute-done.6.refs_0_ = f32[128,256]{1,0:T(8,128)S(1)} collective-permute-done((f32[128,256]{1,0:T(8,128)S(1)}, f32[128,256]{1,0:T(8,128)S(1)}, u32[]{:S(2)}, u32[]{:S(2)}) %collective-permute-start.6) | collective-permute-done | bytes 131104 | tf_op jit(solution)/shard_map/ppermute | solution.py:57
  20.2 0.0 collective-permute-done.7.refs_1_
  20.2 0.1 shard_map.93.refs_0_
  20.3 2.2 %collective-permute-start.8 = (f32[128,256]{1,0:T(8,128)S(1)}, f32[128,256]{1,0:T(8,128)S(1)}, u32[]{:S(2)}, u32[]{:S(2)}) collective-permute-start(f32[128,256]{1,0:T(8,128)S(1)} %shard_map.93.refs_0_), channel_id=1, source_target_pairs={{0,4},{1,5},{2,6},{3,7},{4,0},{5,1},{6,2},{7,3},{8,12},{9,13},{10,... | collective-permute-start | bytes 393224 | tf_op jit(solution)/shard_map/ppermute | solution.py:57
  22.4 0.0 collective-permute-start.9
  22.4 0.4 %shard_map.94 = (f32[128,256]{1,0:T(8,128)S(1)}, f32[128,256]{1,0:T(8,128)S(1)}, f32[128,256]{1,0:T(8,128)S(1)}) custom-call(f32[128,256]{1,0:T(8,128)S(1)} %shard_map.93.refs_0_, f32[128,256]{1,0:T(8,128)S(1)} %shard_map.91.refs_0_.refs_1_, f32[128,256]{1,0:T(8,128)S(1)} %get-tuple-element.26.courant_ref.refs_3_.refs_2_, bf16[4,128,256]{2,1,0:T(8,128)(2,1)S(1)} %bitcast.13, ...), custom_call_target="tpu_custom_call" | custom-call | flops 1310720 | bytes 917504 | tf_op jit(solution)/shard_map/pallas_call | solution.py:23
  22.8 2.6 %collective-permute-done.8.refs_0_ = f32[128,256]{1,0:T(8,128)S(1)} collective-permute-done((f32[128,256]{1,0:T(8,128)S(1)}, f32[128,256]{1,0:T(8,128)S(1)}, u32[]{:S(2)}, u32[]{:S(2)}) %collective-permute-start.8) | collective-permute-done | bytes 131104 | tf_op jit(solution)/shard_map/ppermute | solution.py:57
  25.4 0.0 collective-permute-done.9.refs_1_
  25.4 0.1 shard_map.95
  25.5 1.6 %collective-permute-start.10 = (f32[128,256]{1,0:T(8,128)S(1)}, f32[128,256]{1,0:T(8,128)S(1)}, u32[]{:S(2)}, u32[]{:S(2)}) collective-permute-start(f32[128,256]{1,0:T(8,128)S(1)} %get-tuple-element.43), channel_id=1, source_target_pairs={{0,2},{1,3},{2,0},{3,1},{4,6},{5,7},{6,4},{7,5},{8,10},{9,11},{10,... | collective-permute-start | bytes 393224 | tf_op jit(solution)/shard_map/ppermute | solution.py:265
  27.0 3.5 %collective-permute-done.10 = f32[128,256]{1,0:T(8,128)S(1)} collective-permute-done((f32[128,256]{1,0:T(8,128)S(1)}, f32[128,256]{1,0:T(8,128)S(1)}, u32[]{:S(2)}, u32[]{:S(2)}) %collective-permute-start.10) | collective-permute-done | bytes 131104 | tf_op jit(solution)/shard_map/ppermute | solution.py:265
  30.5 0.1 collective-permute-start.11
  30.6 0.7 %copy.9 = f32[1,4,32,256]{3,2,1,0:T(8,128)} copy(f32[1,4,32,256]{3,2,1,0:T(8,128)S(1)} %bitcast.10) | data formatting | bytes 262144
  31.3 0.7 %collective-permute-done.11 = f32[128,256]{1,0:T(8,128)S(1)} collective-permute-done((f32[128,256]{1,0:T(8,128)S(1)}, f32[128,256]{1,0:T(8,128)S(1)}, u32[]{:S(2)}, u32[]{:S(2)}) %collective-permute-start.11) | collective-permute-done | bytes 131104 | tf_op jit(solution)/shard_map/ppermute | solution.py:265
  31.9 0.7 %add.7 = f32[128,256]{1,0:T(8,128)} add(f32[128,256]{1,0:T(8,128)S(1)} %add.6, f32[128,256]{1,0:T(8,128)S(1)} %collective-permute-done.11) | non-fusion elementwise | flops 32768 | bytes 393216 | tf_op jit(solution)/shard_map/add | solution.py:265
  (1 shorter events, 0.0 us)
Async XLA Ops:
  1.8 8.1 %collective-permute-start = (f32[136,256]{1,0:T(8,128)S(1)}, f32[136,256]{1,0:T(8,128)S(1)}, u32[]{:S(2)}, u32[]{:S(2)}) collective-permute-start(f32[136,256]{1,0:T(8,128)S(1)} %get-tuple-element.23), channel_id=1, source_target_pairs={{0,4},{1,5},{2,6},{3,7},{4,0},{5,1},{6,2},{7,3},{8,12},{9,13},{10,... | collective-permute-start | bytes 417800 | tf_op jit(solution)/shard_map/ppermute | solution.py:57
  4.9 5.0 %collective-permute-start.1 = (f32[128,256]{1,0:T(8,128)S(1)}, f32[128,256]{1,0:T(8,128)S(1)}, u32[]{:S(2)}, u32[]{:S(2)}) collective-permute-start(f32[128,256]{1,0:T(8,128)S(1)} %get-tuple-element.24.now_ref.refs_1_), channel_id=1, source_target_pairs={{0,1},{1,0},{2,3},{3,2},{4,8},{5,9},{6,10},{7,11},{8,4},{9,5},{10,... | collective-permute-start | bytes 393224 | tf_op jit(solution)/shard_map/ppermute | solution.py:56
  4.9 6.9 %collective-permute-start.4 = (f32[8,256]{1,0:T(8,128)S(1)}, f32[8,256]{1,0:T(8,128)S(1)}, u32[]{:S(2)}, u32[]{:S(2)}) collective-permute-start(f32[8,256]{1,0:T(8,128)S(1)} %get-tuple-element.27.refs_0_), channel_id=1, source_target_pairs={{0,12},{4,8},{8,4},{12,0},{1,13},{5,9},{9,5},{13,1},{2,14},{6,10},... | collective-permute-start | bytes 24584 | tf_op jit(solution)/shard_map/ppermute | solution.py:321
  7.3 4.7 %collective-permute-start.5 = (f32[8,256]{1,0:T(8,128)S(1)}, f32[8,256]{1,0:T(8,128)S(1)}, u32[]{:S(2)}, u32[]{:S(2)}) collective-permute-start(f32[8,256]{1,0:T(8,128)S(1)} %get-tuple-element.27.refs_0_), channel_id=1, source_target_pairs={{0,8},{4,12},{8,0},{12,4},{1,9},{5,13},{9,1},{13,5},{2,10},{6,14},... | collective-permute-start | bytes 24584 | tf_op jit(solution)/shard_map/ppermute | solution.py:321
  10.0 3.5 %copy-start = (bf16[1,4,4,32,256]{4,3,2,1,0:T(8,128)(2,1)S(1)}, bf16[1,4,4,32,256]{4,3,2,1,0:T(8,128)(2,1)}, u32[]{:S(2)}) copy-start(bf16[1,4,4,32,256]{4,3,2,1,0:T(8,128)(2,1)} %param.10) | copy-start | bytes 786436
  10.0 5.0 %collective-permute-start.2 = (f32[128,256]{1,0:T(8,128)S(1)}, f32[128,256]{1,0:T(8,128)S(1)}, u32[]{:S(2)}, u32[]{:S(2)}) collective-permute-start(f32[128,256]{1,0:T(8,128)S(1)} %shard_map.88.refs_0_), channel_id=1, source_target_pairs={{0,4},{1,5},{2,6},{3,7},{4,0},{5,1},{6,2},{7,3},{8,12},{9,13},{10,... | collective-permute-start | bytes 393224 | tf_op jit(solution)/shard_map/ppermute | solution.py:57
  11.8 3.3 %collective-permute-start.3 = (f32[128,256]{1,0:T(8,128)S(1)}, f32[128,256]{1,0:T(8,128)S(1)}, u32[]{:S(2)}, u32[]{:S(2)}) collective-permute-start(f32[128,256]{1,0:T(8,128)S(1)} %shard_map.88.refs_0_), channel_id=1, source_target_pairs={{0,1},{1,0},{2,3},{3,2},{4,8},{5,9},{6,10},{7,11},{8,4},{9,5},{10,... | collective-permute-start | bytes 393224 | tf_op jit(solution)/shard_map/ppermute | solution.py:56
  15.1 5.0 %collective-permute-start.6 = (f32[128,256]{1,0:T(8,128)S(1)}, f32[128,256]{1,0:T(8,128)S(1)}, u32[]{:S(2)}, u32[]{:S(2)}) collective-permute-start(f32[128,256]{1,0:T(8,128)S(1)} %shard_map.91.refs_0_.refs_1_), channel_id=1, source_target_pairs={{0,4},{1,5},{2,6},{3,7},{4,0},{5,1},{6,2},{7,3},{8,12},{9,13},{10,... | collective-permute-start | bytes 393224 | tf_op jit(solution)/shard_map/ppermute | solution.py:57
  17.2 3.0 %collective-permute-start.7 = (f32[128,256]{1,0:T(8,128)S(1)}, f32[128,256]{1,0:T(8,128)S(1)}, u32[]{:S(2)}, u32[]{:S(2)}) collective-permute-start(f32[128,256]{1,0:T(8,128)S(1)} %shard_map.91.refs_0_.refs_1_), channel_id=1, source_target_pairs={{0,1},{1,0},{2,3},{3,2},{4,8},{5,9},{6,10},{7,11},{8,4},{9,5},{10,... | collective-permute-start | bytes 393224 | tf_op jit(solution)/shard_map/ppermute | solution.py:56
  20.3 5.1 %collective-permute-start.8 = (f32[128,256]{1,0:T(8,128)S(1)}, f32[128,256]{1,0:T(8,128)S(1)}, u32[]{:S(2)}, u32[]{:S(2)}) collective-permute-start(f32[128,256]{1,0:T(8,128)S(1)} %shard_map.93.refs_0_), channel_id=1, source_target_pairs={{0,4},{1,5},{2,6},{3,7},{4,0},{5,1},{6,2},{7,3},{8,12},{9,13},{10,... | collective-permute-start | bytes 393224 | tf_op jit(solution)/shard_map/ppermute | solution.py:57
  22.4 3.0 %collective-permute-start.9 = (f32[128,256]{1,0:T(8,128)S(1)}, f32[128,256]{1,0:T(8,128)S(1)}, u32[]{:S(2)}, u32[]{:S(2)}) collective-permute-start(f32[128,256]{1,0:T(8,128)S(1)} %shard_map.93.refs_0_), channel_id=1, source_target_pairs={{0,1},{1,0},{2,3},{3,2},{4,8},{5,9},{6,10},{7,11},{8,4},{9,5},{10,... | collective-permute-start | bytes 393224 | tf_op jit(solution)/shard_map/ppermute | solution.py:56
  25.5 5.0 %collective-permute-start.10 = (f32[128,256]{1,0:T(8,128)S(1)}, f32[128,256]{1,0:T(8,128)S(1)}, u32[]{:S(2)}, u32[]{:S(2)}) collective-permute-start(f32[128,256]{1,0:T(8,128)S(1)} %get-tuple-element.43), channel_id=1, source_target_pairs={{0,2},{1,3},{2,0},{3,1},{4,6},{5,7},{6,4},{7,5},{8,10},{9,11},{10,... | collective-permute-start | bytes 393224 | tf_op jit(solution)/shard_map/ppermute | solution.py:265
  30.5 1.4 %collective-permute-start.11 = (f32[128,256]{1,0:T(8,128)S(1)}, f32[128,256]{1,0:T(8,128)S(1)}, u32[]{:S(2)}, u32[]{:S(2)}) collective-permute-start(f32[128,256]{1,0:T(8,128)S(1)} %add.6), channel_id=1, source_target_pairs={{0,1},{1,0},{2,3},{3,2},{4,5},{5,4},{6,7},{7,6},{8,9},{9,8},{10,11... | collective-permute-start | bytes 393224 | tf_op jit(solution)/shard_map/ppermute | solution.py:265
